TPU v7x, 256 devices: a whole 4x4x8 slice. The times are simulated.
256 devices in a mesh: member: 64 (over x, y, z_lo, core), lat: 4 (over z_hi).
Axes of the slice: x: 4, y: 4, z: 8 (z_hi: 4, z_lo: 2; z = z_hi * 2 + z_lo), core: 2. Of those that a mesh axis runs over, the one named last changes fastest.
Arguments:
- noisy_latents: bfloat16 [64, 64, 32, 768], P('member', 'lat'), may hold values from -6 to 6
- frames: bfloat16 [64, 64, 32, 768], P('member', 'lat'), may hold values from -6 to 6
- encoder_members: int32 [2], replicated, may hold values from 0 to 63, as said below
- window_shift: int32 [1], replicated, may hold values from 1 to 7
- encoder_in: bfloat16 [768, 768], replicated, may hold values from -0.21875 to 0.21875
- encoder_out: bfloat16 [768, 768], replicated, may hold values from -0.21875 to 0.21875
- joint_weight: bfloat16 [2304, 768], replicated, may hold values from -0.125 to 0.125
- query_weight: bfloat16 [768, 768], replicated, may hold values from -0.21875 to 0.21875
- keyvalue_weight: bfloat16 [768, 1536], replicated, may hold values from -0.21875 to 0.21875
- output_weight: bfloat16 [768, 768], replicated, may hold values from -0.21875 to 0.21875
- position_bias: float32 [12, 225], replicated, may hold values from -250 to 250
- expand_weight: bfloat16 [3072, 768], P('member'), may hold values from -0.21875 to 0.21875
- reduce_weight: bfloat16 [3072, 768], P('member'), may hold values from -0.109375 to 0.109375
Outputs:
- block_out: bfloat16 [64, 64, 32, 768], P('member', 'lat')
Inputs may be any that keep to these rules, and one draw needn't show every extreme that they name: `encoder_members`: two different members, one of which is the last member, 63, in either position.
All inputs are finite; a program needn't handle non-finite values.
Results may differ from a plain program's by a relative error of at most 0.013.
Values may be sent and summed in bfloat16 or wider, within the bound.
No kernel may reach another device: no remote copies, remote signals or barrier semaphores. Data moves between devices by JAX's collectives and lax.ppermute only.
A program may use at most 128 MiB of HBM per device.

v0:
```python
import jax
import jax.numpy as jnp
from jax import lax
from jax.experimental import pallas as pl
from jax.experimental.pallas import tpu as pltpu
from jax.sharding import Mesh
from jax.sharding import PartitionSpec as P

HD = 64
WIN = 8
D = 768
H = 12
FF = 3072
ROWS = 16
COLS = 32
GROUPS = 3
MEMBER = ("mx", "my", "mz", "core")
PLANE = ("mx", "my")
EPS = 1e-06
F32 = jnp.float32
BF16 = jnp.bfloat16
GRANT = 64_000_000


def dot(a, b):
    return jnp.dot(a, b, preferred_element_type=F32)


def dot_nt(a, b):
    return lax.dot_general(a, b, (((1,), (1,)), ((), ())), preferred_element_type=F32)


def dot_tn(a, b):
    return lax.dot_general(a, b, (((0,), (0,)), ((), ())), preferred_element_type=F32)


def normalised(x):
    scale = lax.rsqrt(jnp.mean(x * x, axis=-1, keepdims=True) + EPS)
    return (x * scale).astype(BF16)


def one_hot(wanted, width):
    lanes = lax.broadcasted_iota(jnp.int32, (wanted.shape[0], width), 1)
    return jnp.where(lanes == wanted, 1.0, 0.0).astype(BF16)


def row_ids(count):
    return lax.broadcasted_iota(jnp.int32, (count, 1), 0)


def window_place(count, shift):
    t = row_ids(count)
    row = (t // WIN) % WIN
    col = ((t // (WIN * WIN)) * WIN + t % WIN - shift + COLS) % COLS
    return row, col


def encode_kernel(scal, frame_hbm, in_hbm, out_hbm, joint_hbm, keep_ref, send_ref, frame, w_in, w_out, w_slot, sems):
    copies = [
        pltpu.make_async_copy(frame_hbm, frame, sems.at[0]),
        pltpu.make_async_copy(in_hbm, w_in, sems.at[1]),
        pltpu.make_async_copy(out_hbm, w_out, sems.at[2]),
        pltpu.make_async_copy(joint_hbm.at[pl.ds(pl.multiple_of(scal[1] * D, D), D), :], w_slot, sems.at[3]),
    ]
    for c in copies:
        c.start()
    tokens = ROWS * COLS
    t = row_ids(tokens)
    half = tokens // 2
    core = jnp.where(t < half, scal[2], 1 - scal[2])
    col = core * (COLS // 2) + (t % half) // ROWS
    order = one_hot((t % ROWS) * COLS + col, tokens)
    copies[0].wait()
    ordered = dot(order, frame[...]).astype(BF16)
    copies[1].wait()
    hidden = jax.nn.gelu(dot(ordered, w_in[...])).astype(BF16)
    copies[2].wait()
    condition = dot(hidden, w_out[...]).astype(BF16)
    copies[3].wait()
    term = dot(condition, w_slot[...])
    term = jnp.where(scal[0] > 0, term, 0.0).astype(BF16)
    keep_ref[...] = term[:half]
    send_ref[...] = term[half:]


def encode(scal, frame, w_in, w_out, joint):
    tokens = ROWS * COLS
    any_spec = pl.BlockSpec(memory_space=pl.ANY)
    out = jax.ShapeDtypeStruct((tokens // 2, D), BF16)
    return pl.pallas_call(
        encode_kernel,
        name="encode",
        in_specs=[pl.BlockSpec(memory_space=pltpu.SMEM)] + [any_spec] * 4,
        out_shape=(out, out),
        scratch_shapes=[
            pltpu.VMEM((tokens, D), BF16),
            pltpu.VMEM((D, D), BF16),
            pltpu.VMEM((D, D), BF16),
            pltpu.VMEM((D, D), BF16),
            pltpu.SemaphoreType.DMA((4,)),
        ],
        compiler_params=pltpu.CompilerParams(vmem_limit_bytes=GRANT),
        cost_estimate=pl.CostEstimate(flops=2 * tokens * D * (3 * D + tokens), bytes_accessed=6_000_000, transcendentals=tokens * D),
    )(scal, frame, w_in, w_out, joint)


def noisy_kernel(scal, up_hbm, own_hbm, down_hbm, joint_hbm, out_ref, tokens, weight, sems):
    edge = up_hbm.shape[0]
    own = own_hbm.shape[0]
    copies = [
        pltpu.make_async_copy(joint_hbm.at[pl.ds(0, D), :], weight, sems.at[0]),
        pltpu.make_async_copy(up_hbm, tokens.at[pl.ds(0, edge), :], sems.at[1]),
        pltpu.make_async_copy(own_hbm, tokens.at[pl.ds(edge, own), :], sems.at[2]),
        pltpu.make_async_copy(down_hbm, tokens.at[pl.ds(edge + own, edge), :], sems.at[3]),
    ]
    for c in copies:
        c.start()
    row, col = window_place(256, scal[0])
    order = one_hot(row * COLS + col, 256)
    for c in copies:
        c.wait()
    for g in range(GROUPS):
        placed = dot(order, tokens[g * 256 : (g + 1) * 256, :]).astype(BF16)
        out_ref[g] = dot(placed, weight[...])


def noisy_share(scal, up, own, down, joint):
    any_spec = pl.BlockSpec(memory_space=pl.ANY)
    return pl.pallas_call(
        noisy_kernel,
        name="noisy_share",
        in_specs=[pl.BlockSpec(memory_space=pltpu.SMEM)] + [any_spec] * 4,
        out_specs=pl.BlockSpec(memory_space=pltpu.VMEM),
        out_shape=jax.ShapeDtypeStruct((GROUPS, 256, D), F32),
        scratch_shapes=[
            pltpu.VMEM((768, D), BF16),
            pltpu.VMEM((D, D), BF16),
            pltpu.SemaphoreType.DMA((4,)),
        ],
        compiler_params=pltpu.CompilerParams(vmem_limit_bytes=GRANT),
        cost_estimate=pl.CostEstimate(flops=2 * 768 * D * (D + 256), bytes_accessed=5_000_000, transcendentals=0),
    )(scal, up, own, down, joint)


def attend_kernel(scal, noisy_hbm, mine_hbm, other_hbm, strip_hbm, wq_hbm, wkv_hbm, wo_hbm, out_ref, bias_ref, stream_ref, normed_ref, qkv_ref, mixed_ref, wqkv, wo, noisy_ref, mine_ref, other_ref, strip_ref, sems):
    copies = [
        pltpu.make_async_copy(wq_hbm, wqkv.at[:, :D], sems.at[0]),
        pltpu.make_async_copy(wkv_hbm, wqkv.at[:, D:], sems.at[1]),
        pltpu.make_async_copy(wo_hbm, wo, sems.at[2]),
    ]
    early = [
        pltpu.make_async_copy(strip_hbm, strip_ref, sems.at[3]),
        pltpu.make_async_copy(mine_hbm, mine_ref, sems.at[4]),
        pltpu.make_async_copy(other_hbm, other_ref, sems.at[5]),
        pltpu.make_async_copy(noisy_hbm, noisy_ref, sems.at[6]),
    ]
    for c in early + copies:
        c.start()
    early[0].wait()
    shift = scal[0]
    core = scal[1]
    band = scal[2]
    last = scal[3]
    pairs = H // 2
    for h in range(H):
        for r in range(WIN):
            at = WIN * (WIN - 1 - r)
            bias_ref[h // 2, WIN * r : WIN * (r + 1), (h % 2) * HD : (h % 2 + 1) * HD] = strip_ref[h, :, at : at + HD]
    row, col = window_place(256, shift)
    half = COLS // 2
    place = (col % half) * WIN + row
    from_mine = one_hot(jnp.where(col // half == core, place, -1), 128)
    from_other = one_hot(jnp.where(col // half == core, -1, place), 128)
    for c in early[1:]:
        c.wait()
    for g in range(GROUPS):
        mine = mine_ref[:, g * WIN : (g + 1) * WIN, :].astype(F32).reshape(128, D).astype(BF16)
        other = other_ref[:, g * WIN : (g + 1) * WIN, :].astype(F32).reshape(128, D).astype(BF16)
        stream = (noisy_ref[g] + (dot(from_mine, mine) + dot(from_other, other))).astype(BF16)
        stream_ref[g * 256 : (g + 1) * 256, :] = stream
        normed_ref[g * 256 : (g + 1) * 256, :] = normalised(stream.astype(F32))
    copies[0].wait()
    copies[1].wait()
    for n in range(3):
        cols = slice(n * D, (n + 1) * D)
        qkv_ref[:, cols] = dot(normed_ref[...], wqkv[:, cols]).astype(BF16)
    low = lax.broadcasted_iota(jnp.int32, (64, 128), 1) < HD
    key_row = lax.broadcasted_iota(jnp.int32, (64, 128), 0)

    def window(w, carry):
        rows = pl.ds(pl.multiple_of(w * 64, 64), 64)
        hide_top = jnp.logical_and(w < 4, band == 0)
        hide_end = jnp.logical_and(w >= 8, band == last)
        first = jnp.where(hide_top, 32, 0)
        end = jnp.where(hide_end, 32, 64)
        seen = jnp.logical_and(key_row >= first, key_row < end)
        scores = []
        for p in range(pairs):
            q = qkv_ref[rows, p * 128 : (p + 1) * 128]
            k = qkv_ref[rows, D + p * 128 : D + (p + 1) * 128]
            zero = jnp.zeros_like(q)
            both = jnp.concatenate([jnp.where(low, q, zero), jnp.where(low, zero, q)], axis=0)
            scores.append(dot_nt(k, both))
        scores = [jnp.where(seen, s * HD ** (-0.5) + bias_ref[p], -1e30) for p, s in enumerate(scores)]
        tops = [jnp.max(s, axis=0, keepdims=True) for s in scores]
        weights = [jnp.exp(s - m) for s, m in zip(scores, tops)]
        sums = [1.0 / jnp.sum(e, axis=0, keepdims=True) for e in weights]
        probs = [(e * i).astype(BF16) for e, i in zip(weights, sums)]
        got = [dot_tn(probs[p], qkv_ref[rows, 2 * D + p * 128 : 2 * D + (p + 1) * 128]) for p in range(pairs)]
        for p in range(pairs):
            mixed_ref[rows, p * 128 : (p + 1) * 128] = jnp.where(low, got[p][:64], got[p][64:]).astype(BF16)
        return carry

    lax.fori_loop(0, 4 * GROUPS, window, 0, unroll=2)
    t = row_ids(128)
    moved = (t % COLS + shift) % COLS
    base = (moved // WIN) * 64 + (t // COLS) * WIN + moved % WIN
    for b in range(4):
        g, first = divmod(4 * b + 4, WIN)
        back = one_hot(base + first * WIN, 256)
        mixed = dot(back, mixed_ref[g * 256 : (g + 1) * 256, :]).astype(BF16)
        normed_ref[b * 128 : (b + 1) * 128, :] = mixed
        qkv_ref[b * 128 : (b + 1) * 128, :D] = dot(back, stream_ref[g * 256 : (g + 1) * 256, :]).astype(BF16)
    copies[2].wait()
    tokens = ROWS * COLS
    out_ref[...] = (qkv_ref[:tokens, :D].astype(F32) + dot(normed_ref[:tokens, :], wo[...])).astype(BF16)


def attend(scal, noisy, mine, other, strip, wq, wkv, wo):
    vmem = pl.BlockSpec(memory_space=pltpu.VMEM)
    any_spec = pl.BlockSpec(memory_space=pl.ANY)
    return pl.pallas_call(
        attend_kernel,
        name="attend",
        in_specs=[pl.BlockSpec(memory_space=pltpu.SMEM)] + [any_spec] * 7,
        out_specs=vmem,
        out_shape=jax.ShapeDtypeStruct((ROWS * COLS, D), BF16),
        scratch_shapes=[
            pltpu.VMEM((H // 2, 64, 128), F32),
            pltpu.VMEM((768, D), BF16),
            pltpu.VMEM((768, D), BF16),
            pltpu.VMEM((768, 3 * D), BF16),
            pltpu.VMEM((768, D), BF16),
            pltpu.VMEM((D, 3 * D), BF16),
            pltpu.VMEM((D, D), BF16),
            pltpu.VMEM(noisy.shape, F32),
            pltpu.VMEM(mine.shape, BF16),
            pltpu.VMEM(other.shape, BF16),
            pltpu.VMEM(strip.shape, F32),
            pltpu.SemaphoreType.DMA((7,)),
        ],
        compiler_params=pltpu.CompilerParams(vmem_limit_bytes=GRANT),
        cost_estimate=pl.CostEstimate(flops=2 * 768 * D * 5 * D, bytes_accessed=10_000_000, transcendentals=768 * 64 * 12),
    )(scal, noisy, mine, other, strip, wq, wkv, wo)


def forward_kernel(keep, att_hbm, *refs):
    ups = refs[0:5]
    downs = refs[5:10]
    out_ref, up, down, total, att_ref, sems = refs[10:]
    taken = pltpu.make_async_copy(att_hbm, att_ref, sems.at[40])
    taken.start()
    unit = 96
    copies = []
    for i in range(4):
        for j in range(4):
            slot = 4 * i + j
            pair = []
            for side, (pieces, held, far, at) in enumerate(((ups, up, i, j), (downs, down, j, i))):
                sem = sems.at[2 * slot + side]
                if far < 3:
                    pair.append(pltpu.make_async_copy(pieces[far].at[at], held.at[pl.ds(slot * unit, unit), :], sem))
                else:
                    h = unit // 2
                    pair.append(pltpu.make_async_copy(pieces[3].at[at], held.at[pl.ds(slot * unit, h), :], sem))
                    pair.append(pltpu.make_async_copy(pieces[4].at[at], held.at[pl.ds(slot * unit + h, h), :], sems.at[32 + 2 * (j if side == 0 else i) + side]))
            for c in pair:
                c.start()
            copies.append(pair)
    taken.wait()
    x = att_ref[...].astype(F32)
    second = normalised(x)
    for n in range(2):
        for pair in copies[8 * n : 8 * n + 8]:
            for c in pair:
                c.wait()
        rows = slice(n * 768, (n + 1) * 768)
        hidden = jax.nn.gelu(dot_nt(second, up[rows, :])).astype(BF16)
        part = dot(hidden, down[rows, :])
        if n == 0:
            total[...] = x + part if keep else part
        else:
            out_ref[...] = (total[...] + part).astype(out_ref.dtype)


def feed_forward(keep, att, ups, downs):
    tokens = ROWS * COLS
    vmem = pl.BlockSpec(memory_space=pltpu.VMEM)
    hbm = pl.BlockSpec(memory_space=pl.ANY)
    return pl.pallas_call(
        lambda *refs: forward_kernel(keep, *refs),
        name="feed_forward_own" if keep else "feed_forward_partner",
        in_specs=[hbm] * 11,
        out_specs=vmem,
        out_shape=jax.ShapeDtypeStruct((tokens, D), F32 if keep else BF16),
        scratch_shapes=[
            pltpu.VMEM((FF // 2, D), BF16),
            pltpu.VMEM((FF // 2, D), BF16),
            pltpu.VMEM((tokens, D), F32),
            pltpu.VMEM((tokens, D), BF16),
            pltpu.SemaphoreType.DMA((41,)),
        ],
        compiler_params=pltpu.CompilerParams(vmem_limit_bytes=GRANT),
        cost_estimate=pl.CostEstimate(flops=2 * tokens * D * FF, bytes_accessed=6_000_000, transcendentals=tokens * FF // 2),
    )(att, *ups, *downs)


def swap(x, axis):
    return lax.ppermute(x, axis, [(0, 1), (1, 0)])


def ring_from_all(mine, axis):
    on = [(i, (i + 1) % 4) for i in range(4)]
    back = [(i, (i - 1) % 4) for i in range(4)]
    behind = lax.ppermute(mine, axis, on)
    ahead = lax.ppermute(mine, axis, back)
    half = mine.shape[1] // 2
    far_on = lax.ppermute(behind[:, :half], axis, on)
    return [mine, behind, ahead, far_on, lax.ppermute(ahead[:, half:], axis, back)]


def row_from_all(mine, axis):
    moves = (1, -1, 2)
    got = [lax.ppermute(mine, axis, [(i, (i + by) % 4) for i in range(4)]) for by in moves]
    return jnp.stack([mine, *got], axis=0)


def gathered_weights(expand, reduce):
    n = expand.shape[0]
    across = swap(jnp.concatenate([expand, reduce], axis=0), "mz")
    ups = row_from_all(jnp.concatenate([expand, across[:n]], axis=0), "mx")
    downs = row_from_all(jnp.concatenate([reduce, across[n:]], axis=0), "my")
    return ring_from_all(ups, "my"), ring_from_all(downs, "mx")


def strip_choice():
    lane = lax.optimization_barrier(jnp.arange(WIN * 15 * WIN))
    key_col = lane // (15 * WIN)
    block = lane // WIN % 15
    wanted = (14 - block) * 15 + key_col - lane % WIN + 7
    return jnp.where(jnp.arange(225)[:, None] == wanted[None, :], 1.0, 0.0).astype(F32)


def body(
    noisy_latents,
    frames,
    encoder_members,
    window_shift,
    encoder_in,
    encoder_out,
    joint_weight,
    query_weight,
    keyvalue_weight,
    output_weight,
    position_bias,
    expand_weight,
    reduce_weight,
):
    tokens = ROWS * COLS
    margin = WIN // 2
    bands = lax.axis_size("lat")
    member = lax.axis_index(MEMBER)
    core = lax.axis_index("core")
    is_second = member == encoder_members[1]
    is_source = jnp.logical_or(member == encoder_members[0], is_second)
    shift = window_shift[0]
    noisy = noisy_latents.reshape(tokens, D)
    down_pairs = [(i, i + 1) for i in range(bands - 1)]
    up_pairs = [(i + 1, i) for i in range(bands - 1)]
    edge = margin * COLS

    enc_scal = jnp.stack([is_source.astype(jnp.int32), 1 + is_second.astype(jnp.int32), core])
    keep, send = encode(enc_scal, frames.reshape(tokens, D), encoder_in, encoder_out, joint_weight)

    noisy_up = lax.ppermute(noisy[tokens - edge :], "lat", down_pairs)
    noisy_down = lax.ppermute(noisy[:edge], "lat", up_pairs)
    ups, downs = gathered_weights(expand_weight, reduce_weight)

    mine = (keep + swap(send, "core")).reshape(COLS // 2, ROWS, D)
    spread = lax.all_to_all(mine, PLANE, 0, 0, tiled=True)
    part = jnp.sum(spread.astype(F32), axis=0).astype(BF16)
    above = lax.ppermute(part[ROWS - margin :], "lat", down_pairs)
    below = lax.ppermute(part[:margin], "lat", up_pairs)
    part = jnp.concatenate([above, part, below], axis=0)
    part = part + swap(part, "mz")
    wide = jnp.broadcast_to(part[None], (COLS // 2, *part.shape))
    mine = lax.all_to_all(wide, PLANE, 0, 0, tiled=True)
    other = swap(mine, "core")

    noisy_wide = noisy_share(jnp.stack([shift, shift]), noisy_up, noisy, noisy_down, joint_weight)
    strip = jnp.dot(position_bias, strip_choice(), precision=lax.Precision.HIGHEST, preferred_element_type=F32)
    strip = strip.reshape(H, WIN, 15 * WIN)
    att_scal = jnp.stack([shift, core, lax.axis_index("lat"), jnp.int32(bands - 1)])
    attended = attend(att_scal, noisy_wide, mine, other, strip, query_weight, keyvalue_weight, output_weight)
    partner = swap(attended, "core")
    own = feed_forward(True, attended, ups, downs)
    theirs = feed_forward(False, partner, ups, downs)
    back = swap(theirs, "core")
    return (own + back.astype(F32)).astype(BF16).reshape(noisy_latents.shape)


def solution(mesh):
    finer = Mesh(mesh.devices.reshape(4, 4, 2, 2, mesh.shape["lat"]), (*MEMBER, "lat"))
    placed = (
        P(MEMBER, "lat", None, None),
        P(MEMBER, "lat", None, None),
        *([P()] * 9),
        P(MEMBER, None),
        P(MEMBER, None),
    )
    return jax.shard_map(
        body,
        mesh=finer,
        in_specs=placed,
        out_specs=P(MEMBER, "lat", None, None),
        check_vma=False,
    )
```

profile of v0, /device:TPU:71, one launch (start us, length us, event | category | flops | bytes accessed | tf_op | source)
XLA Modules:
  0.0 134.0 jit_solution(12280430230231722327)
XLA Ops:
  0.0 1.4 %fusion.19 = (s32[1]{0:T(128)}, s32[1]{0:T(128)}) fusion(s32[2]{0:T(128)} %param.15), kind=kLoop, calls=%fused_computation.40 | loop fusion | bytes 16 | tf_op jit(solution)/shard_map/slice | solution.py:375
  2.7 0.6 pad_add_fusion.2.scal
  3.4 6.3 %encode.1 = (bf16[256,768]{1,0:T(8,128)(2,1)}, bf16[256,768]{1,0:T(8,128)(2,1)}) custom-call(s32[3]{0:T(128)} %pad_add_fusion.2.scal, bf16[512,768]{1,0:T(8,128)(2,1)} %bitcast.34, bf16[768,768]{1,0:T(8,128)(2,1)} %in_hbm.1, bf16[768,768]{1,0:T(8,128)(2,1)} %out_hbm.1, bf16[2304,768]{1,0:T(8,128)(2,1)} %joint_hbm.3), custom_call_target="tpu_custom_call" | custom-call | flops 2214592512 | bytes 6000000 | tf_op jit(solution)/shard_map/encode/pallas_call | solution.py:90
  9.7 0.0 copy-start.1
  9.7 0.8 collective-permute-start.2
  10.5 1.6 %collective-permute-done.2 = bf16[256,768]{1,0:T(8,128)(2,1)S(1)} collective-permute-done((bf16[256,768]{1,0:T(8,128)(2,1)}, bf16[256,768]{1,0:T(8,128)(2,1)S(1)}, u32[]{:S(2)}, u32[]{:S(2)}) %collective-permute-start.2) | collective-permute-done | bytes 393248 | tf_op jit(solution)/shard_map/ppermute | solution.py:319
  12.0 1.9 %add.44 = bf16[256,768]{1,0:T(8,128)(2,1)} add(bf16[256,768]{1,0:T(8,128)(2,1)} %get-tuple-element.7, bf16[256,768]{1,0:T(8,128)(2,1)S(1)} %collective-permute-done.2) | non-fusion elementwise | flops 196608 | bytes 1179648 | tf_op jit(solution)/shard_map/add | solution.py:389
  13.9 6.9 %all-to-all-start = ((bf16[16,16,768]{2,1,0:T(8,128)(2,1)}), bf16[16,16,768]{2,1,0:T(8,128)(2,1)S(1)}, u32[]{:S(2)}, u32[]{:S(2)}) async-start(bf16[16,16,768]{2,1,0:T(8,128)(2,1)} %bitcast.10), calls=%async_computation | async-start | bytes 786432 | tf_op jit(solution)/shard_map/all_to_all | solution.py:390
  20.8 6.1 %collective-permute-start = (bf16[128,768]{1,0:T(8,128)(2,1)S(1)}, bf16[128,768]{1,0:T(8,128)(2,1)S(1)}, u32[]{:S(2)}, u32[]{:S(2)}) collective-permute-start(bf16[128,768]{1,0:T(8,128)(2,1)S(1)} %bitcast.27), channel_id=1, source_target_pairs={{0,1},{1,2},{2,3},{4,5},{5,6},{6,7},{8,9},{9,10},{10,11},{12,13},{... | collective-permute-start | bytes 589832 | tf_op jit(solution)/shard_map/ppermute | solution.py:385
  26.9 1.9 %collective-permute-start.1 = (bf16[128,768]{1,0:T(8,128)(2,1)S(1)}, bf16[128,768]{1,0:T(8,128)(2,1)S(1)}, u32[]{:S(2)}, u32[]{:S(2)}) collective-permute-start(bf16[128,768]{1,0:T(8,128)(2,1)S(1)} %bitcast.26), channel_id=1, source_target_pairs={{1,0},{2,1},{3,2},{5,4},{6,5},{7,6},{9,8},{10,9},{11,10},{13,12},{... | collective-permute-start | bytes 589832 | tf_op jit(solution)/shard_map/ppermute | solution.py:386
  28.9 0.0 all-to-all-done
  28.9 0.1 reduce_sum.12
  29.0 5.5 %collective-permute-start.3 = (bf16[4,768]{1,0:T(4,128)(2,1)S(1)}, bf16[4,768]{1,0:T(4,128)(2,1)S(1)}, u32[]{:S(2)}, u32[]{:S(2)}) collective-permute-start(bf16[4,768]{1,0:T(4,128)(2,1)S(1)} %get-tuple-element.17), channel_id=1, source_target_pairs={{0,1},{1,2},{2,3},{4,5},{5,6},{6,7},{8,9},{9,10},{10,11},{12,13},{... | collective-permute-start | bytes 18440 | tf_op jit(solution)/shard_map/ppermute | solution.py:392
  34.4 1.9 %collective-permute-start.4 = (bf16[4,768]{1,0:T(4,128)(2,1)S(1)}, bf16[4,768]{1,0:T(4,128)(2,1)S(1)}, u32[]{:S(2)}, u32[]{:S(2)}) collective-permute-start(bf16[4,768]{1,0:T(4,128)(2,1)S(1)} %get-tuple-element.18), channel_id=1, source_target_pairs={{1,0},{2,1},{3,2},{5,4},{6,5},{7,6},{9,8},{10,9},{11,10},{13,12},{... | collective-permute-start | bytes 18440 | tf_op jit(solution)/shard_map/ppermute | solution.py:393
  36.4 0.8 collective-permute-start.7
  37.2 0.0 collective-permute-done.3
  37.2 4.3 %collective-permute-done.4 = bf16[4,768]{1,0:T(4,128)(2,1)S(1)} collective-permute-done((bf16[4,768]{1,0:T(4,128)(2,1)S(1)}, bf16[4,768]{1,0:T(4,128)(2,1)S(1)}, u32[]{:S(2)}, u32[]{:S(2)}) %collective-permute-start.4) | collective-permute-done | bytes 6176 | tf_op jit(solution)/shard_map/ppermute | solution.py:393
  41.6 0.9 collective-permute-start.5
  43.2 2.3 %collective-permute-done.5 = bf16[24,768]{1,0:T(8,128)(2,1)S(1)} collective-permute-done((bf16[24,768]{1,0:T(8,128)(2,1)S(1)}, bf16[24,768]{1,0:T(8,128)(2,1)S(1)}, u32[]{:S(2)}, u32[]{:S(2)}) %collective-permute-start.5) | collective-permute-done | bytes 36896 | tf_op jit(solution)/shard_map/ppermute | solution.py:319
  45.5 0.9 broadcast_in_dim.16
  46.3 6.7 %all-to-all-start.1 = ((bf16[16,24,768]{2,1,0:T(8,128)(2,1)}), bf16[16,24,768]{2,1,0:T(8,128)(2,1)S(1)}, u32[]{:S(2)}, u32[]{:S(2)}) async-start(bf16[16,24,768]{2,1,0:T(8,128)(2,1)} %broadcast_in_dim.16), calls=%async_computation.1 | async-start | bytes 1179648 | tf_op jit(solution)/shard_map/all_to_all | solution.py:397
  53.0 0.7 convolution_bitcast_fusion
  53.8 0.2 collective-permute-start.8
  54.0 1.4 %collective-permute-start.9 = (bf16[96,768]{1,0:T(8,128)(2,1)S(1)}, bf16[96,768]{1,0:T(8,128)(2,1)S(1)}, u32[]{:S(2)}, u32[]{:S(2)}) collective-permute-start(bf16[96,768]{1,0:T(8,128)(2,1)S(1)} %get-tuple-element.21), channel_id=1, source_target_pairs={{0,192},{64,0},{128,64},{192,128},{1,193},{65,1},{129,65},{193,129... | collective-permute-start | bytes 442376 | tf_op jit(solution)/shard_map/ppermute | solution.py:334
  55.3 5.3 %all-to-all-done.1.mine_hbm = bf16[16,24,768]{2,1,0:T(8,128)(2,1)S(1)} async-done(((bf16[16,24,768]{2,1,0:T(8,128)(2,1)}), bf16[16,24,768]{2,1,0:T(8,128)(2,1)S(1)}, u32[]{:S(2)}, u32[]{:S(2)}) %all-to-all-start.1) | async-done | bytes 589856 | tf_op jit(solution)/shard_map/all_to_all | solution.py:397
  60.6 5.4 %collective-permute-start.6 = (bf16[16,24,768]{2,1,0:T(8,128)(2,1)S(1)}, bf16[16,24,768]{2,1,0:T(8,128)(2,1)}, u32[]{:S(2)}, u32[]{:S(2)}) collective-permute-start(bf16[16,24,768]{2,1,0:T(8,128)(2,1)S(1)} %all-to-all-done.1.mine_hbm), channel_id=1, source_target_pairs={{0,4},{4,0},{1,5},{5,1},{2,6},{6,2},{3,7},{7,3},{8,12},{12,8},{9,1... | collective-permute-start | bytes 1769480 | tf_op jit(solution)/shard_map/ppermute | solution.py:319
  66.0 0.6 pad_add_fusion.1.scal
  66.7 1.0 collective-permute-start.10
  67.7 0.7 pad_add_fusion.scal
  68.4 0.7 reshape.22.strip_hbm
  69.0 0.0 collective-permute-done.1.down_hbm
  69.1 0.1 collective-permute-start.15
  69.1 2.6 %collective-permute-start.16 = (bf16[96,768]{1,0:T(8,128)(2,1)S(1)}, bf16[96,768]{1,0:T(8,128)(2,1)S(1)}, u32[]{:S(2)}, u32[]{:S(2)}) collective-permute-start(bf16[96,768]{1,0:T(8,128)(2,1)S(1)} %get-tuple-element.12), channel_id=1, source_target_pairs={{0,48},{16,0},{32,16},{48,32},{1,49},{17,1},{33,17},{49,33},{2,50}... | collective-permute-start | bytes 442376 | tf_op jit(solution)/shard_map/ppermute | solution.py:334
  71.7 0.0 collective-permute-done.9
  71.7 0.2 collective-permute-start.17
  71.9 5.2 %noisy_share.1.noisy_hbm = f32[3,256,768]{2,1,0:T(8,128)} custom-call(s32[2]{0:T(128)} %pad_add_fusion.1.scal, bf16[128,768]{1,0:T(8,128)(2,1)} %copy-done.7, bf16[512,768]{1,0:T(8,128)(2,1)} %bitcast.25, bf16[128,768]{1,0:T(8,128)(2,1)} %copy-done.8, bf16[2304,768]{1,0:T(8,128)(2,1)} %joint_hbm.3), custom_call_target="tpu_custom_call" | custom-call | flops 1207959552 | bytes 5000000 | tf_op jit(solution)/shard_map/noisy_share/pallas_call | solution.py:129
  77.1 0.1 pad_maximum_fusion.refs_1_
  77.2 0.8 collective-permute-start.11
  78.0 2.0 %collective-permute-start.12 = (bf16[4,96,768]{2,1,0:T(8,128)(2,1)S(1)}, bf16[4,96,768]{2,1,0:T(8,128)(2,1)}, u32[]{:S(2)}, u32[]{:S(2)}) collective-permute-start(bf16[4,96,768]{2,1,0:T(8,128)(2,1)S(1)} %pad_maximum_fusion.refs_1_), channel_id=1, source_target_pairs={{0,48},{16,0},{32,16},{48,32},{1,49},{17,1},{33,17},{49,33},{2,50}... | collective-permute-start | bytes 1769480 | tf_op jit(solution)/shard_map/ppermute | solution.py:326
  80.0 0.0 collective-permute-done.16
  80.0 0.0 collective-permute-done.17
  80.0 0.1 pad_maximum_fusion.1.refs_6_
  80.1 1.6 %collective-permute-start.18 = (bf16[4,96,768]{2,1,0:T(8,128)(2,1)S(1)}, bf16[4,96,768]{2,1,0:T(8,128)(2,1)S(1)}, u32[]{:S(2)}, u32[]{:S(2)}) collective-permute-start(bf16[4,96,768]{2,1,0:T(8,128)(2,1)S(1)} %pad_maximum_fusion.1.refs_6_), channel_id=1, source_target_pairs={{0,64},{64,128},{128,192},{192,0},{1,65},{65,129},{129,193},{193,1... | collective-permute-start | bytes 1769480 | tf_op jit(solution)/shard_map/ppermute | solution.py:325
  81.7 14.3 %attend.1.refs_0_ = bf16[512,768]{1,0:T(8,128)(2,1)} custom-call(s32[4]{0:T(128)} %pad_add_fusion.scal, f32[3,256,768]{2,1,0:T(8,128)} %noisy_share.1.noisy_hbm, bf16[16,24,768]{2,1,0:T(8,128)(2,1)} %copy-done.2, bf16[16,24,768]{2,1,0:T(8,128)(2,1)} %collective-permute-done.6.other_hbm, f32[12,8,120]{2,1,0:T(8,128)} %reshape.22.strip_hbm, ...), custom_call_target="tpu_custom_call" | custom-call | flops 4529848320 | bytes 10000000 | tf_op jit(solution)/shard_map/attend/pallas_call | solution.py:232
  96.0 2.4 %collective-permute-start.22 = (bf16[512,768]{1,0:T(8,128)(2,1)}, bf16[512,768]{1,0:T(8,128)(2,1)}, u32[]{:S(2)}, u32[]{:S(2)}) collective-permute-start(bf16[512,768]{1,0:T(8,128)(2,1)} %attend.1.refs_0_), channel_id=1, source_target_pairs={{0,4},{4,0},{1,5},{5,1},{2,6},{6,2},{3,7},{7,3},{8,12},{12,8},{9,1... | collective-permute-start | bytes 2359304 | tf_op jit(solution)/shard_map/ppermute | solution.py:319
  98.4 1.0 slice.59
  99.4 0.1 collective-permute-start.13
  99.4 0.0 collective-permute-done.12.refs_3_
  99.5 1.0 slice.60
  100.4 2.9 %collective-permute-start.14 = (bf16[4,48,768]{2,1,0:T(8,128)(2,1)S(1)}, bf16[4,48,768]{2,1,0:T(8,128)(2,1)S(1)}, u32[]{:S(2)}, u32[]{:S(2)}) collective-permute-start(bf16[4,48,768]{2,1,0:T(8,128)(2,1)S(1)} %slice.60), channel_id=1, source_target_pairs={{0,48},{16,0},{32,16},{48,32},{1,49},{17,1},{33,17},{49,33},{2,50}... | collective-permute-start | bytes 884744 | tf_op jit(solution)/shard_map/ppermute | solution.py:329
  103.4 0.0 collective-permute-done.18.refs_7_
  103.4 2.8 %collective-permute-start.20 = (bf16[4,48,768]{2,1,0:T(8,128)(2,1)S(1)}, bf16[4,48,768]{2,1,0:T(8,128)(2,1)S(1)}, u32[]{:S(2)}, u32[]{:S(2)}) collective-permute-start(bf16[4,48,768]{2,1,0:T(8,128)(2,1)S(1)} %slice.62), channel_id=1, source_target_pairs={{0,64},{64,128},{128,192},{192,0},{1,65},{65,129},{129,193},{193,1... | collective-permute-start | bytes 884744 | tf_op jit(solution)/shard_map/ppermute | solution.py:328
  106.2 0.0 collective-permute-done.19.refs_8_
  106.2 1.0 slice.63
  107.2 0.1 collective-permute-start.21
  107.3 1.9 %collective-permute-done.13.refs_4_ = bf16[4,48,768]{2,1,0:T(8,128)(2,1)S(1)} collective-permute-done((bf16[4,48,768]{2,1,0:T(8,128)(2,1)S(1)}, bf16[4,48,768]{2,1,0:T(8,128)(2,1)S(1)}, u32[]{:S(2)}, u32[]{:S(2)}) %collective-permute-start.13) | collective-permute-done | bytes 294944 | tf_op jit(solution)/shard_map/ppermute | solution.py:328
  109.2 0.3 collective-permute-done.14.refs_5_
  109.5 2.5 %collective-permute-done.20.refs_9_ = bf16[4,48,768]{2,1,0:T(8,128)(2,1)S(1)} collective-permute-done((bf16[4,48,768]{2,1,0:T(8,128)(2,1)S(1)}, bf16[4,48,768]{2,1,0:T(8,128)(2,1)S(1)}, u32[]{:S(2)}, u32[]{:S(2)}) %collective-permute-start.20) | collective-permute-done | bytes 294944 | tf_op jit(solution)/shard_map/ppermute | solution.py:328
  112.0 4.2 %collective-permute-done.21.refs_10_ = bf16[4,48,768]{2,1,0:T(8,128)(2,1)S(1)} collective-permute-done((bf16[4,48,768]{2,1,0:T(8,128)(2,1)S(1)}, bf16[4,48,768]{2,1,0:T(8,128)(2,1)S(1)}, u32[]{:S(2)}, u32[]{:S(2)}) %collective-permute-start.21) | collective-permute-done | bytes 294944 | tf_op jit(solution)/shard_map/ppermute | solution.py:329
  116.2 0.7 copy-done.13
  116.9 6.3 %feed_forward_partner.1 = bf16[512,768]{1,0:T(8,128)(2,1)} custom-call(bf16[512,768]{1,0:T(8,128)(2,1)} %collective-permute-done.22.refs_0_, bf16[4,96,768]{2,1,0:T(8,128)(2,1)} %copy-done.3, bf16[4,96,768]{2,1,0:T(8,128)(2,1)} %collective-permute-done.11.refs_2_, bf16[4,96,768]{2,1,0:T(8,128)(2,1)} %collective-permute-done.12.refs_3_, ...), custom_call_target="tpu_custom_call" | custom-call | flops 2415919104 | bytes 6000000 | tf_op jit(solution)/shard_map/feed_forward_partner/pallas_call | solution.py:300
  123.2 1.8 %collective-permute-start.23 = (bf16[512,768]{1,0:T(8,128)(2,1)}, bf16[512,768]{1,0:T(8,128)(2,1)S(1)}, u32[]{:S(2)}, u32[]{:S(2)}) collective-permute-start(bf16[512,768]{1,0:T(8,128)(2,1)} %feed_forward_partner.1), channel_id=1, source_target_pairs={{0,4},{4,0},{1,5},{5,1},{2,6},{6,2},{3,7},{7,3},{8,12},{12,8},{9,1... | collective-permute-start | bytes 2359304 | tf_op jit(solution)/shard_map/ppermute | solution.py:319
  125.0 6.5 %feed_forward_own.1 = f32[512,768]{1,0:T(8,128)} custom-call(bf16[512,768]{1,0:T(8,128)(2,1)} %attend.1.refs_0_, bf16[4,96,768]{2,1,0:T(8,128)(2,1)} %copy-done.3, bf16[4,96,768]{2,1,0:T(8,128)(2,1)} %collective-permute-done.11.refs_2_, bf16[4,96,768]{2,1,0:T(8,128)(2,1)} %collective-permute-done.12.refs_3_, bf16[4,48,768]{2,1,0:T(8,128)(2,1)} %copy-done.10, ...), custom_call_target="tpu_custom_call" | custom-call | flops 2415919104 | bytes 6000000 | tf_op jit(solution)/shard_map/feed_forward_own/pallas_call | solution.py:300
  131.5 2.5 %add_convert_fusion = bf16[512,768]{1,0:T(8,128)(2,1)} fusion(f32[512,768]{1,0:T(8,128)} %feed_forward_own.1, bf16[512,768]{1,0:T(8,128)(2,1)S(1)} %collective-permute-done.23), kind=kLoop, calls=%fused_computation | loop fusion | flops 1179648 | bytes 3145728 | tf_op jit(solution)/shard_map/convert_element_type | solution.py:409
  (46 shorter events, 0.3 us)
Async XLA Ops:
  0.0 53.0 %copy-start = (f32[12,225]{1,0:T(8,128)S(1)}, f32[12,225]{1,0:T(8,128)}, u32[]{:S(2)}) copy-start(f32[12,225]{1,0:T(8,128)} %param.23) | copy-start | bytes 32404
  9.7 11.1 %copy-start.1 = (bf16[1,16,32,768]{3,2,1,0:T(8,128)(2,1)S(1)}, bf16[1,16,32,768]{3,2,1,0:T(8,128)(2,1)}, u32[]{:S(2)}) copy-start(bf16[1,16,32,768]{3,2,1,0:T(8,128)(2,1)} %param.13) | copy-start | bytes 2359300
  9.7 2.3 %collective-permute-start.2 = (bf16[256,768]{1,0:T(8,128)(2,1)}, bf16[256,768]{1,0:T(8,128)(2,1)S(1)}, u32[]{:S(2)}, u32[]{:S(2)}) collective-permute-start(bf16[256,768]{1,0:T(8,128)(2,1)} %get-tuple-element.8), channel_id=1, source_target_pairs={{0,4},{4,0},{1,5},{5,1},{2,6},{6,2},{3,7},{7,3},{8,12},{12,8},{9,1... | collective-permute-start | bytes 1179656 | tf_op jit(solution)/shard_map/ppermute | solution.py:319
  12.0 24.3 %copy-start.5 = (bf16[48,768]{1,0:T(8,128)(2,1)S(1)}, bf16[48,768]{1,0:T(8,128)(2,1)}, u32[]{:S(2)}) copy-start(bf16[48,768]{1,0:T(8,128)(2,1)} %param.24) | copy-start | bytes 221188
  12.0 24.3 %copy-start.6 = (bf16[48,768]{1,0:T(8,128)(2,1)S(1)}, bf16[48,768]{1,0:T(8,128)(2,1)}, u32[]{:S(2)}) copy-start(bf16[48,768]{1,0:T(8,128)(2,1)} %param.25) | copy-start | bytes 221188
  13.9 15.0 %all-to-all-start = ((bf16[16,16,768]{2,1,0:T(8,128)(2,1)}), bf16[16,16,768]{2,1,0:T(8,128)(2,1)S(1)}, u32[]{:S(2)}, u32[]{:S(2)}) async-start(bf16[16,16,768]{2,1,0:T(8,128)(2,1)} %bitcast.10), calls=%async_computation | async-start | bytes 786432 | tf_op jit(solution)/shard_map/all_to_all | solution.py:390
  20.8 45.8 %collective-permute-start = (bf16[128,768]{1,0:T(8,128)(2,1)S(1)}, bf16[128,768]{1,0:T(8,128)(2,1)S(1)}, u32[]{:S(2)}, u32[]{:S(2)}) collective-permute-start(bf16[128,768]{1,0:T(8,128)(2,1)S(1)} %bitcast.27), channel_id=1, source_target_pairs={{0,1},{1,2},{2,3},{4,5},{5,6},{6,7},{8,9},{9,10},{10,11},{12,13},{... | collective-permute-start | bytes 589832 | tf_op jit(solution)/shard_map/ppermute | solution.py:385
  26.9 42.1 %collective-permute-start.1 = (bf16[128,768]{1,0:T(8,128)(2,1)S(1)}, bf16[128,768]{1,0:T(8,128)(2,1)S(1)}, u32[]{:S(2)}, u32[]{:S(2)}) collective-permute-start(bf16[128,768]{1,0:T(8,128)(2,1)S(1)} %bitcast.26), channel_id=1, source_target_pairs={{1,0},{2,1},{3,2},{5,4},{6,5},{7,6},{9,8},{10,9},{11,10},{13,12},{... | collective-permute-start | bytes 589832 | tf_op jit(solution)/shard_map/ppermute | solution.py:386
  29.0 8.3 %collective-permute-start.3 = (bf16[4,768]{1,0:T(4,128)(2,1)S(1)}, bf16[4,768]{1,0:T(4,128)(2,1)S(1)}, u32[]{:S(2)}, u32[]{:S(2)}) collective-permute-start(bf16[4,768]{1,0:T(4,128)(2,1)S(1)} %get-tuple-element.17), channel_id=1, source_target_pairs={{0,1},{1,2},{2,3},{4,5},{5,6},{6,7},{8,9},{9,10},{10,11},{12,13},{... | collective-permute-start | bytes 18440 | tf_op jit(solution)/shard_map/ppermute | solution.py:392
  34.4 7.1 %collective-permute-start.4 = (bf16[4,768]{1,0:T(4,128)(2,1)S(1)}, bf16[4,768]{1,0:T(4,128)(2,1)S(1)}, u32[]{:S(2)}, u32[]{:S(2)}) collective-permute-start(bf16[4,768]{1,0:T(4,128)(2,1)S(1)} %get-tuple-element.18), channel_id=1, source_target_pairs={{1,0},{2,1},{3,2},{5,4},{6,5},{7,6},{9,8},{10,9},{11,10},{13,12},{... | collective-permute-start | bytes 18440 | tf_op jit(solution)/shard_map/ppermute | solution.py:393
  36.4 17.3 %collective-permute-start.7 = (bf16[96,768]{1,0:T(8,128)(2,1)S(1)}, bf16[96,768]{1,0:T(8,128)(2,1)S(1)}, u32[]{:S(2)}, u32[]{:S(2)}) collective-permute-start(bf16[96,768]{1,0:T(8,128)(2,1)S(1)} %pad_maximum_fusion.2), channel_id=1, source_target_pairs={{0,8},{8,0},{1,9},{9,1},{2,10},{10,2},{3,11},{11,3},{4,12},{12,4},... | collective-permute-start | bytes 442376 | tf_op jit(solution)/shard_map/ppermute | solution.py:319
  41.6 3.9 %collective-permute-start.5 = (bf16[24,768]{1,0:T(8,128)(2,1)S(1)}, bf16[24,768]{1,0:T(8,128)(2,1)S(1)}, u32[]{:S(2)}, u32[]{:S(2)}) collective-permute-start(bf16[24,768]{1,0:T(8,128)(2,1)S(1)} %pad_maximum_fusion.5), channel_id=1, source_target_pairs={{0,8},{8,0},{1,9},{9,1},{2,10},{10,2},{3,11},{11,3},{4,12},{12,4},... | collective-permute-start | bytes 110600 | tf_op jit(solution)/shard_map/ppermute | solution.py:319
  46.3 14.3 %all-to-all-start.1 = ((bf16[16,24,768]{2,1,0:T(8,128)(2,1)}), bf16[16,24,768]{2,1,0:T(8,128)(2,1)S(1)}, u32[]{:S(2)}, u32[]{:S(2)}) async-start(bf16[16,24,768]{2,1,0:T(8,128)(2,1)} %broadcast_in_dim.16), calls=%async_computation.1 | async-start | bytes 1179648 | tf_op jit(solution)/shard_map/all_to_all | solution.py:397
  53.8 15.3 %collective-permute-start.8 = (bf16[96,768]{1,0:T(8,128)(2,1)S(1)}, bf16[96,768]{1,0:T(8,128)(2,1)S(1)}, u32[]{:S(2)}, u32[]{:S(2)}) collective-permute-start(bf16[96,768]{1,0:T(8,128)(2,1)S(1)} %get-tuple-element.21), channel_id=1, source_target_pairs={{0,64},{64,128},{128,192},{192,0},{1,65},{65,129},{129,193},{193,1... | collective-permute-start | bytes 442376 | tf_op jit(solution)/shard_map/ppermute | solution.py:334
  54.0 17.8 %collective-permute-start.9 = (bf16[96,768]{1,0:T(8,128)(2,1)S(1)}, bf16[96,768]{1,0:T(8,128)(2,1)S(1)}, u32[]{:S(2)}, u32[]{:S(2)}) collective-permute-start(bf16[96,768]{1,0:T(8,128)(2,1)S(1)} %get-tuple-element.21), channel_id=1, source_target_pairs={{0,192},{64,0},{128,64},{192,128},{1,193},{65,1},{129,65},{193,129... | collective-permute-start | bytes 442376 | tf_op jit(solution)/shard_map/ppermute | solution.py:334
  60.6 16.5 %copy-start.2 = (bf16[16,24,768]{2,1,0:T(8,128)(2,1)}, bf16[16,24,768]{2,1,0:T(8,128)(2,1)S(1)}, u32[]{:S(2)}) copy-start(bf16[16,24,768]{2,1,0:T(8,128)(2,1)S(1)} %all-to-all-done.1.mine_hbm) | copy-start | bytes 1769476
  60.6 21.0 %collective-permute-start.6 = (bf16[16,24,768]{2,1,0:T(8,128)(2,1)S(1)}, bf16[16,24,768]{2,1,0:T(8,128)(2,1)}, u32[]{:S(2)}, u32[]{:S(2)}) collective-permute-start(bf16[16,24,768]{2,1,0:T(8,128)(2,1)S(1)} %all-to-all-done.1.mine_hbm), channel_id=1, source_target_pairs={{0,4},{4,0},{1,5},{5,1},{2,6},{6,2},{3,7},{7,3},{8,12},{12,8},{9,1... | collective-permute-start | bytes 1769480 | tf_op jit(solution)/shard_map/ppermute | solution.py:319
  66.7 5.2 %copy-start.7 = (bf16[128,768]{1,0:T(8,128)(2,1)}, bf16[128,768]{1,0:T(8,128)(2,1)S(1)}, u32[]{:S(2)}) copy-start(bf16[128,768]{1,0:T(8,128)(2,1)S(1)} %collective-permute-done.up_hbm) | copy-start | bytes 589828
  66.7 10.4 %collective-permute-start.10 = (bf16[96,768]{1,0:T(8,128)(2,1)S(1)}, bf16[96,768]{1,0:T(8,128)(2,1)S(1)}, u32[]{:S(2)}, u32[]{:S(2)}) collective-permute-start(bf16[96,768]{1,0:T(8,128)(2,1)S(1)} %get-tuple-element.21), channel_id=1, source_target_pairs={{0,128},{64,192},{128,0},{192,64},{1,129},{65,193},{129,1},{193,65... | collective-permute-start | bytes 442376 | tf_op jit(solution)/shard_map/ppermute | solution.py:334
  69.1 2.8 %copy-start.8 = (bf16[128,768]{1,0:T(8,128)(2,1)}, bf16[128,768]{1,0:T(8,128)(2,1)S(1)}, u32[]{:S(2)}) copy-start(bf16[128,768]{1,0:T(8,128)(2,1)S(1)} %collective-permute-done.1.down_hbm) | copy-start | bytes 589828
  69.1 9.0 %collective-permute-start.15 = (bf16[96,768]{1,0:T(8,128)(2,1)S(1)}, bf16[96,768]{1,0:T(8,128)(2,1)S(1)}, u32[]{:S(2)}, u32[]{:S(2)}) collective-permute-start(bf16[96,768]{1,0:T(8,128)(2,1)S(1)} %get-tuple-element.12), channel_id=1, source_target_pairs={{0,16},{16,32},{32,48},{48,0},{1,17},{17,33},{33,49},{49,1},{2,18}... | collective-permute-start | bytes 442376 | tf_op jit(solution)/shard_map/ppermute | solution.py:334
  69.1 10.9 %collective-permute-start.16 = (bf16[96,768]{1,0:T(8,128)(2,1)S(1)}, bf16[96,768]{1,0:T(8,128)(2,1)S(1)}, u32[]{:S(2)}, u32[]{:S(2)}) collective-permute-start(bf16[96,768]{1,0:T(8,128)(2,1)S(1)} %get-tuple-element.12), channel_id=1, source_target_pairs={{0,48},{16,0},{32,16},{48,32},{1,49},{17,1},{33,17},{49,33},{2,50}... | collective-permute-start | bytes 442376 | tf_op jit(solution)/shard_map/ppermute | solution.py:334
  71.7 8.3 %collective-permute-start.17 = (bf16[96,768]{1,0:T(8,128)(2,1)S(1)}, bf16[96,768]{1,0:T(8,128)(2,1)S(1)}, u32[]{:S(2)}, u32[]{:S(2)}) collective-permute-start(bf16[96,768]{1,0:T(8,128)(2,1)S(1)} %get-tuple-element.12), channel_id=1, source_target_pairs={{0,32},{16,48},{32,0},{48,16},{1,33},{17,49},{33,1},{49,17},{2,34}... | collective-permute-start | bytes 442376 | tf_op jit(solution)/shard_map/ppermute | solution.py:334
  77.2 18.7 %copy-start.3 = (bf16[4,96,768]{2,1,0:T(8,128)(2,1)}, bf16[4,96,768]{2,1,0:T(8,128)(2,1)S(1)}, u32[]{:S(2)}) copy-start(bf16[4,96,768]{2,1,0:T(8,128)(2,1)S(1)} %pad_maximum_fusion.refs_1_) | copy-start | bytes 1769476
  77.2 21.1 %collective-permute-start.11 = (bf16[4,96,768]{2,1,0:T(8,128)(2,1)S(1)}, bf16[4,96,768]{2,1,0:T(8,128)(2,1)}, u32[]{:S(2)}, u32[]{:S(2)}) collective-permute-start(bf16[4,96,768]{2,1,0:T(8,128)(2,1)S(1)} %pad_maximum_fusion.refs_1_), channel_id=1, source_target_pairs={{0,16},{16,32},{32,48},{48,0},{1,17},{17,33},{33,49},{49,1},{2,18}... | collective-permute-start | bytes 1769480 | tf_op jit(solution)/shard_map/ppermute | solution.py:325
  78.0 21.4 %collective-permute-start.12 = (bf16[4,96,768]{2,1,0:T(8,128)(2,1)S(1)}, bf16[4,96,768]{2,1,0:T(8,128)(2,1)}, u32[]{:S(2)}, u32[]{:S(2)}) collective-permute-start(bf16[4,96,768]{2,1,0:T(8,128)(2,1)S(1)} %pad_maximum_fusion.refs_1_), channel_id=1, source_target_pairs={{0,48},{16,0},{32,16},{48,32},{1,49},{17,1},{33,17},{49,33},{2,50}... | collective-permute-start | bytes 1769480 | tf_op jit(solution)/shard_map/ppermute | solution.py:326
  80.1 15.9 %copy-start.4 = (bf16[4,96,768]{2,1,0:T(8,128)(2,1)}, bf16[4,96,768]{2,1,0:T(8,128)(2,1)S(1)}, u32[]{:S(2)}) copy-start(bf16[4,96,768]{2,1,0:T(8,128)(2,1)S(1)} %pad_maximum_fusion.1.refs_6_) | copy-start | bytes 1769476
  80.1 23.3 %collective-permute-start.18 = (bf16[4,96,768]{2,1,0:T(8,128)(2,1)S(1)}, bf16[4,96,768]{2,1,0:T(8,128)(2,1)S(1)}, u32[]{:S(2)}, u32[]{:S(2)}) collective-permute-start(bf16[4,96,768]{2,1,0:T(8,128)(2,1)S(1)} %pad_maximum_fusion.1.refs_6_), channel_id=1, source_target_pairs={{0,64},{64,128},{128,192},{192,0},{1,65},{65,129},{129,193},{193,1... | collective-permute-start | bytes 1769480 | tf_op jit(solution)/shard_map/ppermute | solution.py:325
  81.7 24.5 %collective-permute-start.19 = (bf16[4,96,768]{2,1,0:T(8,128)(2,1)S(1)}, bf16[4,96,768]{2,1,0:T(8,128)(2,1)}, u32[]{:S(2)}, u32[]{:S(2)}) collective-permute-start(bf16[4,96,768]{2,1,0:T(8,128)(2,1)S(1)} %pad_maximum_fusion.1.refs_6_), channel_id=1, source_target_pairs={{0,192},{64,0},{128,64},{192,128},{1,193},{65,1},{129,65},{193,129... | collective-permute-start | bytes 1769480 | tf_op jit(solution)/shard_map/ppermute | solution.py:326
  96.0 20.2 %collective-permute-start.22 = (bf16[512,768]{1,0:T(8,128)(2,1)}, bf16[512,768]{1,0:T(8,128)(2,1)}, u32[]{:S(2)}, u32[]{:S(2)}) collective-permute-start(bf16[512,768]{1,0:T(8,128)(2,1)} %attend.1.refs_0_), channel_id=1, source_target_pairs={{0,4},{4,0},{1,5},{5,1},{2,6},{6,2},{3,7},{7,3},{8,12},{12,8},{9,1... | collective-permute-start | bytes 2359304 | tf_op jit(solution)/shard_map/ppermute | solution.py:319
  99.4 9.8 %collective-permute-start.13 = (bf16[4,48,768]{2,1,0:T(8,128)(2,1)S(1)}, bf16[4,48,768]{2,1,0:T(8,128)(2,1)S(1)}, u32[]{:S(2)}, u32[]{:S(2)}) collective-permute-start(bf16[4,48,768]{2,1,0:T(8,128)(2,1)S(1)} %slice.59), channel_id=1, source_target_pairs={{0,16},{16,32},{32,48},{48,0},{1,17},{17,33},{33,49},{49,1},{2,18}... | collective-permute-start | bytes 884744 | tf_op jit(solution)/shard_map/ppermute | solution.py:328
  100.4 9.0 %collective-permute-start.14 = (bf16[4,48,768]{2,1,0:T(8,128)(2,1)S(1)}, bf16[4,48,768]{2,1,0:T(8,128)(2,1)S(1)}, u32[]{:S(2)}, u32[]{:S(2)}) collective-permute-start(bf16[4,48,768]{2,1,0:T(8,128)(2,1)S(1)} %slice.60), channel_id=1, source_target_pairs={{0,48},{16,0},{32,16},{48,32},{1,49},{17,1},{33,17},{49,33},{2,50}... | collective-permute-start | bytes 884744 | tf_op jit(solution)/shard_map/ppermute | solution.py:329
  103.4 12.8 %copy-start.9 = (bf16[4,96,768]{2,1,0:T(8,128)(2,1)}, bf16[4,96,768]{2,1,0:T(8,128)(2,1)S(1)}, u32[]{:S(2)}) copy-start(bf16[4,96,768]{2,1,0:T(8,128)(2,1)S(1)} %collective-permute-done.18.refs_7_) | copy-start | bytes 1769476
  103.4 8.6 %collective-permute-start.20 = (bf16[4,48,768]{2,1,0:T(8,128)(2,1)S(1)}, bf16[4,48,768]{2,1,0:T(8,128)(2,1)S(1)}, u32[]{:S(2)}, u32[]{:S(2)}) collective-permute-start(bf16[4,48,768]{2,1,0:T(8,128)(2,1)S(1)} %slice.62), channel_id=1, source_target_pairs={{0,64},{64,128},{128,192},{192,0},{1,65},{65,129},{129,193},{193,1... | collective-permute-start | bytes 884744 | tf_op jit(solution)/shard_map/ppermute | solution.py:328
  107.2 9.0 %collective-permute-start.21 = (bf16[4,48,768]{2,1,0:T(8,128)(2,1)S(1)}, bf16[4,48,768]{2,1,0:T(8,128)(2,1)S(1)}, u32[]{:S(2)}, u32[]{:S(2)}) collective-permute-start(bf16[4,48,768]{2,1,0:T(8,128)(2,1)S(1)} %slice.63), channel_id=1, source_target_pairs={{0,192},{64,0},{128,64},{192,128},{1,193},{65,1},{129,65},{193,129... | collective-permute-start | bytes 884744 | tf_op jit(solution)/shard_map/ppermute | solution.py:329
  109.2 7.0 %copy-start.10 = (bf16[4,48,768]{2,1,0:T(8,128)(2,1)}, bf16[4,48,768]{2,1,0:T(8,128)(2,1)S(1)}, u32[]{:S(2)}) copy-start(bf16[4,48,768]{2,1,0:T(8,128)(2,1)S(1)} %collective-permute-done.13.refs_4_) | copy-start | bytes 884740
  109.5 6.8 %copy-start.11 = (bf16[4,48,768]{2,1,0:T(8,128)(2,1)}, bf16[4,48,768]{2,1,0:T(8,128)(2,1)S(1)}, u32[]{:S(2)}) copy-start(bf16[4,48,768]{2,1,0:T(8,128)(2,1)S(1)} %collective-permute-done.14.refs_5_) | copy-start | bytes 884740
  112.0 4.2 %copy-start.12 = (bf16[4,48,768]{2,1,0:T(8,128)(2,1)}, bf16[4,48,768]{2,1,0:T(8,128)(2,1)S(1)}, u32[]{:S(2)}) copy-start(bf16[4,48,768]{2,1,0:T(8,128)(2,1)S(1)} %collective-permute-done.20.refs_9_) | copy-start | bytes 884740
  116.2 0.7 copy-start.13
  123.2 8.4 %collective-permute-start.23 = (bf16[512,768]{1,0:T(8,128)(2,1)}, bf16[512,768]{1,0:T(8,128)(2,1)S(1)}, u32[]{:S(2)}, u32[]{:S(2)}) collective-permute-start(bf16[512,768]{1,0:T(8,128)(2,1)} %feed_forward_partner.1), channel_id=1, source_target_pairs={{0,4},{4,0},{1,5},{5,1},{2,6},{6,2},{3,7},{7,3},{8,12},{12,8},{9,1... | collective-permute-start | bytes 2359304 | tf_op jit(solution)/shard_map/ppermute | solution.py:319
where the time goes:
time: 135 us; the launch traced here: 134 us
  starting transfers between devices  56.7 us (42%)
  Pallas kernels  38.6 us (29%)
  waiting for transfers between devices  22.4 us (17%)
  local copies, waits for them, and re-layouts  6.66 us (5%)
  other arithmetic  6.65 us (5%)
  between operations  2.31 us (2%)
    pallas_call x1, Pallas kernels, attend(): pl.pallas_call(attend_kernel, name='attend', in_specs=[pl.BlockSpec(memor...  14.3 us
    pallas_call x2, Pallas kernels, feed_forward(): pl.pallas_call(lambda *refs: forward_kernel(keep, *refs), name='feed_forw...  12.8 us
    ppermute x6, starting transfers between devices, swap(): return lax.ppermute(x, axis, [(0, 1), (1, 0)])  12.1 us
    all_to_all x1, starting transfers between devices, body(): spread = lax.all_to_all(mine, PLANE, 0, 0, tiled=True)  6.87 us
    all_to_all x1, starting transfers between devices, body(): mine = lax.all_to_all(wide, PLANE, 0, 0, tiled=True)  6.67 us
    pallas_call x1, Pallas kernels, encode(): pl.pallas_call(encode_kernel, name='encode', in_specs=[pl.BlockSpec(memor...  6.34 us
    ppermute x1, starting transfers between devices, body(): noisy_up = lax.ppermute(noisy[tokens - edge:], 'lat', down_pairs)  6.11 us
    ppermute x1, starting transfers between devices, body(): above = lax.ppermute(part[ROWS - margin:], 'lat', down_pairs)  5.47 us
  transfers between devices with their start and end apart: 26, of which 8 were waited for; matrix products, arithmetic and copies ran while one was open for 5% of the time, Pallas kernels for 19%

commit v1 on v0

v1 whole, which is shorter than its diff:
```python
import jax
import jax.numpy as jnp
from jax import lax
from jax.experimental import pallas as pl
from jax.experimental.pallas import tpu as pltpu
from jax.sharding import Mesh
from jax.sharding import PartitionSpec as P

HD = 64
WIN = 8
D = 768
H = 12
FF = 3072
ROWS = 16
COLS = 32
NLAT = 64
GROUPS = 3
MEMBER = ("mx", "my", "mz", "core")
PLANE = ("mx", "my")
EPS = 1e-06
F32 = jnp.float32
BF16 = jnp.bfloat16
axis_index = lax.axis_index


def in_hbm(x):
    return pltpu.with_memory_space_constraint(x, pltpu.HBM)


def dot(a, b):
    return jnp.dot(a, b, preferred_element_type=F32)


def dot_nt(a, b):
    return lax.dot_general(a, b, (((1,), (1,)), ((), ())), preferred_element_type=F32)


def dot_tn(a, b):
    return lax.dot_general(a, b, (((0,), (0,)), ((), ())), preferred_element_type=F32)


def normalised(x):
    scale = lax.rsqrt(jnp.mean(x * x, axis=-1, keepdims=True) + EPS)
    return (x * scale).astype(BF16)


def one_hot(wanted, width):
    lanes = lax.broadcasted_iota(jnp.int32, (wanted.shape[0], width), 1)
    return jnp.where(lanes == wanted, 1.0, 0.0).astype(BF16)


def row_ids(count):
    return lax.broadcasted_iota(jnp.int32, (count, 1), 0)


def window_place(count, shift):
    t = row_ids(count)
    row = (t // WIN) % WIN
    col = ((t // (WIN * WIN)) * WIN + t % WIN - shift + COLS) % COLS
    return row, col


def encode_kernel(chosen, frame_hbm, in_hbm, out_hbm, joint_hbm, keep_ref, send_ref, frame, w_in, w_out, w_slot, sems):
    own_core = axis_index("core")
    member = axis_index(MEMBER)
    is_second = member == chosen[1]
    is_source = jnp.logical_or(member == chosen[0], is_second)
    slot = jnp.where(is_second, 2, 1)
    copies = [
        pltpu.make_async_copy(frame_hbm, frame, sems.at[0]),
        pltpu.make_async_copy(in_hbm, w_in, sems.at[1]),
        pltpu.make_async_copy(out_hbm, w_out, sems.at[2]),
        pltpu.make_async_copy(joint_hbm.at[pl.ds(pl.multiple_of(slot * D, D), D), :], w_slot, sems.at[3]),
    ]
    for c in copies:
        c.start()
    tokens = ROWS * COLS
    t = row_ids(tokens)
    half = tokens // 2
    core = jnp.where(t < half, own_core, 1 - own_core)
    col = core * (COLS // 2) + (t % half) // ROWS
    order = one_hot((t % ROWS) * COLS + col, tokens)
    copies[0].wait()
    ordered = dot(order, frame[...]).astype(BF16)
    copies[1].wait()
    hidden = jax.nn.gelu(dot(ordered, w_in[...])).astype(BF16)
    copies[2].wait()
    condition = dot(hidden, w_out[...]).astype(BF16)
    copies[3].wait()
    term = dot(condition, w_slot[...])
    term = jnp.where(is_source, term, 0.0).astype(BF16)
    keep_ref[...] = term[:half]
    send_ref[...] = term[half:]


def encode(chosen, frame, w_in, w_out, joint):
    tokens = ROWS * COLS
    any_spec = pl.BlockSpec(memory_space=pltpu.HBM)
    out = jax.ShapeDtypeStruct((tokens // 2, D), BF16)
    return pl.pallas_call(
        encode_kernel,
        name="encode",
        in_specs=[pl.BlockSpec(memory_space=pltpu.SMEM)] + [any_spec] * 4,
        out_shape=(out, out),
        scratch_shapes=[
            pltpu.VMEM((tokens, D), BF16),
            pltpu.VMEM((D, D), BF16),
            pltpu.VMEM((D, D), BF16),
            pltpu.VMEM((D, D), BF16),
            pltpu.SemaphoreType.DMA((4,)),
        ],
        compiler_params=pltpu.CompilerParams(vmem_limit_bytes=24 << 20),
        cost_estimate=pl.CostEstimate(flops=2 * tokens * D * (3 * D + tokens), bytes_accessed=6_000_000, transcendentals=tokens * D),
    )(chosen, *map(in_hbm, (frame, w_in, w_out, joint)))


def attend_kernel(shift_ref, up_ref, own_ref, down_ref, mine_ref, other_ref, strip_ref, w0_hbm, wq_hbm, wkv_hbm, wo_hbm, out_ref, bias_ref, stream_ref, normed_ref, qkv_ref, mixed_ref, w0, wqkv, wo, sems):
    copies = [
        pltpu.make_async_copy(w0_hbm.at[pl.ds(0, D), :], w0, sems.at[0]),
        pltpu.make_async_copy(wq_hbm, wqkv.at[:, :D], sems.at[1]),
        pltpu.make_async_copy(wkv_hbm, wqkv.at[:, D:], sems.at[2]),
        pltpu.make_async_copy(wo_hbm, wo, sems.at[3]),
    ]
    for c in copies:
        c.start()
    shift = shift_ref[0]
    core = axis_index("core")
    band = axis_index("lat")
    last = NLAT // ROWS - 1
    pairs = H // 2
    for h in range(H):
        for r in range(WIN):
            at = WIN * (WIN - 1 - r)
            bias_ref[h // 2, WIN * r : WIN * (r + 1), (h % 2) * HD : (h % 2 + 1) * HD] = strip_ref[h, :, at : at + HD]
    row, col = window_place(256, shift)
    half = COLS // 2
    place = (col % half) * WIN + row
    from_mine = one_hot(jnp.where(col // half == core, place, -1), 128)
    from_other = one_hot(jnp.where(col // half == core, -1, place), 128)
    order = one_hot(row * COLS + col, 256)
    tokens = ((up_ref[...], own_ref[:128, :]), (own_ref[128:384, :],), (own_ref[384:, :], down_ref[...]))
    for g in range(GROUPS):
        placed = dot(order, jnp.concatenate(tokens[g], axis=0) if len(tokens[g]) > 1 else tokens[g][0])
        mixed_ref[g * 256 : (g + 1) * 256, :] = placed.astype(BF16)
    copies[0].wait()
    noisy = dot(mixed_ref[...], w0[...])
    for g in range(GROUPS):
        mine = mine_ref[:, g * WIN : (g + 1) * WIN, :].astype(F32).reshape(128, D).astype(BF16)
        other = other_ref[:, g * WIN : (g + 1) * WIN, :].astype(F32).reshape(128, D).astype(BF16)
        stream = (noisy[g * 256 : (g + 1) * 256] + (dot(from_mine, mine) + dot(from_other, other))).astype(BF16)
        stream_ref[g * 256 : (g + 1) * 256, :] = stream
        normed_ref[g * 256 : (g + 1) * 256, :] = normalised(stream.astype(F32))
    copies[1].wait()
    copies[2].wait()
    for n in range(3):
        cols = slice(n * D, (n + 1) * D)
        qkv_ref[:, cols] = dot(normed_ref[...], wqkv[:, cols]).astype(BF16)
    low = lax.broadcasted_iota(jnp.int32, (64, 128), 1) < HD
    key_row = lax.broadcasted_iota(jnp.int32, (64, 128), 0)

    def window(w, carry):
        rows = pl.ds(pl.multiple_of(w * 64, 64), 64)
        hide_top = jnp.logical_and(w < 4, band == 0)
        hide_end = jnp.logical_and(w >= 8, band == last)
        first = jnp.where(hide_top, 32, 0)
        end = jnp.where(hide_end, 32, 64)
        seen = jnp.logical_and(key_row >= first, key_row < end)
        scores = []
        for p in range(pairs):
            q = qkv_ref[rows, p * 128 : (p + 1) * 128]
            k = qkv_ref[rows, D + p * 128 : D + (p + 1) * 128]
            zero = jnp.zeros_like(q)
            both = jnp.concatenate([jnp.where(low, q, zero), jnp.where(low, zero, q)], axis=0)
            scores.append(dot_nt(k, both))
        scores = [jnp.where(seen, s * HD ** (-0.5) + bias_ref[p], -1e30) for p, s in enumerate(scores)]
        tops = [jnp.max(s, axis=0, keepdims=True) for s in scores]
        weights = [jnp.exp(s - m) for s, m in zip(scores, tops)]
        sums = [1.0 / jnp.sum(e, axis=0, keepdims=True) for e in weights]
        probs = [(e * i).astype(BF16) for e, i in zip(weights, sums)]
        got = [dot_tn(probs[p], qkv_ref[rows, 2 * D + p * 128 : 2 * D + (p + 1) * 128]) for p in range(pairs)]
        for p in range(pairs):
            mixed_ref[rows, p * 128 : (p + 1) * 128] = jnp.where(low, got[p][:64], got[p][64:]).astype(BF16)
        return carry

    lax.fori_loop(0, 4 * GROUPS, window, 0, unroll=2)
    t = row_ids(128)
    moved = (t % COLS + shift) % COLS
    base = (moved // WIN) * 64 + (t // COLS) * WIN + moved % WIN
    for b in range(4):
        g, first = divmod(4 * b + 4, WIN)
        back = one_hot(base + first * WIN, 256)
        mixed = dot(back, mixed_ref[g * 256 : (g + 1) * 256, :]).astype(BF16)
        normed_ref[b * 128 : (b + 1) * 128, :] = mixed
        qkv_ref[b * 128 : (b + 1) * 128, :D] = dot(back, stream_ref[g * 256 : (g + 1) * 256, :]).astype(BF16)
    copies[3].wait()
    tokens = ROWS * COLS
    out_ref[...] = (qkv_ref[:tokens, :D].astype(F32) + dot(normed_ref[:tokens, :], wo[...])).astype(BF16)


def attend(shift, up, own, down, mine, other, strip, joint, wq, wkv, wo):
    args = (up, own, down, mine, other, strip)
    return pl.pallas_call(
        attend_kernel,
        name="attend",
        in_specs=[
            pl.BlockSpec(memory_space=pltpu.SMEM),
            *(pl.BlockSpec(memory_space=pltpu.VMEM) for _ in args),
            *(pl.BlockSpec(memory_space=pltpu.HBM) for _ in range(4)),
        ],
        out_specs=pl.BlockSpec(memory_space=pltpu.VMEM),
        out_shape=jax.ShapeDtypeStruct((ROWS * COLS, D), BF16),
        scratch_shapes=[
            pltpu.VMEM((H // 2, 64, 128), F32),
            pltpu.VMEM((768, D), BF16),
            pltpu.VMEM((768, D), BF16),
            pltpu.VMEM((768, 3 * D), BF16),
            pltpu.VMEM((768, D), BF16),
            pltpu.VMEM((D, D), BF16),
            pltpu.VMEM((D, 3 * D), BF16),
            pltpu.VMEM((D, D), BF16),
            pltpu.SemaphoreType.DMA((4,)),
        ],
        compiler_params=pltpu.CompilerParams(vmem_limit_bytes=36 << 20),
        cost_estimate=pl.CostEstimate(flops=2 * 768 * D * 6 * D, bytes_accessed=10_000_000, transcendentals=768 * 64 * 12),
    )(shift, *args, *map(in_hbm, (joint, wq, wkv, wo)))


def forward_kernel(keep, att_ref, *refs):
    ups = refs[0:4]
    downs = refs[4:8]
    out_ref, total = refs[8:]
    unit = ups[0].shape[1]
    x = att_ref[...].astype(F32)
    second = normalised(x)
    for n in range(2):
        rings = (2 * n, 2 * n + 1)
        up = jnp.concatenate([ups[i][...].reshape(4 * unit, D) for i in rings], axis=0)
        hidden = jax.nn.gelu(dot_nt(second, up)).astype(BF16)
        down = jnp.concatenate([downs[j][i] for i in rings for j in range(4)], axis=0)
        part = dot(hidden, down)
        if n == 0:
            total[...] = x + part if keep else part
        else:
            out_ref[...] = (total[...] + part).astype(out_ref.dtype)


def feed_forward(keep, att, ups, downs):
    tokens = ROWS * COLS
    vmem = pl.BlockSpec(memory_space=pltpu.VMEM)
    return pl.pallas_call(
        lambda *refs: forward_kernel(keep, *refs),
        name="feed_forward_own" if keep else "feed_forward_partner",
        in_specs=[vmem] * 9,
        out_specs=vmem,
        out_shape=jax.ShapeDtypeStruct((tokens, D), F32 if keep else BF16),
        scratch_shapes=[pltpu.VMEM((tokens, D), F32)],
        compiler_params=pltpu.CompilerParams(vmem_limit_bytes=20 << 20),
        cost_estimate=pl.CostEstimate(flops=2 * tokens * D * FF, bytes_accessed=6_000_000, transcendentals=tokens * FF // 2),
    )(att, *ups, *downs)


def swap(x, axis):
    return lax.ppermute(x, axis, [(0, 1), (1, 0)])


def ring_from_all(mine, axis):
    on = [(i, (i + 1) % 4) for i in range(4)]
    back = [(i, (i - 1) % 4) for i in range(4)]
    behind = lax.ppermute(mine, axis, on)
    ahead = lax.ppermute(mine, axis, back)
    return [mine, behind, ahead, lax.ppermute(behind, axis, on)]


def row_from_all(mine, axis):
    moves = (1, -1, 2)
    got = [lax.ppermute(mine, axis, [(i, (i + by) % 4) for i in range(4)]) for by in moves]
    return jnp.stack([mine, *got], axis=0)


def gathered_weights(expand, reduce):
    n = expand.shape[0]
    across = swap(jnp.concatenate([expand, reduce], axis=0), "mz")
    ups = row_from_all(jnp.concatenate([expand, across[:n]], axis=0), "mx")
    downs = row_from_all(jnp.concatenate([reduce, across[n:]], axis=0), "my")
    return ring_from_all(ups, "my"), ring_from_all(downs, "mx")


def strip_choice():
    lane = lax.optimization_barrier(jnp.arange(WIN * 15 * WIN))
    key_col = lane // (15 * WIN)
    block = lane // WIN % 15
    wanted = (14 - block) * 15 + key_col - lane % WIN + 7
    return jnp.where(jnp.arange(225)[:, None] == wanted[None, :], 1.0, 0.0).astype(F32)


def body(
    noisy_latents,
    frames,
    encoder_members,
    window_shift,
    encoder_in,
    encoder_out,
    joint_weight,
    query_weight,
    keyvalue_weight,
    output_weight,
    position_bias,
    expand_weight,
    reduce_weight,
):
    tokens = ROWS * COLS
    margin = WIN // 2
    bands = lax.axis_size("lat")
    noisy = noisy_latents.reshape(tokens, D)
    to_next = [(i, (i + 1) % bands) for i in range(bands)]
    to_last = [(i, (i - 1) % bands) for i in range(bands)]
    edge = margin * COLS

    keep, send = encode(encoder_members, frames.reshape(tokens, D), encoder_in, encoder_out, joint_weight)
    ups, downs = gathered_weights(expand_weight, reduce_weight)
    noisy_up = lax.ppermute(noisy[tokens - edge :], "lat", to_next)
    noisy_down = lax.ppermute(noisy[:edge], "lat", to_last)

    mine = (keep + swap(send, "core")).reshape(COLS // 2, ROWS, D)
    spread = lax.all_to_all(mine, PLANE, 0, 0, tiled=True)
    part = jnp.sum(spread.astype(F32), axis=0).astype(BF16)
    above = lax.ppermute(part[ROWS - margin :], "lat", to_next)
    below = lax.ppermute(part[:margin], "lat", to_last)
    part = jnp.concatenate([above, part, below], axis=0)
    part = part + swap(part, "mz")
    wide = jnp.broadcast_to(part[None], (COLS // 2, *part.shape))
    mine = lax.all_to_all(wide, PLANE, 0, 0, tiled=True)
    other = swap(mine, "core")

    strip = jnp.dot(position_bias, strip_choice(), precision=lax.Precision.HIGHEST, preferred_element_type=F32)
    strip = strip.reshape(H, WIN, 15 * WIN)
    attended = attend(
        window_shift, noisy_up, noisy, noisy_down, mine, other, strip, joint_weight, query_weight, keyvalue_weight, output_weight
    )
    partner = swap(attended, "core")
    own = feed_forward(True, attended, ups, downs)
    theirs = feed_forward(False, partner, ups, downs)
    back = swap(theirs, "core")
    return (own + back.astype(F32)).astype(BF16).reshape(noisy_latents.shape)


def solution(mesh):
    finer = Mesh(mesh.devices.reshape(4, 4, 2, 2, mesh.shape["lat"]), (*MEMBER, "lat"))
    placed = (
        P(MEMBER, "lat", None, None),
        P(MEMBER, "lat", None, None),
        *([P()] * 9),
        P(MEMBER, None),
        P(MEMBER, None),
    )
    return jax.shard_map(
        body,
        mesh=finer,
        in_specs=placed,
        out_specs=P(MEMBER, "lat", None, None),
        check_vma=False,
    )
```

time: 135 us -> 119 us (0.88)
  the two profiles are of different devices: /device:TPU:71 before, /device:TPU:32 now
where the time goes in v1:
time: 119 us; the launch traced here: 118 us
  waiting for transfers between devices  36.7 us (31%)
  starting transfers between devices  33.5 us (28%)
  Pallas kernels  24.5 us (21%)
  blocking collectives  17.1 us (14%)
  other arithmetic  3.08 us (3%)
  local copies, waits for them, and re-layouts  1.68 us (1%)
    all_to_all x1, blocking collectives, body(): spread = lax.all_to_all(mine, PLANE, 0, 0, tiled=True)  17.1 us
    pallas_call x1, Pallas kernels, attend(): pl.pallas_call(attend_kernel, name='attend', in_specs=[pl.BlockSpec(memor...  13.2 us
    ppermute x2, waiting for transfers between devices, ring_from_all(): ahead = lax.ppermute(mine, axis, back)  12.5 us
    ppermute x6, starting transfers between devices, row_from_all(): lax.ppermute(mine, axis, [(i, (i + by) % 4) for i in range(4)])  11.1 us
    ppermute x6, waiting for transfers between devices, row_from_all(): lax.ppermute(mine, axis, [(i, (i + by) % 4) for i in range(4)])  5.94 us
    pallas_call x2, Pallas kernels, feed_forward(): pl.pallas_call(lambda *refs: forward_kernel(keep, *refs), name='feed_forw...  5.82 us
    pallas_call x1, Pallas kernels, encode(): pl.pallas_call(encode_kernel, name='encode', in_specs=[pl.BlockSpec(memor...  5.42 us
    ppermute x1, waiting for transfers between devices, body(): noisy_down = lax.ppermute(noisy[:edge], 'lat', to_last)  4.49 us
  transfers between devices with their start and end apart: 23, of which 12 were waited for; matrix products, arithmetic and copies ran while one was open for 3% of the time, Pallas kernels for 14%

profile of v1, /device:TPU:32, one launch (start us, length us, event | category | flops | bytes accessed | tf_op | source)
XLA Modules:
  0.0 118.1 jit_solution(6274676608449457991)
XLA Ops:
  0.0 0.7 copy-done.2
  0.7 5.4 %encode.1 = (bf16[256,768]{1,0:T(8,128)(2,1)S(1)}, bf16[256,768]{1,0:T(8,128)(2,1)S(1)}) custom-call(s32[2]{0:T(128)S(1)} %copy-done.2, bf16[512,768]{1,0:T(8,128)(2,1)} %bitcast.28, bf16[768,768]{1,0:T(8,128)(2,1)} %in_hbm.1, bf16[768,768]{1,0:T(8,128)(2,1)} %out_hbm.1, bf16[2304,768]{1,0:T(8,128)(2,1)} %w0_hbm.1), custom_call_target="tpu_custom_call" | custom-call | flops 2214592512 | bytes 6000000 | tf_op jit(solution)/shard_map/encode/pallas_call | solution.py:100
  6.1 0.0 copy-start.3
  6.1 0.0 copy-start.4
  6.1 0.1 collective-permute-start.2
  6.2 1.7 %collective-permute-done.2 = bf16[256,768]{1,0:T(8,128)(2,1)S(1)} collective-permute-done((bf16[256,768]{1,0:T(8,128)(2,1)S(1)}, bf16[256,768]{1,0:T(8,128)(2,1)S(1)}, u32[]{:S(2)}, u32[]{:S(2)}) %collective-permute-start.2) | collective-permute-done | bytes 393248 | tf_op jit(solution)/shard_map/ppermute | solution.py:263
  7.9 0.1 add.28
  8.0 0.0 copy-start.1
  8.0 17.1 %all_to_all.10 = bf16[16,16,768]{2,1,0:T(8,128)(2,1)S(1)} all-to-all(bf16[16,16,768]{2,1,0:T(8,128)(2,1)S(1)} %bitcast.20), channel_id=1, replica_groups=mesh['mx'=4,'my'=4,'mz'=2,'core'=2,'lat'=4] {'mx','my'}, dimensions={0} | all-to-all | bytes 786432 | tf_op jit(solution)/shard_map/all_to_all | solution.py:325
  25.1 0.1 reduce_sum.12
  25.2 3.3 %collective-permute-start.3 = (bf16[4,768]{1,0:T(4,128)(2,1)S(1)}, bf16[4,768]{1,0:T(4,128)(2,1)S(1)}, u32[]{:S(2)}, u32[]{:S(2)}) collective-permute-start(bf16[4,768]{1,0:T(4,128)(2,1)S(1)} %get-tuple-element.17), channel_id=1, source_target_pairs={{0,1},{1,2},{2,3},{3,0},{4,5},{5,6},{6,7},{7,4},{8,9},{9,10},{10,1... | collective-permute-start | bytes 18440 | tf_op jit(solution)/shard_map/ppermute | solution.py:327
  28.6 2.2 %collective-permute-start.4 = (bf16[4,768]{1,0:T(4,128)(2,1)S(1)}, bf16[4,768]{1,0:T(4,128)(2,1)S(1)}, u32[]{:S(2)}, u32[]{:S(2)}) collective-permute-start(bf16[4,768]{1,0:T(4,128)(2,1)S(1)} %get-tuple-element.18), channel_id=1, source_target_pairs={{0,3},{1,0},{2,1},{3,2},{4,7},{5,4},{6,5},{7,6},{8,11},{9,8},{10,9... | collective-permute-start | bytes 18440 | tf_op jit(solution)/shard_map/ppermute | solution.py:328
  30.8 1.5 %collective-permute-done.3 = bf16[4,768]{1,0:T(4,128)(2,1)S(1)} collective-permute-done((bf16[4,768]{1,0:T(4,128)(2,1)S(1)}, bf16[4,768]{1,0:T(4,128)(2,1)S(1)}, u32[]{:S(2)}, u32[]{:S(2)}) %collective-permute-start.3) | collective-permute-done | bytes 6176 | tf_op jit(solution)/shard_map/ppermute | solution.py:327
  32.3 1.4 %collective-permute-done.4 = bf16[4,768]{1,0:T(4,128)(2,1)S(1)} collective-permute-done((bf16[4,768]{1,0:T(4,128)(2,1)S(1)}, bf16[4,768]{1,0:T(4,128)(2,1)S(1)}, u32[]{:S(2)}, u32[]{:S(2)}) %collective-permute-start.4) | collective-permute-done | bytes 6176 | tf_op jit(solution)/shard_map/ppermute | solution.py:328
  33.8 1.1 collective-permute-start.5
  34.9 1.1 collective-permute-start.7
  36.0 1.8 %collective-permute-done.5 = bf16[24,768]{1,0:T(8,128)(2,1)S(1)} collective-permute-done((bf16[24,768]{1,0:T(8,128)(2,1)S(1)}, bf16[24,768]{1,0:T(8,128)(2,1)S(1)}, u32[]{:S(2)}, u32[]{:S(2)}) %collective-permute-start.5) | collective-permute-done | bytes 36896 | tf_op jit(solution)/shard_map/ppermute | solution.py:263
  37.8 0.9 broadcast_in_dim.16
  38.7 3.7 %all-to-all-start.1 = ((bf16[16,24,768]{2,1,0:T(8,128)(2,1)}), bf16[16,24,768]{2,1,0:T(8,128)(2,1)S(1)}, u32[]{:S(2)}, u32[]{:S(2)}) async-start(bf16[16,24,768]{2,1,0:T(8,128)(2,1)} %broadcast_in_dim.16), calls=%async_computation.1 | async-start | bytes 1179648 | tf_op jit(solution)/shard_map/all_to_all | solution.py:332
  42.5 0.0 collective-permute-done.7
  42.5 0.7 fusion.14
  43.2 3.1 %collective-permute-start.15 = (bf16[96,768]{1,0:T(8,128)(2,1)}, bf16[96,768]{1,0:T(8,128)(2,1)S(1)}, u32[]{:S(2)}, u32[]{:S(2)}) collective-permute-start(bf16[96,768]{1,0:T(8,128)(2,1)} %get-tuple-element.12), channel_id=1, source_target_pairs={{0,48},{16,0},{32,16},{48,32},{1,49},{17,1},{33,17},{49,33},{2,50}... | collective-permute-start | bytes 442376 | tf_op jit(solution)/shard_map/ppermute | solution.py:276
  46.4 2.7 %collective-permute-start.9 = (bf16[96,768]{1,0:T(8,128)(2,1)}, bf16[96,768]{1,0:T(8,128)(2,1)S(1)}, u32[]{:S(2)}, u32[]{:S(2)}) collective-permute-start(bf16[96,768]{1,0:T(8,128)(2,1)} %get-tuple-element.19), channel_id=1, source_target_pairs={{0,192},{64,0},{128,64},{192,128},{1,193},{65,1},{129,65},{193,129... | collective-permute-start | bytes 442376 | tf_op jit(solution)/shard_map/ppermute | solution.py:276
  49.1 3.8 %all-to-all-done.1.mine_ref = bf16[16,24,768]{2,1,0:T(8,128)(2,1)S(1)} async-done(((bf16[16,24,768]{2,1,0:T(8,128)(2,1)}), bf16[16,24,768]{2,1,0:T(8,128)(2,1)S(1)}, u32[]{:S(2)}, u32[]{:S(2)}) %all-to-all-start.1) | async-done | bytes 589856 | tf_op jit(solution)/shard_map/all_to_all | solution.py:332
  52.9 0.0 collective-permute-start.6
  52.9 0.6 collective-permute-start.14
  53.5 1.8 %collective-permute-start.16 = (bf16[96,768]{1,0:T(8,128)(2,1)}, bf16[96,768]{1,0:T(8,128)(2,1)S(1)}, u32[]{:S(2)}, u32[]{:S(2)}) collective-permute-start(bf16[96,768]{1,0:T(8,128)(2,1)} %get-tuple-element.12), channel_id=1, source_target_pairs={{0,32},{16,48},{32,0},{48,16},{1,33},{17,49},{33,1},{49,17},{2,34}... | collective-permute-start | bytes 442376 | tf_op jit(solution)/shard_map/ppermute | solution.py:276
  55.3 0.0 collective-permute-done.15
  55.3 0.7 collective-permute-start.8
  56.0 0.0 collective-permute-done.9
  56.0 2.2 %collective-permute-start.10 = (bf16[96,768]{1,0:T(8,128)(2,1)}, bf16[96,768]{1,0:T(8,128)(2,1)}, u32[]{:S(2)}, u32[]{:S(2)}) collective-permute-start(bf16[96,768]{1,0:T(8,128)(2,1)} %get-tuple-element.19), channel_id=1, source_target_pairs={{0,128},{64,192},{128,0},{192,64},{1,129},{65,193},{129,1},{193,65... | collective-permute-start | bytes 442376 | tf_op jit(solution)/shard_map/ppermute | solution.py:276
  58.2 0.7 convolution_bitcast_fusion
  59.6 0.1 reshape.22.strip_ref
  59.7 5.9 %collective-permute-done.8 = bf16[96,768]{1,0:T(8,128)(2,1)S(1)} collective-permute-done((bf16[96,768]{1,0:T(8,128)(2,1)}, bf16[96,768]{1,0:T(8,128)(2,1)S(1)}, u32[]{:S(2)}, u32[]{:S(2)}) %collective-permute-start.8) | collective-permute-done | bytes 147488 | tf_op jit(solution)/shard_map/ppermute | solution.py:276
  65.6 3.8 %collective-permute-start = (bf16[128,768]{1,0:T(8,128)(2,1)S(1)}, bf16[128,768]{1,0:T(8,128)(2,1)S(1)}, u32[]{:S(2)}, u32[]{:S(2)}) collective-permute-start(bf16[128,768]{1,0:T(8,128)(2,1)S(1)} %bitcast.22), channel_id=1, source_target_pairs={{0,1},{1,2},{2,3},{3,0},{4,5},{5,6},{6,7},{7,4},{8,9},{9,10},{10,1... | collective-permute-start | bytes 589832 | tf_op jit(solution)/shard_map/ppermute | solution.py:321
  69.4 0.0 collective-permute-done.10
  69.4 0.3 collective-permute-start.1
  69.7 1.0 pad_maximum_fusion.refs_1_
  70.7 0.0 collective-permute-done.14
  70.7 1.8 %collective-permute-start.11 = (bf16[4,96,768]{2,1,0:T(8,128)(2,1)S(1)}, bf16[4,96,768]{2,1,0:T(8,128)(2,1)S(1)}, u32[]{:S(2)}, u32[]{:S(2)}) collective-permute-start(bf16[4,96,768]{2,1,0:T(8,128)(2,1)S(1)} %pad_maximum_fusion.refs_1_), channel_id=1, source_target_pairs={{0,16},{16,32},{32,48},{48,0},{1,17},{17,33},{33,49},{49,1},{2,18}... | collective-permute-start | bytes 1769480 | tf_op jit(solution)/shard_map/ppermute | solution.py:269
  72.6 0.0 collective-permute-done.16
  72.6 0.1 pad_maximum_fusion.1.refs_5_
  72.7 0.1 collective-permute-start.17
  72.7 1.6 %collective-permute-done.up_ref = bf16[128,768]{1,0:T(8,128)(2,1)S(1)} collective-permute-done((bf16[128,768]{1,0:T(8,128)(2,1)S(1)}, bf16[128,768]{1,0:T(8,128)(2,1)S(1)}, u32[]{:S(2)}, u32[]{:S(2)}) %collective-permute-start) | collective-permute-done | bytes 196640 | tf_op jit(solution)/shard_map/ppermute | solution.py:321
  74.4 4.5 %collective-permute-done.1.down_ref = bf16[128,768]{1,0:T(8,128)(2,1)S(1)} collective-permute-done((bf16[128,768]{1,0:T(8,128)(2,1)S(1)}, bf16[128,768]{1,0:T(8,128)(2,1)S(1)}, u32[]{:S(2)}, u32[]{:S(2)}) %collective-permute-start.1) | collective-permute-done | bytes 196640 | tf_op jit(solution)/shard_map/ppermute | solution.py:322
  78.9 0.0 collective-permute-done.6.other_ref
  78.9 13.2 %attend.1.refs_0_ = bf16[512,768]{1,0:T(8,128)(2,1)S(1)} custom-call(s32[1]{0:T(128)S(6)} %copy.14.shift_ref, bf16[128,768]{1,0:T(8,128)(2,1)S(1)} %collective-permute-done.up_ref, bf16[512,768]{1,0:T(8,128)(2,1)S(1)} %bitcast.19, bf16[128,768]{1,0:T(8,128)(2,1)S(1)} %collective-permute-done.1.down_ref, bf16[16,24,768]{2,1,0:T(8,128)(2,1)S(1)} %all-to-all-done.1.mine_ref, ...), custom_call_target="tpu_custom_call" | custom-call | flops 5435817984 | bytes 10000000 | tf_op jit(solution)/shard_map/attend/pallas_call | solution.py:202
  92.1 0.1 collective-permute-start.20
  92.2 1.8 %collective-permute-start.12 = (bf16[4,96,768]{2,1,0:T(8,128)(2,1)S(1)}, bf16[4,96,768]{2,1,0:T(8,128)(2,1)S(1)}, u32[]{:S(2)}, u32[]{:S(2)}) collective-permute-start(bf16[4,96,768]{2,1,0:T(8,128)(2,1)S(1)} %pad_maximum_fusion.refs_1_), channel_id=1, source_target_pairs={{0,48},{16,0},{32,16},{48,32},{1,49},{17,1},{33,17},{49,33},{2,50}... | collective-permute-start | bytes 1769480 | tf_op jit(solution)/shard_map/ppermute | solution.py:270
  94.0 0.0 collective-permute-start.18
  94.0 0.0 collective-permute-done.11.refs_2_
  94.0 0.9 collective-permute-start.13
  94.9 0.0 collective-permute-done.17.refs_6_
  94.9 1.9 %collective-permute-start.19 = (bf16[4,96,768]{2,1,0:T(8,128)(2,1)S(1)}, bf16[4,96,768]{2,1,0:T(8,128)(2,1)S(1)}, u32[]{:S(2)}, u32[]{:S(2)}) collective-permute-start(bf16[4,96,768]{2,1,0:T(8,128)(2,1)S(1)} %collective-permute-done.17.refs_6_), channel_id=1, source_target_pairs={{0,64},{64,128},{128,192},{192,0},{1,65},{65,129},{129,193},{193,1... | collective-permute-start | bytes 1769480 | tf_op jit(solution)/shard_map/ppermute | solution.py:271
  96.8 11.6 %collective-permute-done.12.refs_3_ = bf16[4,96,768]{2,1,0:T(8,128)(2,1)S(1)} collective-permute-done((bf16[4,96,768]{2,1,0:T(8,128)(2,1)S(1)}, bf16[4,96,768]{2,1,0:T(8,128)(2,1)S(1)}, u32[]{:S(2)}, u32[]{:S(2)}) %collective-permute-start.12) | collective-permute-done | bytes 589856 | tf_op jit(solution)/shard_map/ppermute | solution.py:270
  108.4 1.0 collective-permute-done.18.refs_7_
  109.4 1.2 %collective-permute-done.13.refs_4_ = bf16[4,96,768]{2,1,0:T(8,128)(2,1)S(1)} collective-permute-done((bf16[4,96,768]{2,1,0:T(8,128)(2,1)S(1)}, bf16[4,96,768]{2,1,0:T(8,128)(2,1)S(1)}, u32[]{:S(2)}, u32[]{:S(2)}) %collective-permute-start.13) | collective-permute-done | bytes 589856 | tf_op jit(solution)/shard_map/ppermute | solution.py:271
  110.6 0.6 collective-permute-done.19.refs_8_
  111.1 0.0 collective-permute-done.20.refs_0_
  111.1 2.9 %feed_forward_partner.1 = bf16[512,768]{1,0:T(8,128)(2,1)S(1)} custom-call(bf16[512,768]{1,0:T(8,128)(2,1)S(1)} %collective-permute-done.20.refs_0_, bf16[4,96,768]{2,1,0:T(8,128)(2,1)S(1)} %pad_maximum_fusion.refs_1_, bf16[4,96,768]{2,1,0:T(8,128)(2,1)S(1)} %collective-permute-done.11.refs_2_, bf16[4,96,768]{2,1,0:T(8,128)(2,1)S(1)} %collective-permute-done.12.refs_3_, ...), custom_call_target="tpu_custom_call" | custom-call | flops 2415919104 | bytes 6000000 | tf_op jit(solution)/shard_map/feed_forward_partner/pallas_call | solution.py:250
  114.1 0.1 collective-permute-start.21
  114.2 2.9 %feed_forward_own.1 = f32[512,768]{1,0:T(8,128)S(1)} custom-call(bf16[512,768]{1,0:T(8,128)(2,1)S(1)} %attend.1.refs_0_, bf16[4,96,768]{2,1,0:T(8,128)(2,1)S(1)} %pad_maximum_fusion.refs_1_, bf16[4,96,768]{2,1,0:T(8,128)(2,1)S(1)} %collective-permute-done.11.refs_2_, bf16[4,96,768]{2,1,0:T(8,128)(2,1)S(1)} %collective-permute-done.12.refs_3_, ...), custom_call_target="tpu_custom_call" | custom-call | flops 2415919104 | bytes 6000000 | tf_op jit(solution)/shard_map/feed_forward_own/pallas_call | solution.py:250
  117.1 0.0 collective-permute-done.21
  117.1 1.0 add_convert_fusion
  (14 shorter events, 0.1 us)
Async XLA Ops:
  0.0 58.2 %copy-start = (f32[12,225]{1,0:T(8,128)S(1)}, f32[12,225]{1,0:T(8,128)}, u32[]{:S(2)}) copy-start(f32[12,225]{1,0:T(8,128)} %param.23) | copy-start | bytes 32404
  0.0 0.7 copy-start.2
  6.1 28.8 %copy-start.3 = (bf16[48,768]{1,0:T(8,128)(2,1)S(1)}, bf16[48,768]{1,0:T(8,128)(2,1)}, u32[]{:S(2)}) copy-start(bf16[48,768]{1,0:T(8,128)(2,1)} %param.24) | copy-start | bytes 221188
  6.1 28.8 %copy-start.4 = (bf16[48,768]{1,0:T(8,128)(2,1)S(1)}, bf16[48,768]{1,0:T(8,128)(2,1)}, u32[]{:S(2)}) copy-start(bf16[48,768]{1,0:T(8,128)(2,1)} %param.25) | copy-start | bytes 221188
  6.1 1.8 %collective-permute-start.2 = (bf16[256,768]{1,0:T(8,128)(2,1)S(1)}, bf16[256,768]{1,0:T(8,128)(2,1)S(1)}, u32[]{:S(2)}, u32[]{:S(2)}) collective-permute-start(bf16[256,768]{1,0:T(8,128)(2,1)S(1)} %get-tuple-element.8), channel_id=1, source_target_pairs={{0,4},{4,0},{1,5},{5,1},{2,6},{6,2},{3,7},{7,3},{8,12},{12,8},{9,1... | collective-permute-start | bytes 1179656 | tf_op jit(solution)/shard_map/ppermute | solution.py:263
  8.0 34.4 %copy-start.1 = (bf16[1,16,32,768]{3,2,1,0:T(8,128)(2,1)S(1)}, bf16[1,16,32,768]{3,2,1,0:T(8,128)(2,1)}, u32[]{:S(2)}) copy-start(bf16[1,16,32,768]{3,2,1,0:T(8,128)(2,1)} %param.13) | copy-start | bytes 2359300
  25.2 7.1 %collective-permute-start.3 = (bf16[4,768]{1,0:T(4,128)(2,1)S(1)}, bf16[4,768]{1,0:T(4,128)(2,1)S(1)}, u32[]{:S(2)}, u32[]{:S(2)}) collective-permute-start(bf16[4,768]{1,0:T(4,128)(2,1)S(1)} %get-tuple-element.17), channel_id=1, source_target_pairs={{0,1},{1,2},{2,3},{3,0},{4,5},{5,6},{6,7},{7,4},{8,9},{9,10},{10,1... | collective-permute-start | bytes 18440 | tf_op jit(solution)/shard_map/ppermute | solution.py:327
  28.6 5.2 %collective-permute-start.4 = (bf16[4,768]{1,0:T(4,128)(2,1)S(1)}, bf16[4,768]{1,0:T(4,128)(2,1)S(1)}, u32[]{:S(2)}, u32[]{:S(2)}) collective-permute-start(bf16[4,768]{1,0:T(4,128)(2,1)S(1)} %get-tuple-element.18), channel_id=1, source_target_pairs={{0,3},{1,0},{2,1},{3,2},{4,7},{5,4},{6,5},{7,6},{8,11},{9,8},{10,9... | collective-permute-start | bytes 18440 | tf_op jit(solution)/shard_map/ppermute | solution.py:328
  33.8 4.0 %collective-permute-start.5 = (bf16[24,768]{1,0:T(8,128)(2,1)S(1)}, bf16[24,768]{1,0:T(8,128)(2,1)S(1)}, u32[]{:S(2)}, u32[]{:S(2)}) collective-permute-start(bf16[24,768]{1,0:T(8,128)(2,1)S(1)} %pad_maximum_fusion.5), channel_id=1, source_target_pairs={{0,8},{8,0},{1,9},{9,1},{2,10},{10,2},{3,11},{11,3},{4,12},{12,4},... | collective-permute-start | bytes 110600 | tf_op jit(solution)/shard_map/ppermute | solution.py:263
  34.9 7.6 %collective-permute-start.7 = (bf16[96,768]{1,0:T(8,128)(2,1)S(1)}, bf16[96,768]{1,0:T(8,128)(2,1)S(1)}, u32[]{:S(2)}, u32[]{:S(2)}) collective-permute-start(bf16[96,768]{1,0:T(8,128)(2,1)S(1)} %pad_maximum_fusion.2), channel_id=1, source_target_pairs={{0,8},{8,0},{1,9},{9,1},{2,10},{10,2},{3,11},{11,3},{4,12},{12,4},... | collective-permute-start | bytes 442376 | tf_op jit(solution)/shard_map/ppermute | solution.py:263
  38.7 14.2 %all-to-all-start.1 = ((bf16[16,24,768]{2,1,0:T(8,128)(2,1)}), bf16[16,24,768]{2,1,0:T(8,128)(2,1)S(1)}, u32[]{:S(2)}, u32[]{:S(2)}) async-start(bf16[16,24,768]{2,1,0:T(8,128)(2,1)} %broadcast_in_dim.16), calls=%async_computation.1 | async-start | bytes 1179648 | tf_op jit(solution)/shard_map/all_to_all | solution.py:332
  43.2 12.1 %collective-permute-start.15 = (bf16[96,768]{1,0:T(8,128)(2,1)}, bf16[96,768]{1,0:T(8,128)(2,1)S(1)}, u32[]{:S(2)}, u32[]{:S(2)}) collective-permute-start(bf16[96,768]{1,0:T(8,128)(2,1)} %get-tuple-element.12), channel_id=1, source_target_pairs={{0,48},{16,0},{32,16},{48,32},{1,49},{17,1},{33,17},{49,33},{2,50}... | collective-permute-start | bytes 442376 | tf_op jit(solution)/shard_map/ppermute | solution.py:276
  46.4 9.6 %collective-permute-start.9 = (bf16[96,768]{1,0:T(8,128)(2,1)}, bf16[96,768]{1,0:T(8,128)(2,1)S(1)}, u32[]{:S(2)}, u32[]{:S(2)}) collective-permute-start(bf16[96,768]{1,0:T(8,128)(2,1)} %get-tuple-element.19), channel_id=1, source_target_pairs={{0,192},{64,0},{128,64},{192,128},{1,193},{65,1},{129,65},{193,129... | collective-permute-start | bytes 442376 | tf_op jit(solution)/shard_map/ppermute | solution.py:276
  52.9 26.0 %collective-permute-start.6 = (bf16[16,24,768]{2,1,0:T(8,128)(2,1)S(1)}, bf16[16,24,768]{2,1,0:T(8,128)(2,1)S(1)}, u32[]{:S(2)}, u32[]{:S(2)}) collective-permute-start(bf16[16,24,768]{2,1,0:T(8,128)(2,1)S(1)} %all-to-all-done.1.mine_ref), channel_id=1, source_target_pairs={{0,4},{4,0},{1,5},{5,1},{2,6},{6,2},{3,7},{7,3},{8,12},{12,8},{9,1... | collective-permute-start | bytes 1769480 | tf_op jit(solution)/shard_map/ppermute | solution.py:263
  52.9 17.8 %collective-permute-start.14 = (bf16[96,768]{1,0:T(8,128)(2,1)}, bf16[96,768]{1,0:T(8,128)(2,1)S(1)}, u32[]{:S(2)}, u32[]{:S(2)}) collective-permute-start(bf16[96,768]{1,0:T(8,128)(2,1)} %get-tuple-element.12), channel_id=1, source_target_pairs={{0,16},{16,32},{32,48},{48,0},{1,17},{17,33},{33,49},{49,1},{2,18}... | collective-permute-start | bytes 442376 | tf_op jit(solution)/shard_map/ppermute | solution.py:276
  53.5 19.0 %collective-permute-start.16 = (bf16[96,768]{1,0:T(8,128)(2,1)}, bf16[96,768]{1,0:T(8,128)(2,1)S(1)}, u32[]{:S(2)}, u32[]{:S(2)}) collective-permute-start(bf16[96,768]{1,0:T(8,128)(2,1)} %get-tuple-element.12), channel_id=1, source_target_pairs={{0,32},{16,48},{32,0},{48,16},{1,33},{17,49},{33,1},{49,17},{2,34}... | collective-permute-start | bytes 442376 | tf_op jit(solution)/shard_map/ppermute | solution.py:276
  55.3 10.3 %collective-permute-start.8 = (bf16[96,768]{1,0:T(8,128)(2,1)}, bf16[96,768]{1,0:T(8,128)(2,1)S(1)}, u32[]{:S(2)}, u32[]{:S(2)}) collective-permute-start(bf16[96,768]{1,0:T(8,128)(2,1)} %get-tuple-element.19), channel_id=1, source_target_pairs={{0,64},{64,128},{128,192},{192,0},{1,65},{65,129},{129,193},{193,1... | collective-permute-start | bytes 442376 | tf_op jit(solution)/shard_map/ppermute | solution.py:276
  56.0 13.4 %collective-permute-start.10 = (bf16[96,768]{1,0:T(8,128)(2,1)}, bf16[96,768]{1,0:T(8,128)(2,1)}, u32[]{:S(2)}, u32[]{:S(2)}) collective-permute-start(bf16[96,768]{1,0:T(8,128)(2,1)} %get-tuple-element.19), channel_id=1, source_target_pairs={{0,128},{64,192},{128,0},{192,64},{1,129},{65,193},{129,1},{193,65... | collective-permute-start | bytes 442376 | tf_op jit(solution)/shard_map/ppermute | solution.py:276
  65.6 8.8 %collective-permute-start = (bf16[128,768]{1,0:T(8,128)(2,1)S(1)}, bf16[128,768]{1,0:T(8,128)(2,1)S(1)}, u32[]{:S(2)}, u32[]{:S(2)}) collective-permute-start(bf16[128,768]{1,0:T(8,128)(2,1)S(1)} %bitcast.22), channel_id=1, source_target_pairs={{0,1},{1,2},{2,3},{3,0},{4,5},{5,6},{6,7},{7,4},{8,9},{9,10},{10,1... | collective-permute-start | bytes 589832 | tf_op jit(solution)/shard_map/ppermute | solution.py:321
  69.4 9.4 %collective-permute-start.1 = (bf16[128,768]{1,0:T(8,128)(2,1)S(1)}, bf16[128,768]{1,0:T(8,128)(2,1)S(1)}, u32[]{:S(2)}, u32[]{:S(2)}) collective-permute-start(bf16[128,768]{1,0:T(8,128)(2,1)S(1)} %bitcast.21), channel_id=1, source_target_pairs={{0,3},{1,0},{2,1},{3,2},{4,7},{5,4},{6,5},{7,6},{8,11},{9,8},{10,9... | collective-permute-start | bytes 589832 | tf_op jit(solution)/shard_map/ppermute | solution.py:322
  70.7 23.3 %collective-permute-start.11 = (bf16[4,96,768]{2,1,0:T(8,128)(2,1)S(1)}, bf16[4,96,768]{2,1,0:T(8,128)(2,1)S(1)}, u32[]{:S(2)}, u32[]{:S(2)}) collective-permute-start(bf16[4,96,768]{2,1,0:T(8,128)(2,1)S(1)} %pad_maximum_fusion.refs_1_), channel_id=1, source_target_pairs={{0,16},{16,32},{32,48},{48,0},{1,17},{17,33},{33,49},{49,1},{2,18}... | collective-permute-start | bytes 1769480 | tf_op jit(solution)/shard_map/ppermute | solution.py:269
  72.7 22.2 %collective-permute-start.17 = (bf16[4,96,768]{2,1,0:T(8,128)(2,1)S(1)}, bf16[4,96,768]{2,1,0:T(8,128)(2,1)S(1)}, u32[]{:S(2)}, u32[]{:S(2)}) collective-permute-start(bf16[4,96,768]{2,1,0:T(8,128)(2,1)S(1)} %pad_maximum_fusion.1.refs_5_), channel_id=1, source_target_pairs={{0,64},{64,128},{128,192},{192,0},{1,65},{65,129},{129,193},{193,1... | collective-permute-start | bytes 1769480 | tf_op jit(solution)/shard_map/ppermute | solution.py:269
  92.1 19.0 %collective-permute-start.20 = (bf16[512,768]{1,0:T(8,128)(2,1)S(1)}, bf16[512,768]{1,0:T(8,128)(2,1)S(1)}, u32[]{:S(2)}, u32[]{:S(2)}) collective-permute-start(bf16[512,768]{1,0:T(8,128)(2,1)S(1)} %attend.1.refs_0_), channel_id=1, source_target_pairs={{0,4},{4,0},{1,5},{5,1},{2,6},{6,2},{3,7},{7,3},{8,12},{12,8},{9,1... | collective-permute-start | bytes 2359304 | tf_op jit(solution)/shard_map/ppermute | solution.py:263
  92.2 16.2 %collective-permute-start.12 = (bf16[4,96,768]{2,1,0:T(8,128)(2,1)S(1)}, bf16[4,96,768]{2,1,0:T(8,128)(2,1)S(1)}, u32[]{:S(2)}, u32[]{:S(2)}) collective-permute-start(bf16[4,96,768]{2,1,0:T(8,128)(2,1)S(1)} %pad_maximum_fusion.refs_1_), channel_id=1, source_target_pairs={{0,48},{16,0},{32,16},{48,32},{1,49},{17,1},{33,17},{49,33},{2,50}... | collective-permute-start | bytes 1769480 | tf_op jit(solution)/shard_map/ppermute | solution.py:270
  94.0 15.4 %collective-permute-start.18 = (bf16[4,96,768]{2,1,0:T(8,128)(2,1)S(1)}, bf16[4,96,768]{2,1,0:T(8,128)(2,1)S(1)}, u32[]{:S(2)}, u32[]{:S(2)}) collective-permute-start(bf16[4,96,768]{2,1,0:T(8,128)(2,1)S(1)} %pad_maximum_fusion.1.refs_5_), channel_id=1, source_target_pairs={{0,192},{64,0},{128,64},{192,128},{1,193},{65,1},{129,65},{193,129... | collective-permute-start | bytes 1769480 | tf_op jit(solution)/shard_map/ppermute | solution.py:270
  94.0 16.6 %collective-permute-start.13 = (bf16[4,96,768]{2,1,0:T(8,128)(2,1)S(1)}, bf16[4,96,768]{2,1,0:T(8,128)(2,1)S(1)}, u32[]{:S(2)}, u32[]{:S(2)}) collective-permute-start(bf16[4,96,768]{2,1,0:T(8,128)(2,1)S(1)} %collective-permute-done.11.refs_2_), channel_id=1, source_target_pairs={{0,16},{16,32},{32,48},{48,0},{1,17},{17,33},{33,49},{49,1},{2,18}... | collective-permute-start | bytes 1769480 | tf_op jit(solution)/shard_map/ppermute | solution.py:271
  94.9 16.3 %collective-permute-start.19 = (bf16[4,96,768]{2,1,0:T(8,128)(2,1)S(1)}, bf16[4,96,768]{2,1,0:T(8,128)(2,1)S(1)}, u32[]{:S(2)}, u32[]{:S(2)}) collective-permute-start(bf16[4,96,768]{2,1,0:T(8,128)(2,1)S(1)} %collective-permute-done.17.refs_6_), channel_id=1, source_target_pairs={{0,64},{64,128},{128,192},{192,0},{1,65},{65,129},{129,193},{193,1... | collective-permute-start | bytes 1769480 | tf_op jit(solution)/shard_map/ppermute | solution.py:271
  114.1 3.0 %collective-permute-start.21 = (bf16[512,768]{1,0:T(8,128)(2,1)S(1)}, bf16[512,768]{1,0:T(8,128)(2,1)S(1)}, u32[]{:S(2)}, u32[]{:S(2)}) collective-permute-start(bf16[512,768]{1,0:T(8,128)(2,1)S(1)} %feed_forward_partner.1), channel_id=1, source_target_pairs={{0,4},{4,0},{1,5},{5,1},{2,6},{6,2},{3,7},{7,3},{8,12},{12,8},{9,1... | collective-permute-start | bytes 2359304 | tf_op jit(solution)/shard_map/ppermute | solution.py:263

commit v2 on v1

--- a/solution.py
+++ b/solution.py
@@ -14,6 +14,7 @@
 ROWS = 16
 COLS = 32
 NLAT = 64
+EDGE = WIN // 2 * COLS
 GROUPS = 3
 MEMBER = ("mx", "my", "mz", "core")
 PLANE = ("mx", "my")
@@ -60,7 +61,7 @@
     return row, col
 
 
-def encode_kernel(chosen, frame_hbm, in_hbm, out_hbm, joint_hbm, keep_ref, send_ref, frame, w_in, w_out, w_slot, sems):
+def encode_kernel(chosen, frame_hbm, in_hbm, out_hbm, joint_hbm, noisy_hbm, keep_ref, send_ref, head_ref, tail_ref, frame, w_in, w_out, w_slot, sems):
     own_core = axis_index("core")
     member = axis_index(MEMBER)
     is_second = member == chosen[1]
@@ -71,6 +72,8 @@
         pltpu.make_async_copy(in_hbm, w_in, sems.at[1]),
         pltpu.make_async_copy(out_hbm, w_out, sems.at[2]),
         pltpu.make_async_copy(joint_hbm.at[pl.ds(pl.multiple_of(slot * D, D), D), :], w_slot, sems.at[3]),
+        pltpu.make_async_copy(noisy_hbm.at[pl.ds(0, EDGE), :], head_ref, sems.at[4]),
+        pltpu.make_async_copy(noisy_hbm.at[pl.ds(ROWS * COLS - EDGE, EDGE), :], tail_ref, sems.at[5]),
     ]
     for c in copies:
         c.start()
@@ -91,27 +94,30 @@
     term = jnp.where(is_source, term, 0.0).astype(BF16)
     keep_ref[...] = term[:half]
     send_ref[...] = term[half:]
-
-
-def encode(chosen, frame, w_in, w_out, joint):
+    copies[4].wait()
+    copies[5].wait()
+
+
+def encode(chosen, frame, w_in, w_out, joint, noisy):
     tokens = ROWS * COLS
     any_spec = pl.BlockSpec(memory_space=pltpu.HBM)
     out = jax.ShapeDtypeStruct((tokens // 2, D), BF16)
+    rim = jax.ShapeDtypeStruct((EDGE, D), BF16)
     return pl.pallas_call(
         encode_kernel,
         name="encode",
-        in_specs=[pl.BlockSpec(memory_space=pltpu.SMEM)] + [any_spec] * 4,
-        out_shape=(out, out),
+        in_specs=[pl.BlockSpec(memory_space=pltpu.SMEM)] + [any_spec] * 5,
+        out_shape=(out, out, rim, rim),
         scratch_shapes=[
             pltpu.VMEM((tokens, D), BF16),
             pltpu.VMEM((D, D), BF16),
             pltpu.VMEM((D, D), BF16),
             pltpu.VMEM((D, D), BF16),
-            pltpu.SemaphoreType.DMA((4,)),
+            pltpu.SemaphoreType.DMA((6,)),
         ],
         compiler_params=pltpu.CompilerParams(vmem_limit_bytes=24 << 20),
         cost_estimate=pl.CostEstimate(flops=2 * tokens * D * (3 * D + tokens), bytes_accessed=6_000_000, transcendentals=tokens * D),
-    )(chosen, *map(in_hbm, (frame, w_in, w_out, joint)))
+    )(chosen, *map(in_hbm, (frame, w_in, w_out, joint, noisy)))
 
 
 def attend_kernel(shift_ref, up_ref, own_ref, down_ref, mine_ref, other_ref, strip_ref, w0_hbm, wq_hbm, wkv_hbm, wo_hbm, out_ref, bias_ref, stream_ref, normed_ref, qkv_ref, mixed_ref, w0, wqkv, wo, sems):
@@ -135,8 +141,7 @@
     row, col = window_place(256, shift)
     half = COLS // 2
     place = (col % half) * WIN + row
-    from_mine = one_hot(jnp.where(col // half == core, place, -1), 128)
-    from_other = one_hot(jnp.where(col // half == core, -1, place), 128)
+    placing = one_hot(jnp.where(col // half == core, place, place + 128), 256)
     order = one_hot(row * COLS + col, 256)
     tokens = ((up_ref[...], own_ref[:128, :]), (own_ref[128:384, :],), (own_ref[384:, :], down_ref[...]))
     for g in range(GROUPS):
@@ -145,16 +150,17 @@
     copies[0].wait()
     noisy = dot(mixed_ref[...], w0[...])
     for g in range(GROUPS):
-        mine = mine_ref[:, g * WIN : (g + 1) * WIN, :].astype(F32).reshape(128, D).astype(BF16)
-        other = other_ref[:, g * WIN : (g + 1) * WIN, :].astype(F32).reshape(128, D).astype(BF16)
-        stream = (noisy[g * 256 : (g + 1) * 256] + (dot(from_mine, mine) + dot(from_other, other))).astype(BF16)
+        both = [half_ref[:, g * WIN : (g + 1) * WIN, :].astype(F32).reshape(128, D) for half_ref in (mine_ref, other_ref)]
+        condition = jnp.concatenate(both, axis=0).astype(BF16)
+        stream = (noisy[g * 256 : (g + 1) * 256] + dot(placing, condition)).astype(BF16)
         stream_ref[g * 256 : (g + 1) * 256, :] = stream
         normed_ref[g * 256 : (g + 1) * 256, :] = normalised(stream.astype(F32))
     copies[1].wait()
     copies[2].wait()
     for n in range(3):
         cols = slice(n * D, (n + 1) * D)
-        qkv_ref[:, cols] = dot(normed_ref[...], wqkv[:, cols]).astype(BF16)
+        made = dot(normed_ref[...], wqkv[:, cols])
+        qkv_ref[:, cols] = (made * HD ** (-0.5) if n == 0 else made).astype(BF16)
     low = lax.broadcasted_iota(jnp.int32, (64, 128), 1) < HD
     key_row = lax.broadcasted_iota(jnp.int32, (64, 128), 0)
 
@@ -172,7 +178,7 @@
             zero = jnp.zeros_like(q)
             both = jnp.concatenate([jnp.where(low, q, zero), jnp.where(low, zero, q)], axis=0)
             scores.append(dot_nt(k, both))
-        scores = [jnp.where(seen, s * HD ** (-0.5) + bias_ref[p], -1e30) for p, s in enumerate(scores)]
+        scores = [jnp.where(seen, s + bias_ref[p], -1e30) for p, s in enumerate(scores)]
         tops = [jnp.max(s, axis=0, keepdims=True) for s in scores]
         weights = [jnp.exp(s - m) for s, m in zip(scores, tops)]
         sums = [1.0 / jnp.sum(e, axis=0, keepdims=True) for e in weights]
@@ -271,18 +277,35 @@
     return [mine, behind, ahead, lax.ppermute(behind, axis, on)]
 
 
-def row_from_all(mine, axis):
-    moves = (1, -1, 2)
-    got = [lax.ppermute(mine, axis, [(i, (i + by) % 4) for i in range(4)]) for by in moves]
-    return jnp.stack([mine, *got], axis=0)
-
-
-def gathered_weights(expand, reduce):
+PAIRS = {"a": [(0, 1), (1, 0), (2, 3), (3, 2)], "b": [(1, 2), (2, 1), (3, 0), (0, 3)]}
+
+
+def held_back(x, after):
+    first = lax.slice(after, (0,) * after.ndim, (1,) * after.ndim).reshape((1,) * x.ndim)
+    return jnp.where(first < jnp.inf, x, jnp.zeros_like(x))
+
+
+def row_start(mine, axis):
+    return mine, lax.ppermute(mine, axis, PAIRS["a"])
+
+
+def row_rest(mine, first, after, axis):
+    pair = jnp.stack([mine, held_back(first, after)], axis=0)
+    return mine, first, lax.ppermute(pair, axis, PAIRS["b"])
+
+
+def row_sorted(mine, first, second, after, axis):
+    even = lax.axis_index(axis) % 2 == 0
+    second = held_back(second, after)
+    behind = jnp.where(even, second[0], first)
+    return jnp.stack([mine, behind, jnp.where(even, first, second[0]), second[1]], axis=0)
+
+
+def weights_start(expand, reduce):
     n = expand.shape[0]
     across = swap(jnp.concatenate([expand, reduce], axis=0), "mz")
-    ups = row_from_all(jnp.concatenate([expand, across[:n]], axis=0), "mx")
-    downs = row_from_all(jnp.concatenate([reduce, across[n:]], axis=0), "my")
-    return ring_from_all(ups, "my"), ring_from_all(downs, "mx")
+    ups = row_start(jnp.concatenate([expand, across[:n]], axis=0), "mx")
+    return ups, row_start(jnp.concatenate([reduce, across[n:]], axis=0), "my")
 
 
 def strip_choice():
@@ -314,18 +337,24 @@
     noisy = noisy_latents.reshape(tokens, D)
     to_next = [(i, (i + 1) % bands) for i in range(bands)]
     to_last = [(i, (i - 1) % bands) for i in range(bands)]
-    edge = margin * COLS
-
-    keep, send = encode(encoder_members, frames.reshape(tokens, D), encoder_in, encoder_out, joint_weight)
-    ups, downs = gathered_weights(expand_weight, reduce_weight)
-    noisy_up = lax.ppermute(noisy[tokens - edge :], "lat", to_next)
-    noisy_down = lax.ppermute(noisy[:edge], "lat", to_last)
-
-    mine = (keep + swap(send, "core")).reshape(COLS // 2, ROWS, D)
+
+    keep, send, head, tail = encode(
+        encoder_members, frames.reshape(tokens, D), encoder_in, encoder_out, joint_weight, noisy
+    )
+    ups, downs = weights_start(expand_weight, reduce_weight)
+    noisy_up = lax.ppermute(tail, "lat", to_next)
+    noisy_down = lax.ppermute(head, "lat", to_last)
+
+    handed = swap(send, "core")
+    mine = (keep + handed).reshape(COLS // 2, ROWS, D)
     spread = lax.all_to_all(mine, PLANE, 0, 0, tiled=True)
+    ups = row_rest(*ups, handed, "mx")
+    downs = row_rest(*downs, handed, "my")
     part = jnp.sum(spread.astype(F32), axis=0).astype(BF16)
     above = lax.ppermute(part[ROWS - margin :], "lat", to_next)
     below = lax.ppermute(part[:margin], "lat", to_last)
+    ups = ring_from_all(row_sorted(*ups, above, "mx"), "my")
+    downs = ring_from_all(row_sorted(*downs, above, "my"), "mx")
     part = jnp.concatenate([above, part, below], axis=0)
     part = part + swap(part, "mz")
     wide = jnp.broadcast_to(part[None], (COLS // 2, *part.shape))

time: 119 us -> 107 us (0.90)
  the two profiles are of different devices: /device:TPU:32 before, /device:TPU:65 now
where the time goes in v2:
time: 107 us
  starting transfers between devices  41.7 us (39%)
  waiting for transfers between devices  32.1 us (30%)
  Pallas kernels  24.3 us (23%)
  other arithmetic  3.35 us (3%)
  local copies, waits for them, and re-layouts  2.66 us (2%)
  between operations  2.1 us (2%)
    pallas_call x1, Pallas kernels, attend(): pl.pallas_call(attend_kernel, name='attend', in_specs=[pl.BlockSpec(memor...  13 us
    ppermute x6, starting transfers between devices, swap(): return lax.ppermute(x, axis, [(0, 1), (1, 0)])  12.4 us
    ppermute x2, waiting for transfers between devices, ring_from_all(): ahead = lax.ppermute(mine, axis, back)  12 us
    all_to_all x1, waiting for transfers between devices, body(): mine = lax.all_to_all(wide, PLANE, 0, 0, tiled=True)  7.58 us
    all_to_all x1, starting transfers between devices, body(): spread = lax.all_to_all(mine, PLANE, 0, 0, tiled=True)  6.46 us
    pallas_call x2, Pallas kernels, feed_forward(): pl.pallas_call(lambda *refs: forward_kernel(keep, *refs), name='feed_forw...  5.82 us
    pallas_call x1, Pallas kernels, encode(): pl.pallas_call(encode_kernel, name='encode', in_specs=[pl.BlockSpec(memor...  5.44 us
    ppermute x2, starting transfers between devices, ring_from_all(): ahead = lax.ppermute(mine, axis, back)  4.37 us
  transfers between devices with their start and end apart: 22, of which 10 were waited for; matrix products, arithmetic and copies ran while one was open for 4% of the time, Pallas kernels for 20%

profile of v2, /device:TPU:65, one launch (start us, length us, event | category | flops | bytes accessed | tf_op | source)
XLA Modules:
  0.0 106.9 jit_solution(10934702514823339252)
XLA Ops:
  0.0 0.0 copy-start
  0.0 0.9 pad_maximum_fusion.4
  0.9 1.7 %collective-permute-start.7 = (bf16[96,768]{1,0:T(8,128)(2,1)S(1)}, bf16[96,768]{1,0:T(8,128)(2,1)S(1)}, u32[]{:S(2)}, u32[]{:S(2)}) collective-permute-start(bf16[96,768]{1,0:T(8,128)(2,1)S(1)} %pad_maximum_fusion.4), channel_id=1, source_target_pairs={{0,8},{8,0},{1,9},{9,1},{2,10},{10,2},{3,11},{11,3},{4,12},{12,4},... | collective-permute-start | bytes 442376 | tf_op jit(solution)/shard_map/ppermute | solution.py:269
  2.7 0.7 copy-done.2
  3.3 5.4 %encode.1 = (bf16[256,768]{1,0:T(8,128)(2,1)S(1)}, bf16[256,768]{1,0:T(8,128)(2,1)S(1)}, bf16[128,768]{1,0:T(8,128)(2,1)S(1)}, bf16[128,768]{1,0:T(8,128)(2,1)S(1)}) custom-call(s32[2]{0:T(128)S(1)} %copy-done.2, bf16[512,768]{1,0:T(8,128)(2,1)} %bitcast.39, bf16[768,768]{1,0:T(8,128)(2,1)} %in_hbm.1, bf16[768,768]{1,0:T(8,128)(2,1)} %out_hbm.1, ...), custom_call_target="tpu_custom_call" | custom-call | flops 2214592512 | bytes 6000000 | tf_op jit(solution)/shard_map/encode/pallas_call | solution.py:106
  8.8 1.0 collective-permute-start.2
  9.8 3.3 %collective-permute-start = (bf16[128,768]{1,0:T(8,128)(2,1)S(1)}, bf16[128,768]{1,0:T(8,128)(2,1)S(1)}, u32[]{:S(2)}, u32[]{:S(2)}) collective-permute-start(bf16[128,768]{1,0:T(8,128)(2,1)S(1)} %get-tuple-element.9), channel_id=1, source_target_pairs={{0,1},{1,2},{2,3},{3,0},{4,5},{5,6},{6,7},{7,4},{8,9},{9,10},{10,1... | collective-permute-start | bytes 589832 | tf_op jit(solution)/shard_map/ppermute | solution.py:345
  13.1 0.0 collective-permute-start.1
  13.1 0.0 collective-permute-done.7
  13.2 0.0 copy-done.3
  13.2 1.4 %collective-permute-start.13 = (bf16[96,768]{1,0:T(8,128)(2,1)S(1)}, bf16[96,768]{1,0:T(8,128)(2,1)S(1)}, u32[]{:S(2)}, u32[]{:S(2)}) collective-permute-start(bf16[96,768]{1,0:T(8,128)(2,1)S(1)} %get-tuple-element.18), channel_id=1, source_target_pairs={{0,16},{16,0},{32,48},{48,32},{1,17},{17,1},{33,49},{49,33},{2,18}... | collective-permute-start | bytes 442376 | tf_op jit(solution)/shard_map/ppermute | solution.py:289
  14.6 0.0 collective-permute-done.2
  14.6 0.8 add.35
  15.5 6.5 %all-to-all-start = ((bf16[16,16,768]{2,1,0:T(8,128)(2,1)}), bf16[16,16,768]{2,1,0:T(8,128)(2,1)S(1)}, u32[]{:S(2)}, u32[]{:S(2)}) async-start(bf16[16,16,768]{2,1,0:T(8,128)(2,1)} %bitcast.2), calls=%async_computation | async-start | bytes 786432 | tf_op jit(solution)/shard_map/all_to_all | solution.py:350
  22.0 1.4 %collective-permute-start.8 = (bf16[96,768]{1,0:T(8,128)(2,1)S(1)}, bf16[96,768]{1,0:T(8,128)(2,1)S(1)}, u32[]{:S(2)}, u32[]{:S(2)}) collective-permute-start(bf16[96,768]{1,0:T(8,128)(2,1)S(1)} %get-tuple-element.25), channel_id=1, source_target_pairs={{0,64},{64,0},{128,192},{192,128},{1,65},{65,1},{129,193},{193,129... | collective-permute-start | bytes 442376 | tf_op jit(solution)/shard_map/ppermute | solution.py:289
  23.4 0.5 slice.48
  24.5 0.0 collective-permute-done.13
  24.6 2.5 %collective-permute-start.14 = (bf16[2,96,768]{2,1,0:T(8,128)(2,1)S(1)}, bf16[2,96,768]{2,1,0:T(8,128)(2,1)S(1)}, u32[]{:S(2)}, u32[]{:S(2)}) collective-permute-start(bf16[2,96,768]{2,1,0:T(8,128)(2,1)S(1)} %pad_maximum_fusion.3), channel_id=1, source_target_pairs={{16,32},{32,16},{48,0},{0,48},{17,33},{33,17},{49,1},{1,49},{18,34... | collective-permute-start | bytes 884744 | tf_op jit(solution)/shard_map/ppermute | solution.py:294
  27.0 3.1 %all-to-all-done = bf16[16,16,768]{2,1,0:T(8,128)(2,1)S(1)} async-done(((bf16[16,16,768]{2,1,0:T(8,128)(2,1)}), bf16[16,16,768]{2,1,0:T(8,128)(2,1)S(1)}, u32[]{:S(2)}, u32[]{:S(2)}) %all-to-all-start) | async-done | bytes 393248 | tf_op jit(solution)/shard_map/all_to_all | solution.py:350
  30.2 0.1 reduce_sum.12
  30.3 3.4 %collective-permute-start.3 = (bf16[4,768]{1,0:T(4,128)(2,1)S(1)}, bf16[4,768]{1,0:T(4,128)(2,1)S(1)}, u32[]{:S(2)}, u32[]{:S(2)}) collective-permute-start(bf16[4,768]{1,0:T(4,128)(2,1)S(1)} %get-tuple-element.23), channel_id=1, source_target_pairs={{0,1},{1,2},{2,3},{3,0},{4,5},{5,6},{6,7},{7,4},{8,9},{9,10},{10,1... | collective-permute-start | bytes 18440 | tf_op jit(solution)/shard_map/ppermute | solution.py:354
  33.7 0.0 collective-permute-done.8
  33.7 0.0 collective-permute-start.4
  33.7 0.7 collective-permute-done.3
  34.4 3.8 %collective-permute-done.4 = bf16[4,768]{1,0:T(4,128)(2,1)S(1)} collective-permute-done((bf16[4,768]{1,0:T(4,128)(2,1)S(1)}, bf16[4,768]{1,0:T(4,128)(2,1)S(1)}, u32[]{:S(2)}, u32[]{:S(2)}) %collective-permute-start.4) | collective-permute-done | bytes 6176 | tf_op jit(solution)/shard_map/ppermute | solution.py:355
  38.3 0.8 collective-permute-start.5
  39.1 1.6 %collective-permute-start.9 = (bf16[2,96,768]{2,1,0:T(8,128)(2,1)S(1)}, bf16[2,96,768]{2,1,0:T(8,128)(2,1)S(1)}, u32[]{:S(2)}, u32[]{:S(2)}) collective-permute-start(bf16[2,96,768]{2,1,0:T(8,128)(2,1)S(1)} %pad_maximum_fusion.2), channel_id=1, source_target_pairs={{64,128},{128,64},{192,0},{0,192},{65,129},{129,65},{193,1},{1,193... | collective-permute-start | bytes 884744 | tf_op jit(solution)/shard_map/ppermute | solution.py:294
  40.8 0.4 collective-permute-done.5
  41.2 0.9 broadcast_in_dim.42
  42.1 4.1 %all-to-all-start.1 = ((bf16[16,24,768]{2,1,0:T(8,128)(2,1)}), bf16[16,24,768]{2,1,0:T(8,128)(2,1)S(1)}, u32[]{:S(2)}, u32[]{:S(2)}) async-start(bf16[16,24,768]{2,1,0:T(8,128)(2,1)} %broadcast_in_dim.42), calls=%async_computation.1 | async-start | bytes 1179648 | tf_op jit(solution)/shard_map/all_to_all | solution.py:361
  46.2 0.7 convolution_bitcast_fusion
  47.6 0.1 reshape.25.strip_ref
  47.6 0.5 slice.47
  48.7 0.0 collective-permute-done.14
  48.8 0.0 collective-permute-done.9
  48.8 7.6 %all-to-all-done.1.mine_ref = bf16[16,24,768]{2,1,0:T(8,128)(2,1)S(1)} async-done(((bf16[16,24,768]{2,1,0:T(8,128)(2,1)}), bf16[16,24,768]{2,1,0:T(8,128)(2,1)S(1)}, u32[]{:S(2)}, u32[]{:S(2)}) %all-to-all-start.1) | async-done | bytes 589856 | tf_op jit(solution)/shard_map/all_to_all | solution.py:361
  56.4 6.8 %collective-permute-start.6 = (bf16[16,24,768]{2,1,0:T(8,128)(2,1)S(1)}, bf16[16,24,768]{2,1,0:T(8,128)(2,1)S(1)}, u32[]{:S(2)}, u32[]{:S(2)}) collective-permute-start(bf16[16,24,768]{2,1,0:T(8,128)(2,1)S(1)} %all-to-all-done.1.mine_ref), channel_id=1, source_target_pairs={{0,4},{4,0},{1,5},{5,1},{2,6},{6,2},{3,7},{7,3},{8,12},{12,8},{9,1... | collective-permute-start | bytes 1769480 | tf_op jit(solution)/shard_map/ppermute | solution.py:269
  63.2 0.0 copy-start.1
  63.2 0.1 pad_maximum_fusion.refs_1_
  63.3 0.4 collective-permute-start.10
  63.7 0.1 pad_maximum_fusion.1.refs_5_
  63.8 0.1 collective-permute-start.15
  63.9 0.0 collective-permute-done.up_ref
  63.9 0.0 collective-permute-done.1.down_ref
  63.9 0.9 collective-permute-done.6.other_ref
  64.8 0.0 copy-done.1
  64.8 13.0 %attend.1.refs_0_ = bf16[512,768]{1,0:T(8,128)(2,1)S(1)} custom-call(s32[1]{0:T(128)S(6)} %copy.14.shift_ref, bf16[128,768]{1,0:T(8,128)(2,1)S(1)} %collective-permute-done.up_ref, bf16[512,768]{1,0:T(8,128)(2,1)S(1)} %bitcast.38, bf16[128,768]{1,0:T(8,128)(2,1)S(1)} %collective-permute-done.1.down_ref, bf16[16,24,768]{2,1,0:T(8,128)(2,1)S(1)} %all-to-all-done.1.mine_ref, ...), custom_call_target="tpu_custom_call" | custom-call | flops 5435817984 | bytes 10000000 | tf_op jit(solution)/shard_map/attend/pallas_call | solution.py:208
  77.8 0.5 collective-permute-start.18
  78.3 1.4 %collective-permute-start.11 = (bf16[4,96,768]{2,1,0:T(8,128)(2,1)S(1)}, bf16[4,96,768]{2,1,0:T(8,128)(2,1)S(1)}, u32[]{:S(2)}, u32[]{:S(2)}) collective-permute-start(bf16[4,96,768]{2,1,0:T(8,128)(2,1)S(1)} %pad_maximum_fusion.refs_1_), channel_id=1, source_target_pairs={{0,48},{16,0},{32,16},{48,32},{1,49},{17,1},{33,17},{49,33},{2,50}... | collective-permute-start | bytes 1769480 | tf_op jit(solution)/shard_map/ppermute | solution.py:276
  79.7 2.9 %collective-permute-start.16 = (bf16[4,96,768]{2,1,0:T(8,128)(2,1)S(1)}, bf16[4,96,768]{2,1,0:T(8,128)(2,1)S(1)}, u32[]{:S(2)}, u32[]{:S(2)}) collective-permute-start(bf16[4,96,768]{2,1,0:T(8,128)(2,1)S(1)} %pad_maximum_fusion.1.refs_5_), channel_id=1, source_target_pairs={{0,192},{64,0},{128,64},{192,128},{1,193},{65,1},{129,65},{193,129... | collective-permute-start | bytes 1769480 | tf_op jit(solution)/shard_map/ppermute | solution.py:276
  82.6 0.0 collective-permute-done.10.refs_2_
  82.6 0.0 collective-permute-start.12
  82.6 0.0 collective-permute-done.15.refs_6_
  82.6 0.3 collective-permute-start.17
  82.9 10.1 %collective-permute-done.11.refs_3_ = bf16[4,96,768]{2,1,0:T(8,128)(2,1)S(1)} collective-permute-done((bf16[4,96,768]{2,1,0:T(8,128)(2,1)S(1)}, bf16[4,96,768]{2,1,0:T(8,128)(2,1)S(1)}, u32[]{:S(2)}, u32[]{:S(2)}) %collective-permute-start.11) | collective-permute-done | bytes 589856 | tf_op jit(solution)/shard_map/ppermute | solution.py:276
  93.0 1.9 %collective-permute-done.16.refs_7_ = bf16[4,96,768]{2,1,0:T(8,128)(2,1)S(1)} collective-permute-done((bf16[4,96,768]{2,1,0:T(8,128)(2,1)S(1)}, bf16[4,96,768]{2,1,0:T(8,128)(2,1)S(1)}, u32[]{:S(2)}, u32[]{:S(2)}) %collective-permute-start.16) | collective-permute-done | bytes 589856 | tf_op jit(solution)/shard_map/ppermute | solution.py:276
  94.9 3.1 %collective-permute-done.12.refs_4_ = bf16[4,96,768]{2,1,0:T(8,128)(2,1)S(1)} collective-permute-done((bf16[4,96,768]{2,1,0:T(8,128)(2,1)S(1)}, bf16[4,96,768]{2,1,0:T(8,128)(2,1)S(1)}, u32[]{:S(2)}, u32[]{:S(2)}) %collective-permute-start.12) | collective-permute-done | bytes 589856 | tf_op jit(solution)/shard_map/ppermute | solution.py:277
  98.1 0.3 collective-permute-done.17.refs_8_
  98.4 0.0 collective-permute-done.18.refs_0_
  98.4 2.9 %feed_forward_partner.1 = bf16[512,768]{1,0:T(8,128)(2,1)S(1)} custom-call(bf16[512,768]{1,0:T(8,128)(2,1)S(1)} %collective-permute-done.18.refs_0_, bf16[4,96,768]{2,1,0:T(8,128)(2,1)S(1)} %pad_maximum_fusion.refs_1_, bf16[4,96,768]{2,1,0:T(8,128)(2,1)S(1)} %collective-permute-done.10.refs_2_, bf16[4,96,768]{2,1,0:T(8,128)(2,1)S(1)} %collective-permute-done.11.refs_3_, ...), custom_call_target="tpu_custom_call" | custom-call | flops 2415919104 | bytes 6000000 | tf_op jit(solution)/shard_map/feed_forward_partner/pallas_call | solution.py:256
  101.3 1.6 %collective-permute-start.19 = (bf16[512,768]{1,0:T(8,128)(2,1)S(1)}, bf16[512,768]{1,0:T(8,128)(2,1)S(1)}, u32[]{:S(2)}, u32[]{:S(2)}) collective-permute-start(bf16[512,768]{1,0:T(8,128)(2,1)S(1)} %feed_forward_partner.1), channel_id=1, source_target_pairs={{0,4},{4,0},{1,5},{5,1},{2,6},{6,2},{3,7},{7,3},{8,12},{12,8},{9,1... | collective-permute-start | bytes 2359304 | tf_op jit(solution)/shard_map/ppermute | solution.py:269
  102.9 2.9 %feed_forward_own.1 = f32[512,768]{1,0:T(8,128)S(1)} custom-call(bf16[512,768]{1,0:T(8,128)(2,1)S(1)} %attend.1.refs_0_, bf16[4,96,768]{2,1,0:T(8,128)(2,1)S(1)} %pad_maximum_fusion.refs_1_, bf16[4,96,768]{2,1,0:T(8,128)(2,1)S(1)} %collective-permute-done.10.refs_2_, bf16[4,96,768]{2,1,0:T(8,128)(2,1)S(1)} %collective-permute-done.11.refs_3_, ...), custom_call_target="tpu_custom_call" | custom-call | flops 2415919104 | bytes 6000000 | tf_op jit(solution)/shard_map/feed_forward_own/pallas_call | solution.py:256
  105.8 0.0 collective-permute-done.19
  105.8 1.0 add_convert_fusion
  (22 shorter events, 0.4 us)
Async XLA Ops:
  0.0 46.2 %copy-start = (f32[12,225]{1,0:T(8,128)S(1)}, f32[12,225]{1,0:T(8,128)}, u32[]{:S(2)}) copy-start(f32[12,225]{1,0:T(8,128)} %param.23) | copy-start | bytes 32404
  0.9 12.2 %collective-permute-start.7 = (bf16[96,768]{1,0:T(8,128)(2,1)S(1)}, bf16[96,768]{1,0:T(8,128)(2,1)S(1)}, u32[]{:S(2)}, u32[]{:S(2)}) collective-permute-start(bf16[96,768]{1,0:T(8,128)(2,1)S(1)} %pad_maximum_fusion.4), channel_id=1, source_target_pairs={{0,8},{8,0},{1,9},{9,1},{2,10},{10,2},{3,11},{11,3},{4,12},{12,4},... | collective-permute-start | bytes 442376 | tf_op jit(solution)/shard_map/ppermute | solution.py:269
  2.7 0.7 copy-start.2
  3.3 9.8 %copy-start.3 = (bf16[48,768]{1,0:T(8,128)(2,1)S(1)}, bf16[48,768]{1,0:T(8,128)(2,1)}, u32[]{:S(2)}) copy-start(bf16[48,768]{1,0:T(8,128)(2,1)} %param.24) | copy-start | bytes 221188
  3.3 9.8 %copy-start.4 = (bf16[48,768]{1,0:T(8,128)(2,1)S(1)}, bf16[48,768]{1,0:T(8,128)(2,1)}, u32[]{:S(2)}) copy-start(bf16[48,768]{1,0:T(8,128)(2,1)} %param.25) | copy-start | bytes 221188
  8.8 5.8 %collective-permute-start.2 = (bf16[256,768]{1,0:T(8,128)(2,1)S(1)}, bf16[256,768]{1,0:T(8,128)(2,1)S(1)}, u32[]{:S(2)}, u32[]{:S(2)}) collective-permute-start(bf16[256,768]{1,0:T(8,128)(2,1)S(1)} %get-tuple-element.12), channel_id=1, source_target_pairs={{0,4},{4,0},{1,5},{5,1},{2,6},{6,2},{3,7},{7,3},{8,12},{12,8},{9,1... | collective-permute-start | bytes 1179656 | tf_op jit(solution)/shard_map/ppermute | solution.py:269
  9.8 54.1 %collective-permute-start = (bf16[128,768]{1,0:T(8,128)(2,1)S(1)}, bf16[128,768]{1,0:T(8,128)(2,1)S(1)}, u32[]{:S(2)}, u32[]{:S(2)}) collective-permute-start(bf16[128,768]{1,0:T(8,128)(2,1)S(1)} %get-tuple-element.9), channel_id=1, source_target_pairs={{0,1},{1,2},{2,3},{3,0},{4,5},{5,6},{6,7},{7,4},{8,9},{9,10},{10,1... | collective-permute-start | bytes 589832 | tf_op jit(solution)/shard_map/ppermute | solution.py:345
  13.1 50.8 %collective-permute-start.1 = (bf16[128,768]{1,0:T(8,128)(2,1)S(1)}, bf16[128,768]{1,0:T(8,128)(2,1)S(1)}, u32[]{:S(2)}, u32[]{:S(2)}) collective-permute-start(bf16[128,768]{1,0:T(8,128)(2,1)S(1)} %get-tuple-element.10), channel_id=1, source_target_pairs={{0,3},{1,0},{2,1},{3,2},{4,7},{5,4},{6,5},{7,6},{8,11},{9,8},{10,9... | collective-permute-start | bytes 589832 | tf_op jit(solution)/shard_map/ppermute | solution.py:346
  13.2 11.3 %collective-permute-start.13 = (bf16[96,768]{1,0:T(8,128)(2,1)S(1)}, bf16[96,768]{1,0:T(8,128)(2,1)S(1)}, u32[]{:S(2)}, u32[]{:S(2)}) collective-permute-start(bf16[96,768]{1,0:T(8,128)(2,1)S(1)} %get-tuple-element.18), channel_id=1, source_target_pairs={{0,16},{16,0},{32,48},{48,32},{1,17},{17,1},{33,49},{49,33},{2,18}... | collective-permute-start | bytes 442376 | tf_op jit(solution)/shard_map/ppermute | solution.py:289
  15.5 14.7 %all-to-all-start = ((bf16[16,16,768]{2,1,0:T(8,128)(2,1)}), bf16[16,16,768]{2,1,0:T(8,128)(2,1)S(1)}, u32[]{:S(2)}, u32[]{:S(2)}) async-start(bf16[16,16,768]{2,1,0:T(8,128)(2,1)} %bitcast.2), calls=%async_computation | async-start | bytes 786432 | tf_op jit(solution)/shard_map/all_to_all | solution.py:350
  22.0 11.7 %collective-permute-start.8 = (bf16[96,768]{1,0:T(8,128)(2,1)S(1)}, bf16[96,768]{1,0:T(8,128)(2,1)S(1)}, u32[]{:S(2)}, u32[]{:S(2)}) collective-permute-start(bf16[96,768]{1,0:T(8,128)(2,1)S(1)} %get-tuple-element.25), channel_id=1, source_target_pairs={{0,64},{64,0},{128,192},{192,128},{1,65},{65,1},{129,193},{193,129... | collective-permute-start | bytes 442376 | tf_op jit(solution)/shard_map/ppermute | solution.py:289
  24.6 24.2 %collective-permute-start.14 = (bf16[2,96,768]{2,1,0:T(8,128)(2,1)S(1)}, bf16[2,96,768]{2,1,0:T(8,128)(2,1)S(1)}, u32[]{:S(2)}, u32[]{:S(2)}) collective-permute-start(bf16[2,96,768]{2,1,0:T(8,128)(2,1)S(1)} %pad_maximum_fusion.3), channel_id=1, source_target_pairs={{16,32},{32,16},{48,0},{0,48},{17,33},{33,17},{49,1},{1,49},{18,34... | collective-permute-start | bytes 884744 | tf_op jit(solution)/shard_map/ppermute | solution.py:294
  30.3 4.2 %collective-permute-start.3 = (bf16[4,768]{1,0:T(4,128)(2,1)S(1)}, bf16[4,768]{1,0:T(4,128)(2,1)S(1)}, u32[]{:S(2)}, u32[]{:S(2)}) collective-permute-start(bf16[4,768]{1,0:T(4,128)(2,1)S(1)} %get-tuple-element.23), channel_id=1, source_target_pairs={{0,1},{1,2},{2,3},{3,0},{4,5},{5,6},{6,7},{7,4},{8,9},{9,10},{10,1... | collective-permute-start | bytes 18440 | tf_op jit(solution)/shard_map/ppermute | solution.py:354
  33.7 4.6 %collective-permute-start.4 = (bf16[4,768]{1,0:T(4,128)(2,1)S(1)}, bf16[4,768]{1,0:T(4,128)(2,1)S(1)}, u32[]{:S(2)}, u32[]{:S(2)}) collective-permute-start(bf16[4,768]{1,0:T(4,128)(2,1)S(1)} %get-tuple-element.24), channel_id=1, source_target_pairs={{0,3},{1,0},{2,1},{3,2},{4,7},{5,4},{6,5},{7,6},{8,11},{9,8},{10,9... | collective-permute-start | bytes 18440 | tf_op jit(solution)/shard_map/ppermute | solution.py:355
  38.3 2.9 %collective-permute-start.5 = (bf16[24,768]{1,0:T(8,128)(2,1)S(1)}, bf16[24,768]{1,0:T(8,128)(2,1)S(1)}, u32[]{:S(2)}, u32[]{:S(2)}) collective-permute-start(bf16[24,768]{1,0:T(8,128)(2,1)S(1)} %pad_maximum_fusion.7), channel_id=1, source_target_pairs={{0,8},{8,0},{1,9},{9,1},{2,10},{10,2},{3,11},{11,3},{4,12},{12,4},... | collective-permute-start | bytes 110600 | tf_op jit(solution)/shard_map/ppermute | solution.py:269
  39.1 9.6 %collective-permute-start.9 = (bf16[2,96,768]{2,1,0:T(8,128)(2,1)S(1)}, bf16[2,96,768]{2,1,0:T(8,128)(2,1)S(1)}, u32[]{:S(2)}, u32[]{:S(2)}) collective-permute-start(bf16[2,96,768]{2,1,0:T(8,128)(2,1)S(1)} %pad_maximum_fusion.2), channel_id=1, source_target_pairs={{64,128},{128,64},{192,0},{0,192},{65,129},{129,65},{193,1},{1,193... | collective-permute-start | bytes 884744 | tf_op jit(solution)/shard_map/ppermute | solution.py:294
  42.1 14.3 %all-to-all-start.1 = ((bf16[16,24,768]{2,1,0:T(8,128)(2,1)}), bf16[16,24,768]{2,1,0:T(8,128)(2,1)S(1)}, u32[]{:S(2)}, u32[]{:S(2)}) async-start(bf16[16,24,768]{2,1,0:T(8,128)(2,1)} %broadcast_in_dim.42), calls=%async_computation.1 | async-start | bytes 1179648 | tf_op jit(solution)/shard_map/all_to_all | solution.py:361
  56.4 8.4 %collective-permute-start.6 = (bf16[16,24,768]{2,1,0:T(8,128)(2,1)S(1)}, bf16[16,24,768]{2,1,0:T(8,128)(2,1)S(1)}, u32[]{:S(2)}, u32[]{:S(2)}) collective-permute-start(bf16[16,24,768]{2,1,0:T(8,128)(2,1)S(1)} %all-to-all-done.1.mine_ref), channel_id=1, source_target_pairs={{0,4},{4,0},{1,5},{5,1},{2,6},{6,2},{3,7},{7,3},{8,12},{12,8},{9,1... | collective-permute-start | bytes 1769480 | tf_op jit(solution)/shard_map/ppermute | solution.py:269
  63.2 1.6 %copy-start.1 = (bf16[1,16,32,768]{3,2,1,0:T(8,128)(2,1)S(1)}, bf16[1,16,32,768]{3,2,1,0:T(8,128)(2,1)}, u32[]{:S(2)}) copy-start(bf16[1,16,32,768]{3,2,1,0:T(8,128)(2,1)} %param.13) | copy-start | bytes 2359300
  63.3 19.3 %collective-permute-start.10 = (bf16[4,96,768]{2,1,0:T(8,128)(2,1)S(1)}, bf16[4,96,768]{2,1,0:T(8,128)(2,1)S(1)}, u32[]{:S(2)}, u32[]{:S(2)}) collective-permute-start(bf16[4,96,768]{2,1,0:T(8,128)(2,1)S(1)} %pad_maximum_fusion.refs_1_), channel_id=1, source_target_pairs={{0,16},{16,32},{32,48},{48,0},{1,17},{17,33},{33,49},{49,1},{2,18}... | collective-permute-start | bytes 1769480 | tf_op jit(solution)/shard_map/ppermute | solution.py:275
  63.8 18.8 %collective-permute-start.15 = (bf16[4,96,768]{2,1,0:T(8,128)(2,1)S(1)}, bf16[4,96,768]{2,1,0:T(8,128)(2,1)S(1)}, u32[]{:S(2)}, u32[]{:S(2)}) collective-permute-start(bf16[4,96,768]{2,1,0:T(8,128)(2,1)S(1)} %pad_maximum_fusion.1.refs_5_), channel_id=1, source_target_pairs={{0,64},{64,128},{128,192},{192,0},{1,65},{65,129},{129,193},{193,1... | collective-permute-start | bytes 1769480 | tf_op jit(solution)/shard_map/ppermute | solution.py:275
  77.8 20.6 %collective-permute-start.18 = (bf16[512,768]{1,0:T(8,128)(2,1)S(1)}, bf16[512,768]{1,0:T(8,128)(2,1)S(1)}, u32[]{:S(2)}, u32[]{:S(2)}) collective-permute-start(bf16[512,768]{1,0:T(8,128)(2,1)S(1)} %attend.1.refs_0_), channel_id=1, source_target_pairs={{0,4},{4,0},{1,5},{5,1},{2,6},{6,2},{3,7},{7,3},{8,12},{12,8},{9,1... | collective-permute-start | bytes 2359304 | tf_op jit(solution)/shard_map/ppermute | solution.py:269
  78.3 14.8 %collective-permute-start.11 = (bf16[4,96,768]{2,1,0:T(8,128)(2,1)S(1)}, bf16[4,96,768]{2,1,0:T(8,128)(2,1)S(1)}, u32[]{:S(2)}, u32[]{:S(2)}) collective-permute-start(bf16[4,96,768]{2,1,0:T(8,128)(2,1)S(1)} %pad_maximum_fusion.refs_1_), channel_id=1, source_target_pairs={{0,48},{16,0},{32,16},{48,32},{1,49},{17,1},{33,17},{49,33},{2,50}... | collective-permute-start | bytes 1769480 | tf_op jit(solution)/shard_map/ppermute | solution.py:276
  79.7 15.2 %collective-permute-start.16 = (bf16[4,96,768]{2,1,0:T(8,128)(2,1)S(1)}, bf16[4,96,768]{2,1,0:T(8,128)(2,1)S(1)}, u32[]{:S(2)}, u32[]{:S(2)}) collective-permute-start(bf16[4,96,768]{2,1,0:T(8,128)(2,1)S(1)} %pad_maximum_fusion.1.refs_5_), channel_id=1, source_target_pairs={{0,192},{64,0},{128,64},{192,128},{1,193},{65,1},{129,65},{193,129... | collective-permute-start | bytes 1769480 | tf_op jit(solution)/shard_map/ppermute | solution.py:276
  82.6 15.4 %collective-permute-start.12 = (bf16[4,96,768]{2,1,0:T(8,128)(2,1)S(1)}, bf16[4,96,768]{2,1,0:T(8,128)(2,1)S(1)}, u32[]{:S(2)}, u32[]{:S(2)}) collective-permute-start(bf16[4,96,768]{2,1,0:T(8,128)(2,1)S(1)} %collective-permute-done.10.refs_2_), channel_id=1, source_target_pairs={{0,16},{16,32},{32,48},{48,0},{1,17},{17,33},{33,49},{49,1},{2,18}... | collective-permute-start | bytes 1769480 | tf_op jit(solution)/shard_map/ppermute | solution.py:277
  82.6 15.7 %collective-permute-start.17 = (bf16[4,96,768]{2,1,0:T(8,128)(2,1)S(1)}, bf16[4,96,768]{2,1,0:T(8,128)(2,1)S(1)}, u32[]{:S(2)}, u32[]{:S(2)}) collective-permute-start(bf16[4,96,768]{2,1,0:T(8,128)(2,1)S(1)} %collective-permute-done.15.refs_6_), channel_id=1, source_target_pairs={{0,64},{64,128},{128,192},{192,0},{1,65},{65,129},{129,193},{193,1... | collective-permute-start | bytes 1769480 | tf_op jit(solution)/shard_map/ppermute | solution.py:277
  101.3 4.5 %collective-permute-start.19 = (bf16[512,768]{1,0:T(8,128)(2,1)S(1)}, bf16[512,768]{1,0:T(8,128)(2,1)S(1)}, u32[]{:S(2)}, u32[]{:S(2)}) collective-permute-start(bf16[512,768]{1,0:T(8,128)(2,1)S(1)} %feed_forward_partner.1), channel_id=1, source_target_pairs={{0,4},{4,0},{1,5},{5,1},{2,6},{6,2},{3,7},{7,3},{8,12},{12,8},{9,1... | collective-permute-start | bytes 2359304 | tf_op jit(solution)/shard_map/ppermute | solution.py:269

commit v3 on v1

--- a/solution.py
+++ b/solution.py
@@ -14,6 +14,7 @@
 ROWS = 16
 COLS = 32
 NLAT = 64
+EDGE = WIN // 2 * COLS
 GROUPS = 3
 MEMBER = ("mx", "my", "mz", "core")
 PLANE = ("mx", "my")
@@ -60,7 +61,7 @@
     return row, col
 
 
-def encode_kernel(chosen, frame_hbm, in_hbm, out_hbm, joint_hbm, keep_ref, send_ref, frame, w_in, w_out, w_slot, sems):
+def encode_kernel(chosen, frame_hbm, in_hbm, out_hbm, joint_hbm, keep_ref, send_ref, frame, w_in, w_out, w_slot, term_ref, sems):
     own_core = axis_index("core")
     member = axis_index(MEMBER)
     is_second = member == chosen[1]
@@ -74,29 +75,24 @@
     ]
     for c in copies:
         c.start()
-    tokens = ROWS * COLS
-    t = row_ids(tokens)
-    half = tokens // 2
-    core = jnp.where(t < half, own_core, 1 - own_core)
-    col = core * (COLS // 2) + (t % half) // ROWS
-    order = one_hot((t % ROWS) * COLS + col, tokens)
     copies[0].wait()
-    ordered = dot(order, frame[...]).astype(BF16)
     copies[1].wait()
-    hidden = jax.nn.gelu(dot(ordered, w_in[...])).astype(BF16)
+    hidden = jax.nn.gelu(dot(frame[...], w_in[...])).astype(BF16)
     copies[2].wait()
     condition = dot(hidden, w_out[...]).astype(BF16)
     copies[3].wait()
     term = dot(condition, w_slot[...])
-    term = jnp.where(is_source, term, 0.0).astype(BF16)
-    keep_ref[...] = term[:half]
-    send_ref[...] = term[half:]
+    term_ref[...] = jnp.where(is_source, term, 0.0)
+    for half, out_ref in ((own_core, keep_ref), (1 - own_core, send_ref)):
+        for slot, start in enumerate((jnp.where(half == 0, 0, 384), jnp.where(half == 0, 128, 256))):
+            block = term_ref[pl.ds(pl.multiple_of(start, 128), 128), :]
+            out_ref[:, slot * 8 : slot * 8 + 8, :] = block.reshape(16, 8, D).astype(BF16)
 
 
 def encode(chosen, frame, w_in, w_out, joint):
     tokens = ROWS * COLS
     any_spec = pl.BlockSpec(memory_space=pltpu.HBM)
-    out = jax.ShapeDtypeStruct((tokens // 2, D), BF16)
+    out = jax.ShapeDtypeStruct((16, 16, D), BF16)
     return pl.pallas_call(
         encode_kernel,
         name="encode",
@@ -107,6 +103,7 @@
             pltpu.VMEM((D, D), BF16),
             pltpu.VMEM((D, D), BF16),
             pltpu.VMEM((D, D), BF16),
+            pltpu.VMEM((tokens, D), F32),
             pltpu.SemaphoreType.DMA((4,)),
         ],
         compiler_params=pltpu.CompilerParams(vmem_limit_bytes=24 << 20),
@@ -133,28 +130,26 @@
             at = WIN * (WIN - 1 - r)
             bias_ref[h // 2, WIN * r : WIN * (r + 1), (h % 2) * HD : (h % 2 + 1) * HD] = strip_ref[h, :, at : at + HD]
     row, col = window_place(256, shift)
-    half = COLS // 2
-    place = (col % half) * WIN + row
-    from_mine = one_hot(jnp.where(col // half == core, place, -1), 128)
-    from_other = one_hot(jnp.where(col // half == core, -1, place), 128)
     order = one_hot(row * COLS + col, 256)
-    tokens = ((up_ref[...], own_ref[:128, :]), (own_ref[128:384, :],), (own_ref[384:, :], down_ref[...]))
-    for g in range(GROUPS):
-        placed = dot(order, jnp.concatenate(tokens[g], axis=0) if len(tokens[g]) > 1 else tokens[g][0])
-        mixed_ref[g * 256 : (g + 1) * 256, :] = placed.astype(BF16)
+    tokens = jnp.concatenate([up_ref[...], own_ref[...], down_ref[...]], axis=0)
     copies[0].wait()
-    noisy = dot(mixed_ref[...], w0[...])
-    for g in range(GROUPS):
-        mine = mine_ref[:, g * WIN : (g + 1) * WIN, :].astype(F32).reshape(128, D).astype(BF16)
-        other = other_ref[:, g * WIN : (g + 1) * WIN, :].astype(F32).reshape(128, D).astype(BF16)
-        stream = (noisy[g * 256 : (g + 1) * 256] + (dot(from_mine, mine) + dot(from_other, other))).astype(BF16)
-        stream_ref[g * 256 : (g + 1) * 256, :] = stream
-        normed_ref[g * 256 : (g + 1) * 256, :] = normalised(stream.astype(F32))
+    noisy = dot(tokens, w0[...])
+
+    def block(half, slot):
+        mine, other = (ref[:, slot * 8 : slot * 8 + 8, :].astype(F32).reshape(128, D) for ref in (mine_ref, other_ref))
+        return jnp.where(core == half, mine, other)
+
+    for g, (low, high) in enumerate((((1, 2), (0, 0)), ((0, 1), (1, 1)), ((1, 0), (0, 2)))):
+        rows = slice(g * 256, (g + 1) * 256)
+        stream = (noisy[rows] + jnp.concatenate([block(*low), block(*high)], axis=0)).astype(BF16)
+        stream_ref[rows, :] = stream
+        normed_ref[rows, :] = dot(order, normalised(stream.astype(F32))).astype(BF16)
     copies[1].wait()
     copies[2].wait()
     for n in range(3):
         cols = slice(n * D, (n + 1) * D)
-        qkv_ref[:, cols] = dot(normed_ref[...], wqkv[:, cols]).astype(BF16)
+        made = dot(normed_ref[...], wqkv[:, cols])
+        qkv_ref[:, cols] = (made * HD ** (-0.5) if n == 0 else made).astype(BF16)
     low = lax.broadcasted_iota(jnp.int32, (64, 128), 1) < HD
     key_row = lax.broadcasted_iota(jnp.int32, (64, 128), 0)
 
@@ -172,7 +167,7 @@
             zero = jnp.zeros_like(q)
             both = jnp.concatenate([jnp.where(low, q, zero), jnp.where(low, zero, q)], axis=0)
             scores.append(dot_nt(k, both))
-        scores = [jnp.where(seen, s * HD ** (-0.5) + bias_ref[p], -1e30) for p, s in enumerate(scores)]
+        scores = [jnp.where(seen, s + bias_ref[p], -1e30) for p, s in enumerate(scores)]
         tops = [jnp.max(s, axis=0, keepdims=True) for s in scores]
         weights = [jnp.exp(s - m) for s, m in zip(scores, tops)]
         sums = [1.0 / jnp.sum(e, axis=0, keepdims=True) for e in weights]
@@ -191,10 +186,9 @@
         back = one_hot(base + first * WIN, 256)
         mixed = dot(back, mixed_ref[g * 256 : (g + 1) * 256, :]).astype(BF16)
         normed_ref[b * 128 : (b + 1) * 128, :] = mixed
-        qkv_ref[b * 128 : (b + 1) * 128, :D] = dot(back, stream_ref[g * 256 : (g + 1) * 256, :]).astype(BF16)
     copies[3].wait()
     tokens = ROWS * COLS
-    out_ref[...] = (qkv_ref[:tokens, :D].astype(F32) + dot(normed_ref[:tokens, :], wo[...])).astype(BF16)
+    out_ref[...] = (stream_ref[EDGE : EDGE + tokens, :].astype(F32) + dot(normed_ref[:tokens, :], wo[...])).astype(BF16)
 
 
 def attend(shift, up, own, down, mine, other, strip, joint, wq, wkv, wo):
@@ -309,26 +303,23 @@
     reduce_weight,
 ):
     tokens = ROWS * COLS
-    margin = WIN // 2
     bands = lax.axis_size("lat")
     noisy = noisy_latents.reshape(tokens, D)
     to_next = [(i, (i + 1) % bands) for i in range(bands)]
     to_last = [(i, (i - 1) % bands) for i in range(bands)]
-    edge = margin * COLS
 
     keep, send = encode(encoder_members, frames.reshape(tokens, D), encoder_in, encoder_out, joint_weight)
     ups, downs = gathered_weights(expand_weight, reduce_weight)
-    noisy_up = lax.ppermute(noisy[tokens - edge :], "lat", to_next)
-    noisy_down = lax.ppermute(noisy[:edge], "lat", to_last)
-
-    mine = (keep + swap(send, "core")).reshape(COLS // 2, ROWS, D)
+    noisy_up = lax.ppermute(noisy[tokens - EDGE :], "lat", to_next)
+    noisy_down = lax.ppermute(noisy[:EDGE], "lat", to_last)
+
+    mine = keep + swap(send, "core")
     spread = lax.all_to_all(mine, PLANE, 0, 0, tiled=True)
     part = jnp.sum(spread.astype(F32), axis=0).astype(BF16)
-    above = lax.ppermute(part[ROWS - margin :], "lat", to_next)
-    below = lax.ppermute(part[:margin], "lat", to_last)
-    part = jnp.concatenate([above, part, below], axis=0)
+    pairs = [(l, (l - 1) % bands) for l in range(bands)] + [(bands + l, bands + (l + 1) % bands) for l in range(bands)]
+    part = jnp.concatenate([part, lax.ppermute(part[:8], ("core", "lat"), pairs)], axis=0)
     part = part + swap(part, "mz")
-    wide = jnp.broadcast_to(part[None], (COLS // 2, *part.shape))
+    wide = jnp.broadcast_to(part[None], (16, *part.shape))
     mine = lax.all_to_all(wide, PLANE, 0, 0, tiled=True)
     other = swap(mine, "core")
 

time: 119 us -> 116 us (0.975)
  waiting for transfers between devices: 36.7 us -> 33.7 us
    ppermute x4 -> x3, waiting for transfers between devices: 9.09 us -> 5.97 us  [the longest x1 2.43 us: body(): noisy_up = lax.ppermute(noisy[tokens - EDGE:], 'lat', to_next)]
    ppermute x4 -> x3, starting transfers between devices: 9.7 us -> 9.62 us  [the longest x1 5.48 us: body(): lax.ppermute(part[:8], ('core', 'lat'), pairs)]
  transfers between devices with their start and end apart: 23 -> 22, of which waited for: 12 -> 11; matrix products, arithmetic and copies ran while one was open for 3% -> 3% of each run, Pallas kernels for 14% -> 14%
where the time goes in v3:
time: 116 us; the launch traced here: 114 us
  waiting for transfers between devices  33.7 us (29%)
  starting transfers between devices  33.4 us (29%)
  Pallas kernels  23.8 us (21%)
  blocking collectives  17.1 us (15%)
  other arithmetic  3.07 us (3%)
  local copies, waits for them, and re-layouts  1.67 us (1%)
    all_to_all x1, blocking collectives, body(): spread = lax.all_to_all(mine, PLANE, 0, 0, tiled=True)  17.1 us
    pallas_call x1, Pallas kernels, attend(): pl.pallas_call(attend_kernel, name='attend', in_specs=[pl.BlockSpec(memor...  12.7 us
    ppermute x2, waiting for transfers between devices, ring_from_all(): ahead = lax.ppermute(mine, axis, back)  12.7 us
    ppermute x6, starting transfers between devices, row_from_all(): lax.ppermute(mine, axis, [(i, (i + by) % 4) for i in range(4)])  11.3 us
    pallas_call x2, Pallas kernels, feed_forward(): pl.pallas_call(lambda *refs: forward_kernel(keep, *refs), name='feed_forw...  5.82 us
    ppermute x6, waiting for transfers between devices, row_from_all(): lax.ppermute(mine, axis, [(i, (i + by) % 4) for i in range(4)])  5.81 us
    ppermute x1, starting transfers between devices, body(): lax.ppermute(part[:8], ('core', 'lat'), pairs)  5.48 us
    pallas_call x1, Pallas kernels, encode(): pl.pallas_call(encode_kernel, name='encode', in_specs=[pl.BlockSpec(memor...  5.28 us
  transfers between devices with their start and end apart: 22, of which 11 were waited for; matrix products, arithmetic and copies ran while one was open for 3% of the time, Pallas kernels for 14%

profile of v3, /device:TPU:32, one launch (start us, length us, event | category | flops | bytes accessed | tf_op | source)
XLA Modules:
  0.0 114.4 jit_solution(4382407918194072501)
XLA Ops:
  0.0 0.0 copy-start
  0.0 0.7 copy-done.2
  0.7 5.3 %encode.1 = (bf16[16,16,768]{2,1,0:T(8,128)(2,1)S(1)}, bf16[16,16,768]{2,1,0:T(8,128)(2,1)S(1)}) custom-call(s32[2]{0:T(128)S(1)} %copy-done.2, bf16[512,768]{1,0:T(8,128)(2,1)} %bitcast.26, bf16[768,768]{1,0:T(8,128)(2,1)} %in_hbm.1, bf16[768,768]{1,0:T(8,128)(2,1)} %out_hbm.1, bf16[2304,768]{1,0:T(8,128)(2,1)} %w0_hbm.1), custom_call_target="tpu_custom_call" | custom-call | flops 2214592512 | bytes 6000000 | tf_op jit(solution)/shard_map/encode/pallas_call | solution.py:96
  6.0 0.0 copy-start.3
  6.0 0.0 copy-start.4
  6.0 0.1 collective-permute-start.2
  6.1 1.7 %collective-permute-done.2 = bf16[16,16,768]{2,1,0:T(8,128)(2,1)S(1)} collective-permute-done((bf16[16,16,768]{2,1,0:T(8,128)(2,1)S(1)}, bf16[16,16,768]{2,1,0:T(8,128)(2,1)S(1)}, u32[]{:S(2)}, u32[]{:S(2)}) %collective-permute-start.2) | collective-permute-done | bytes 393248 | tf_op jit(solution)/shard_map/ppermute | solution.py:257
  7.8 0.1 add.28
  7.9 0.0 copy-start.1
  7.9 17.1 %all_to_all.10 = bf16[16,16,768]{2,1,0:T(8,128)(2,1)S(1)} all-to-all(bf16[16,16,768]{2,1,0:T(8,128)(2,1)S(1)} %add.28), channel_id=1, replica_groups=mesh['mx'=4,'my'=4,'mz'=2,'core'=2,'lat'=4] {'mx','my'}, dimensions={0} | all-to-all | bytes 786432 | tf_op jit(solution)/shard_map/all_to_all | solution.py:317
  25.0 0.1 reduce_sum.12
  25.1 5.5 %collective-permute-start.3 = (bf16[8,768]{1,0:T(8,128)(2,1)S(1)}, bf16[8,768]{1,0:T(8,128)(2,1)S(1)}, u32[]{:S(2)}, u32[]{:S(2)}) collective-permute-start(bf16[8,768]{1,0:T(8,128)(2,1)S(1)} %slice.28), channel_id=1, source_target_pairs={{0,3},{1,0},{2,1},{3,2},{4,5},{5,6},{6,7},{7,4},{8,11},{9,8},{10,9... | collective-permute-start | bytes 36872 | tf_op jit(solution)/shard_map/ppermute | solution.py:320
  30.5 1.4 %collective-permute-done.3 = bf16[8,768]{1,0:T(8,128)(2,1)S(1)} collective-permute-done((bf16[8,768]{1,0:T(8,128)(2,1)S(1)}, bf16[8,768]{1,0:T(8,128)(2,1)S(1)}, u32[]{:S(2)}, u32[]{:S(2)}) %collective-permute-start.3) | collective-permute-done | bytes 12320 | tf_op jit(solution)/shard_map/ppermute | solution.py:320
  32.0 1.0 collective-permute-start.4
  33.0 0.0 copy-done.4
  33.0 1.1 collective-permute-start.6
  34.1 1.8 %collective-permute-done.4 = bf16[24,768]{1,0:T(8,128)(2,1)S(1)} collective-permute-done((bf16[24,768]{1,0:T(8,128)(2,1)S(1)}, bf16[24,768]{1,0:T(8,128)(2,1)S(1)}, u32[]{:S(2)}, u32[]{:S(2)}) %collective-permute-start.4) | collective-permute-done | bytes 36896 | tf_op jit(solution)/shard_map/ppermute | solution.py:257
  35.9 0.9 broadcast_in_dim.16
  36.8 3.7 %all-to-all-start.1 = ((bf16[16,24,768]{2,1,0:T(8,128)(2,1)}), bf16[16,24,768]{2,1,0:T(8,128)(2,1)S(1)}, u32[]{:S(2)}, u32[]{:S(2)}) async-start(bf16[16,24,768]{2,1,0:T(8,128)(2,1)} %broadcast_in_dim.16), calls=%async_computation.1 | async-start | bytes 1179648 | tf_op jit(solution)/shard_map/all_to_all | solution.py:323
  40.6 0.0 collective-permute-done.6
  40.6 0.8 fusion.14
  41.3 3.1 %collective-permute-start.14 = (bf16[96,768]{1,0:T(8,128)(2,1)}, bf16[96,768]{1,0:T(8,128)(2,1)S(1)}, u32[]{:S(2)}, u32[]{:S(2)}) collective-permute-start(bf16[96,768]{1,0:T(8,128)(2,1)} %get-tuple-element.12), channel_id=1, source_target_pairs={{0,48},{16,0},{32,16},{48,32},{1,49},{17,1},{33,17},{49,33},{2,50}... | collective-permute-start | bytes 442376 | tf_op jit(solution)/shard_map/ppermute | solution.py:270
  44.5 2.7 %collective-permute-start.8 = (bf16[96,768]{1,0:T(8,128)(2,1)}, bf16[96,768]{1,0:T(8,128)(2,1)S(1)}, u32[]{:S(2)}, u32[]{:S(2)}) collective-permute-start(bf16[96,768]{1,0:T(8,128)(2,1)} %get-tuple-element.17), channel_id=1, source_target_pairs={{0,192},{64,0},{128,64},{192,128},{1,193},{65,1},{129,65},{193,129... | collective-permute-start | bytes 442376 | tf_op jit(solution)/shard_map/ppermute | solution.py:270
  47.2 3.9 %all-to-all-done.1.mine_ref = bf16[16,24,768]{2,1,0:T(8,128)(2,1)S(1)} async-done(((bf16[16,24,768]{2,1,0:T(8,128)(2,1)}), bf16[16,24,768]{2,1,0:T(8,128)(2,1)S(1)}, u32[]{:S(2)}, u32[]{:S(2)}) %all-to-all-start.1) | async-done | bytes 589856 | tf_op jit(solution)/shard_map/all_to_all | solution.py:323
  51.0 0.0 collective-permute-start.5
  51.1 0.6 collective-permute-start.13
  51.7 1.8 %collective-permute-start.15 = (bf16[96,768]{1,0:T(8,128)(2,1)}, bf16[96,768]{1,0:T(8,128)(2,1)S(1)}, u32[]{:S(2)}, u32[]{:S(2)}) collective-permute-start(bf16[96,768]{1,0:T(8,128)(2,1)} %get-tuple-element.12), channel_id=1, source_target_pairs={{0,32},{16,48},{32,0},{48,16},{1,33},{17,49},{33,1},{49,17},{2,34}... | collective-permute-start | bytes 442376 | tf_op jit(solution)/shard_map/ppermute | solution.py:270
  53.5 0.0 collective-permute-done.14
  53.5 0.9 collective-permute-start.7
  54.4 0.0 collective-permute-done.8
  54.4 2.1 %collective-permute-start.9 = (bf16[96,768]{1,0:T(8,128)(2,1)}, bf16[96,768]{1,0:T(8,128)(2,1)}, u32[]{:S(2)}, u32[]{:S(2)}) collective-permute-start(bf16[96,768]{1,0:T(8,128)(2,1)} %get-tuple-element.17), channel_id=1, source_target_pairs={{0,128},{64,192},{128,0},{192,64},{1,129},{65,193},{129,1},{193,65... | collective-permute-start | bytes 442376 | tf_op jit(solution)/shard_map/ppermute | solution.py:270
  56.5 0.7 convolution_bitcast_fusion
  57.9 0.1 reshape.18.strip_ref
  58.0 5.8 %collective-permute-done.7 = bf16[96,768]{1,0:T(8,128)(2,1)S(1)} collective-permute-done((bf16[96,768]{1,0:T(8,128)(2,1)}, bf16[96,768]{1,0:T(8,128)(2,1)S(1)}, u32[]{:S(2)}, u32[]{:S(2)}) %collective-permute-start.7) | collective-permute-done | bytes 147488 | tf_op jit(solution)/shard_map/ppermute | solution.py:270
  63.8 1.9 %collective-permute-start = (bf16[128,768]{1,0:T(8,128)(2,1)S(1)}, bf16[128,768]{1,0:T(8,128)(2,1)S(1)}, u32[]{:S(2)}, u32[]{:S(2)}) collective-permute-start(bf16[128,768]{1,0:T(8,128)(2,1)S(1)} %bitcast.20), channel_id=1, source_target_pairs={{0,1},{1,2},{2,3},{3,0},{4,5},{5,6},{6,7},{7,4},{8,9},{9,10},{10,1... | collective-permute-start | bytes 589832 | tf_op jit(solution)/shard_map/ppermute | solution.py:313
  65.6 0.0 collective-permute-done.9
  65.6 2.3 %collective-permute-start.1 = (bf16[128,768]{1,0:T(8,128)(2,1)S(1)}, bf16[128,768]{1,0:T(8,128)(2,1)S(1)}, u32[]{:S(2)}, u32[]{:S(2)}) collective-permute-start(bf16[128,768]{1,0:T(8,128)(2,1)S(1)} %bitcast.19), channel_id=1, source_target_pairs={{0,3},{1,0},{2,1},{3,2},{4,7},{5,4},{6,5},{7,6},{8,11},{9,8},{10,9... | collective-permute-start | bytes 589832 | tf_op jit(solution)/shard_map/ppermute | solution.py:314
  67.9 1.0 pad_maximum_fusion.refs_1_
  68.9 0.0 collective-permute-done.13
  68.9 2.1 %collective-permute-start.10 = (bf16[4,96,768]{2,1,0:T(8,128)(2,1)S(1)}, bf16[4,96,768]{2,1,0:T(8,128)(2,1)S(1)}, u32[]{:S(2)}, u32[]{:S(2)}) collective-permute-start(bf16[4,96,768]{2,1,0:T(8,128)(2,1)S(1)} %pad_maximum_fusion.refs_1_), channel_id=1, source_target_pairs={{0,16},{16,32},{32,48},{48,0},{1,17},{17,33},{33,49},{49,1},{2,18}... | collective-permute-start | bytes 1769480 | tf_op jit(solution)/shard_map/ppermute | solution.py:263
  71.1 0.0 collective-permute-done.15
  71.1 0.1 pad_maximum_fusion.1.refs_5_
  71.1 0.1 collective-permute-start.16
  71.2 2.4 %collective-permute-done.up_ref = bf16[128,768]{1,0:T(8,128)(2,1)S(1)} collective-permute-done((bf16[128,768]{1,0:T(8,128)(2,1)S(1)}, bf16[128,768]{1,0:T(8,128)(2,1)S(1)}, u32[]{:S(2)}, u32[]{:S(2)}) %collective-permute-start) | collective-permute-done | bytes 196640 | tf_op jit(solution)/shard_map/ppermute | solution.py:313
  73.7 2.1 %collective-permute-done.1.down_ref = bf16[128,768]{1,0:T(8,128)(2,1)S(1)} collective-permute-done((bf16[128,768]{1,0:T(8,128)(2,1)S(1)}, bf16[128,768]{1,0:T(8,128)(2,1)S(1)}, u32[]{:S(2)}, u32[]{:S(2)}) %collective-permute-start.1) | collective-permute-done | bytes 196640 | tf_op jit(solution)/shard_map/ppermute | solution.py:314
  75.8 0.0 collective-permute-done.5.other_ref
  75.8 12.7 %attend.1.refs_0_ = bf16[512,768]{1,0:T(8,128)(2,1)S(1)} custom-call(s32[1]{0:T(128)S(6)} %copy.14.shift_ref, bf16[128,768]{1,0:T(8,128)(2,1)S(1)} %collective-permute-done.up_ref, bf16[512,768]{1,0:T(8,128)(2,1)S(1)} %bitcast.18, bf16[128,768]{1,0:T(8,128)(2,1)S(1)} %collective-permute-done.1.down_ref, bf16[16,24,768]{2,1,0:T(8,128)(2,1)S(1)} %all-to-all-done.1.mine_ref, ...), custom_call_target="tpu_custom_call" | custom-call | flops 5435817984 | bytes 10000000 | tf_op jit(solution)/shard_map/attend/pallas_call | solution.py:196
  88.5 0.1 collective-permute-start.19
  88.6 1.6 %collective-permute-start.11 = (bf16[4,96,768]{2,1,0:T(8,128)(2,1)S(1)}, bf16[4,96,768]{2,1,0:T(8,128)(2,1)S(1)}, u32[]{:S(2)}, u32[]{:S(2)}) collective-permute-start(bf16[4,96,768]{2,1,0:T(8,128)(2,1)S(1)} %pad_maximum_fusion.refs_1_), channel_id=1, source_target_pairs={{0,48},{16,0},{32,16},{48,32},{1,49},{17,1},{33,17},{49,33},{2,50}... | collective-permute-start | bytes 1769480 | tf_op jit(solution)/shard_map/ppermute | solution.py:264
  90.2 0.0 collective-permute-start.17
  90.2 0.0 collective-permute-done.10.refs_2_
  90.2 0.7 collective-permute-start.12
  90.9 0.0 collective-permute-done.16.refs_6_
  90.9 1.9 %collective-permute-start.18 = (bf16[4,96,768]{2,1,0:T(8,128)(2,1)S(1)}, bf16[4,96,768]{2,1,0:T(8,128)(2,1)S(1)}, u32[]{:S(2)}, u32[]{:S(2)}) collective-permute-start(bf16[4,96,768]{2,1,0:T(8,128)(2,1)S(1)} %collective-permute-done.16.refs_6_), channel_id=1, source_target_pairs={{0,64},{64,128},{128,192},{192,0},{1,65},{65,129},{129,193},{193,1... | collective-permute-start | bytes 1769480 | tf_op jit(solution)/shard_map/ppermute | solution.py:265
  92.9 11.8 %collective-permute-done.11.refs_3_ = bf16[4,96,768]{2,1,0:T(8,128)(2,1)S(1)} collective-permute-done((bf16[4,96,768]{2,1,0:T(8,128)(2,1)S(1)}, bf16[4,96,768]{2,1,0:T(8,128)(2,1)S(1)}, u32[]{:S(2)}, u32[]{:S(2)}) %collective-permute-start.11) | collective-permute-done | bytes 589856 | tf_op jit(solution)/shard_map/ppermute | solution.py:264
  104.6 0.9 collective-permute-done.17.refs_7_
  105.6 1.2 %collective-permute-done.12.refs_4_ = bf16[4,96,768]{2,1,0:T(8,128)(2,1)S(1)} collective-permute-done((bf16[4,96,768]{2,1,0:T(8,128)(2,1)S(1)}, bf16[4,96,768]{2,1,0:T(8,128)(2,1)S(1)}, u32[]{:S(2)}, u32[]{:S(2)}) %collective-permute-start.12) | collective-permute-done | bytes 589856 | tf_op jit(solution)/shard_map/ppermute | solution.py:265
  106.8 0.6 collective-permute-done.18.refs_8_
  107.4 0.0 collective-permute-done.19.refs_0_
  107.4 2.9 %feed_forward_partner.1 = bf16[512,768]{1,0:T(8,128)(2,1)S(1)} custom-call(bf16[512,768]{1,0:T(8,128)(2,1)S(1)} %collective-permute-done.19.refs_0_, bf16[4,96,768]{2,1,0:T(8,128)(2,1)S(1)} %pad_maximum_fusion.refs_1_, bf16[4,96,768]{2,1,0:T(8,128)(2,1)S(1)} %collective-permute-done.10.refs_2_, bf16[4,96,768]{2,1,0:T(8,128)(2,1)S(1)} %collective-permute-done.11.refs_3_, ...), custom_call_target="tpu_custom_call" | custom-call | flops 2415919104 | bytes 6000000 | tf_op jit(solution)/shard_map/feed_forward_partner/pallas_call | solution.py:244
  110.3 0.1 collective-permute-start.20
  110.4 2.9 %feed_forward_own.1 = f32[512,768]{1,0:T(8,128)S(1)} custom-call(bf16[512,768]{1,0:T(8,128)(2,1)S(1)} %attend.1.refs_0_, bf16[4,96,768]{2,1,0:T(8,128)(2,1)S(1)} %pad_maximum_fusion.refs_1_, bf16[4,96,768]{2,1,0:T(8,128)(2,1)S(1)} %collective-permute-done.10.refs_2_, bf16[4,96,768]{2,1,0:T(8,128)(2,1)S(1)} %collective-permute-done.11.refs_3_, ...), custom_call_target="tpu_custom_call" | custom-call | flops 2415919104 | bytes 6000000 | tf_op jit(solution)/shard_map/feed_forward_own/pallas_call | solution.py:244
  113.3 0.0 collective-permute-done.20
  113.4 1.0 add_convert_fusion
  (12 shorter events, 0.1 us)
Async XLA Ops:
  0.0 56.5 %copy-start = (f32[12,225]{1,0:T(8,128)S(1)}, f32[12,225]{1,0:T(8,128)}, u32[]{:S(2)}) copy-start(f32[12,225]{1,0:T(8,128)} %param.23) | copy-start | bytes 32404
  0.0 0.7 copy-start.2
  6.0 27.0 %copy-start.3 = (bf16[48,768]{1,0:T(8,128)(2,1)S(1)}, bf16[48,768]{1,0:T(8,128)(2,1)}, u32[]{:S(2)}) copy-start(bf16[48,768]{1,0:T(8,128)(2,1)} %param.24) | copy-start | bytes 221188
  6.0 27.0 %copy-start.4 = (bf16[48,768]{1,0:T(8,128)(2,1)S(1)}, bf16[48,768]{1,0:T(8,128)(2,1)}, u32[]{:S(2)}) copy-start(bf16[48,768]{1,0:T(8,128)(2,1)} %param.25) | copy-start | bytes 221188
  6.0 1.8 %collective-permute-start.2 = (bf16[16,16,768]{2,1,0:T(8,128)(2,1)S(1)}, bf16[16,16,768]{2,1,0:T(8,128)(2,1)S(1)}, u32[]{:S(2)}, u32[]{:S(2)}) collective-permute-start(bf16[16,16,768]{2,1,0:T(8,128)(2,1)S(1)} %get-tuple-element.8), channel_id=1, source_target_pairs={{0,4},{4,0},{1,5},{5,1},{2,6},{6,2},{3,7},{7,3},{8,12},{12,8},{9,1... | collective-permute-start | bytes 1179656 | tf_op jit(solution)/shard_map/ppermute | solution.py:257
  7.9 32.6 %copy-start.1 = (bf16[1,16,32,768]{3,2,1,0:T(8,128)(2,1)S(1)}, bf16[1,16,32,768]{3,2,1,0:T(8,128)(2,1)}, u32[]{:S(2)}) copy-start(bf16[1,16,32,768]{3,2,1,0:T(8,128)(2,1)} %param.13) | copy-start | bytes 2359300
  25.1 6.9 %collective-permute-start.3 = (bf16[8,768]{1,0:T(8,128)(2,1)S(1)}, bf16[8,768]{1,0:T(8,128)(2,1)S(1)}, u32[]{:S(2)}, u32[]{:S(2)}) collective-permute-start(bf16[8,768]{1,0:T(8,128)(2,1)S(1)} %slice.28), channel_id=1, source_target_pairs={{0,3},{1,0},{2,1},{3,2},{4,5},{5,6},{6,7},{7,4},{8,11},{9,8},{10,9... | collective-permute-start | bytes 36872 | tf_op jit(solution)/shard_map/ppermute | solution.py:320
  32.0 4.0 %collective-permute-start.4 = (bf16[24,768]{1,0:T(8,128)(2,1)S(1)}, bf16[24,768]{1,0:T(8,128)(2,1)S(1)}, u32[]{:S(2)}, u32[]{:S(2)}) collective-permute-start(bf16[24,768]{1,0:T(8,128)(2,1)S(1)} %pad_maximum_fusion.5), channel_id=1, source_target_pairs={{0,8},{8,0},{1,9},{9,1},{2,10},{10,2},{3,11},{11,3},{4,12},{12,4},... | collective-permute-start | bytes 110600 | tf_op jit(solution)/shard_map/ppermute | solution.py:257
  33.0 7.6 %collective-permute-start.6 = (bf16[96,768]{1,0:T(8,128)(2,1)S(1)}, bf16[96,768]{1,0:T(8,128)(2,1)S(1)}, u32[]{:S(2)}, u32[]{:S(2)}) collective-permute-start(bf16[96,768]{1,0:T(8,128)(2,1)S(1)} %pad_maximum_fusion.2), channel_id=1, source_target_pairs={{0,8},{8,0},{1,9},{9,1},{2,10},{10,2},{3,11},{11,3},{4,12},{12,4},... | collective-permute-start | bytes 442376 | tf_op jit(solution)/shard_map/ppermute | solution.py:257
  36.8 14.2 %all-to-all-start.1 = ((bf16[16,24,768]{2,1,0:T(8,128)(2,1)}), bf16[16,24,768]{2,1,0:T(8,128)(2,1)S(1)}, u32[]{:S(2)}, u32[]{:S(2)}) async-start(bf16[16,24,768]{2,1,0:T(8,128)(2,1)} %broadcast_in_dim.16), calls=%async_computation.1 | async-start | bytes 1179648 | tf_op jit(solution)/shard_map/all_to_all | solution.py:323
  41.3 12.1 %collective-permute-start.14 = (bf16[96,768]{1,0:T(8,128)(2,1)}, bf16[96,768]{1,0:T(8,128)(2,1)S(1)}, u32[]{:S(2)}, u32[]{:S(2)}) collective-permute-start(bf16[96,768]{1,0:T(8,128)(2,1)} %get-tuple-element.12), channel_id=1, source_target_pairs={{0,48},{16,0},{32,16},{48,32},{1,49},{17,1},{33,17},{49,33},{2,50}... | collective-permute-start | bytes 442376 | tf_op jit(solution)/shard_map/ppermute | solution.py:270
  44.5 9.9 %collective-permute-start.8 = (bf16[96,768]{1,0:T(8,128)(2,1)}, bf16[96,768]{1,0:T(8,128)(2,1)S(1)}, u32[]{:S(2)}, u32[]{:S(2)}) collective-permute-start(bf16[96,768]{1,0:T(8,128)(2,1)} %get-tuple-element.17), channel_id=1, source_target_pairs={{0,192},{64,0},{128,64},{192,128},{1,193},{65,1},{129,65},{193,129... | collective-permute-start | bytes 442376 | tf_op jit(solution)/shard_map/ppermute | solution.py:270
  51.0 24.8 %collective-permute-start.5 = (bf16[16,24,768]{2,1,0:T(8,128)(2,1)S(1)}, bf16[16,24,768]{2,1,0:T(8,128)(2,1)S(1)}, u32[]{:S(2)}, u32[]{:S(2)}) collective-permute-start(bf16[16,24,768]{2,1,0:T(8,128)(2,1)S(1)} %all-to-all-done.1.mine_ref), channel_id=1, source_target_pairs={{0,4},{4,0},{1,5},{5,1},{2,6},{6,2},{3,7},{7,3},{8,12},{12,8},{9,1... | collective-permute-start | bytes 1769480 | tf_op jit(solution)/shard_map/ppermute | solution.py:257
  51.1 17.8 %collective-permute-start.13 = (bf16[96,768]{1,0:T(8,128)(2,1)}, bf16[96,768]{1,0:T(8,128)(2,1)S(1)}, u32[]{:S(2)}, u32[]{:S(2)}) collective-permute-start(bf16[96,768]{1,0:T(8,128)(2,1)} %get-tuple-element.12), channel_id=1, source_target_pairs={{0,16},{16,32},{32,48},{48,0},{1,17},{17,33},{33,49},{49,1},{2,18}... | collective-permute-start | bytes 442376 | tf_op jit(solution)/shard_map/ppermute | solution.py:270
  51.7 19.4 %collective-permute-start.15 = (bf16[96,768]{1,0:T(8,128)(2,1)}, bf16[96,768]{1,0:T(8,128)(2,1)S(1)}, u32[]{:S(2)}, u32[]{:S(2)}) collective-permute-start(bf16[96,768]{1,0:T(8,128)(2,1)} %get-tuple-element.12), channel_id=1, source_target_pairs={{0,32},{16,48},{32,0},{48,16},{1,33},{17,49},{33,1},{49,17},{2,34}... | collective-permute-start | bytes 442376 | tf_op jit(solution)/shard_map/ppermute | solution.py:270
  53.5 10.3 %collective-permute-start.7 = (bf16[96,768]{1,0:T(8,128)(2,1)}, bf16[96,768]{1,0:T(8,128)(2,1)S(1)}, u32[]{:S(2)}, u32[]{:S(2)}) collective-permute-start(bf16[96,768]{1,0:T(8,128)(2,1)} %get-tuple-element.17), channel_id=1, source_target_pairs={{0,64},{64,128},{128,192},{192,0},{1,65},{65,129},{129,193},{193,1... | collective-permute-start | bytes 442376 | tf_op jit(solution)/shard_map/ppermute | solution.py:270
  54.4 11.3 %collective-permute-start.9 = (bf16[96,768]{1,0:T(8,128)(2,1)}, bf16[96,768]{1,0:T(8,128)(2,1)}, u32[]{:S(2)}, u32[]{:S(2)}) collective-permute-start(bf16[96,768]{1,0:T(8,128)(2,1)} %get-tuple-element.17), channel_id=1, source_target_pairs={{0,128},{64,192},{128,0},{192,64},{1,129},{65,193},{129,1},{193,65... | collective-permute-start | bytes 442376 | tf_op jit(solution)/shard_map/ppermute | solution.py:270
  63.8 9.9 %collective-permute-start = (bf16[128,768]{1,0:T(8,128)(2,1)S(1)}, bf16[128,768]{1,0:T(8,128)(2,1)S(1)}, u32[]{:S(2)}, u32[]{:S(2)}) collective-permute-start(bf16[128,768]{1,0:T(8,128)(2,1)S(1)} %bitcast.20), channel_id=1, source_target_pairs={{0,1},{1,2},{2,3},{3,0},{4,5},{5,6},{6,7},{7,4},{8,9},{9,10},{10,1... | collective-permute-start | bytes 589832 | tf_op jit(solution)/shard_map/ppermute | solution.py:313
  65.6 10.1 %collective-permute-start.1 = (bf16[128,768]{1,0:T(8,128)(2,1)S(1)}, bf16[128,768]{1,0:T(8,128)(2,1)S(1)}, u32[]{:S(2)}, u32[]{:S(2)}) collective-permute-start(bf16[128,768]{1,0:T(8,128)(2,1)S(1)} %bitcast.19), channel_id=1, source_target_pairs={{0,3},{1,0},{2,1},{3,2},{4,7},{5,4},{6,5},{7,6},{8,11},{9,8},{10,9... | collective-permute-start | bytes 589832 | tf_op jit(solution)/shard_map/ppermute | solution.py:314
  68.9 21.3 %collective-permute-start.10 = (bf16[4,96,768]{2,1,0:T(8,128)(2,1)S(1)}, bf16[4,96,768]{2,1,0:T(8,128)(2,1)S(1)}, u32[]{:S(2)}, u32[]{:S(2)}) collective-permute-start(bf16[4,96,768]{2,1,0:T(8,128)(2,1)S(1)} %pad_maximum_fusion.refs_1_), channel_id=1, source_target_pairs={{0,16},{16,32},{32,48},{48,0},{1,17},{17,33},{33,49},{49,1},{2,18}... | collective-permute-start | bytes 1769480 | tf_op jit(solution)/shard_map/ppermute | solution.py:263
  71.1 19.8 %collective-permute-start.16 = (bf16[4,96,768]{2,1,0:T(8,128)(2,1)S(1)}, bf16[4,96,768]{2,1,0:T(8,128)(2,1)S(1)}, u32[]{:S(2)}, u32[]{:S(2)}) collective-permute-start(bf16[4,96,768]{2,1,0:T(8,128)(2,1)S(1)} %pad_maximum_fusion.1.refs_5_), channel_id=1, source_target_pairs={{0,64},{64,128},{128,192},{192,0},{1,65},{65,129},{129,193},{193,1... | collective-permute-start | bytes 1769480 | tf_op jit(solution)/shard_map/ppermute | solution.py:263
  88.5 18.9 %collective-permute-start.19 = (bf16[512,768]{1,0:T(8,128)(2,1)S(1)}, bf16[512,768]{1,0:T(8,128)(2,1)S(1)}, u32[]{:S(2)}, u32[]{:S(2)}) collective-permute-start(bf16[512,768]{1,0:T(8,128)(2,1)S(1)} %attend.1.refs_0_), channel_id=1, source_target_pairs={{0,4},{4,0},{1,5},{5,1},{2,6},{6,2},{3,7},{7,3},{8,12},{12,8},{9,1... | collective-permute-start | bytes 2359304 | tf_op jit(solution)/shard_map/ppermute | solution.py:257
  88.6 16.0 %collective-permute-start.11 = (bf16[4,96,768]{2,1,0:T(8,128)(2,1)S(1)}, bf16[4,96,768]{2,1,0:T(8,128)(2,1)S(1)}, u32[]{:S(2)}, u32[]{:S(2)}) collective-permute-start(bf16[4,96,768]{2,1,0:T(8,128)(2,1)S(1)} %pad_maximum_fusion.refs_1_), channel_id=1, source_target_pairs={{0,48},{16,0},{32,16},{48,32},{1,49},{17,1},{33,17},{49,33},{2,50}... | collective-permute-start | bytes 1769480 | tf_op jit(solution)/shard_map/ppermute | solution.py:264
  90.2 15.4 %collective-permute-start.17 = (bf16[4,96,768]{2,1,0:T(8,128)(2,1)S(1)}, bf16[4,96,768]{2,1,0:T(8,128)(2,1)S(1)}, u32[]{:S(2)}, u32[]{:S(2)}) collective-permute-start(bf16[4,96,768]{2,1,0:T(8,128)(2,1)S(1)} %pad_maximum_fusion.1.refs_5_), channel_id=1, source_target_pairs={{0,192},{64,0},{128,64},{192,128},{1,193},{65,1},{129,65},{193,129... | collective-permute-start | bytes 1769480 | tf_op jit(solution)/shard_map/ppermute | solution.py:264
  90.2 16.6 %collective-permute-start.12 = (bf16[4,96,768]{2,1,0:T(8,128)(2,1)S(1)}, bf16[4,96,768]{2,1,0:T(8,128)(2,1)S(1)}, u32[]{:S(2)}, u32[]{:S(2)}) collective-permute-start(bf16[4,96,768]{2,1,0:T(8,128)(2,1)S(1)} %collective-permute-done.10.refs_2_), channel_id=1, source_target_pairs={{0,16},{16,32},{32,48},{48,0},{1,17},{17,33},{33,49},{49,1},{2,18}... | collective-permute-start | bytes 1769480 | tf_op jit(solution)/shard_map/ppermute | solution.py:265
  90.9 16.5 %collective-permute-start.18 = (bf16[4,96,768]{2,1,0:T(8,128)(2,1)S(1)}, bf16[4,96,768]{2,1,0:T(8,128)(2,1)S(1)}, u32[]{:S(2)}, u32[]{:S(2)}) collective-permute-start(bf16[4,96,768]{2,1,0:T(8,128)(2,1)S(1)} %collective-permute-done.16.refs_6_), channel_id=1, source_target_pairs={{0,64},{64,128},{128,192},{192,0},{1,65},{65,129},{129,193},{193,1... | collective-permute-start | bytes 1769480 | tf_op jit(solution)/shard_map/ppermute | solution.py:265
  110.3 3.0 %collective-permute-start.20 = (bf16[512,768]{1,0:T(8,128)(2,1)S(1)}, bf16[512,768]{1,0:T(8,128)(2,1)S(1)}, u32[]{:S(2)}, u32[]{:S(2)}) collective-permute-start(bf16[512,768]{1,0:T(8,128)(2,1)S(1)} %feed_forward_partner.1), channel_id=1, source_target_pairs={{0,4},{4,0},{1,5},{5,1},{2,6},{6,2},{3,7},{7,3},{8,12},{12,8},{9,1... | collective-permute-start | bytes 2359304 | tf_op jit(solution)/shard_map/ppermute | solution.py:257
